TPU v7x, 512 devices: a whole 4x8x8 slice. The times are simulated.
512 devices in a mesh: row: 32 (over y, x_hi, core), col: 16 (over z, x_lo).
Axes of the slice: x: 4 (x_hi: 2, x_lo: 2; x = x_hi * 2 + x_lo), y: 8, z: 8, core: 2. Of those that a mesh axis runs over, the one named last changes fastest.
Arguments:
- temps: bfloat16 [12, 64, 262144], P(None, None, ('row', 'col')), may hold values from -6 to 6
- sensors: int32 [12, 2048], replicated, may hold values from 0 to 262143
Outputs:
- corr: bfloat16 [2048, 262144], P('col', 'row')
Inputs may be any that keep to these rules, and one draw needn't show every extreme that they name: `sensors`: each entry is a pixel index of its tier; candidates may repeat.
All inputs are finite; a program needn't handle non-finite values.
Results may differ from a plain program's by a relative error of at most 0.001.
Values may be sent and summed in bfloat16 or wider, within the bound.
No kernel may reach another device: no remote copies, remote signals or barrier semaphores. Data moves between devices by JAX's collectives and lax.ppermute only.
A program may use at most 64 MiB of HBM per device.

v0:
```python
import jax
import jax.numpy as jnp
from jax import lax
from jax.sharding import Mesh
from jax.sharding import PartitionSpec as P

COL = ("col_0", "col_1")
ROW_COL = ("row", "col_0", "col_1")


def scatter_axes(value, axes, dim):
    for axis in axes:
        value = lax.psum_scatter(value, axis, scatter_dimension=dim, tiled=True)
    return value


def filled_up(lines, length):
    spare = -lines.shape[0] % length
    if not spare:
        return lines
    return jnp.concatenate([lines, jnp.zeros((spare, *lines.shape[1:]), lines.dtype)])


def sent_to_all(value, axis):
    length = lax.axis_size(axis)
    return lax.all_to_all(
        jnp.broadcast_to(value[None], (length, *value.shape)), axis, 0, 0, tiled=True
    )


def laid_out(blocks, dim):
    blocks = jnp.moveaxis(blocks, 0, dim)
    shape = blocks.shape
    return blocks.reshape(*shape[:dim], shape[dim] * shape[dim + 1], *shape[dim + 2 :])


def gather_directly(value, axis, dim):
    blocks = sent_to_all(value, axis)
    return laid_out(blocks, dim)


def in_blocks(value, dim, length):
    before, after = (value.shape[:dim], value.shape[dim + 1 :])
    return jnp.moveaxis(value.reshape(*before, length, -1, *after), dim, 0)


def sent_and_summed(value, axis, dim):
    blocks = in_blocks(value, dim, lax.axis_size(axis))
    arrived = lax.all_to_all(blocks, axis, split_axis=0, concat_axis=0, tiled=True)
    return arrived.astype(jnp.float32).sum(axis=0)


def total_of(value, axes):
    lines = value.reshape(-1, value.shape[-1])
    padded = filled_up(lines, lax.axis_size(axes))
    whole = gather_directly(sent_and_summed(padded, axes, 0).astype(jnp.bfloat16), axes, 0)
    return lax.slice_in_dim(whole, 0, len(lines)).reshape(value.shape).astype(jnp.float32)


def select_columns(fields, sensor_rows, first_pixel):
    width = fields.shape[2]
    offsets = sensor_rows - first_pixel
    pixel_ids = lax.broadcasted_iota(jnp.int32, (width, sensor_rows.shape[1]), 0)

    def one_tier(pair):
        tier_fields, tier_offsets = pair
        selector = (pixel_ids == tier_offsets[None, :]).astype(jnp.bfloat16)
        return jnp.dot(tier_fields, selector, preferred_element_type=jnp.float32)

    return lax.map(one_tier, (fields, offsets))


def body(temps, sensors):
    col_count = lax.axis_size(COL)
    first_pixel = (lax.axis_index("row") * col_count + lax.axis_index(COL)) * temps.shape[2]
    local_values = select_columns(temps, sensors, first_pixel)
    owned = (
        scatter_axes(local_values.astype(jnp.bfloat16), COL, 2)
        .astype(jnp.float32)
        .astype(jnp.bfloat16)
    )
    readings = total_of(owned, "row").astype(jnp.bfloat16)
    scale_factor = 1.0 / jnp.sqrt(jnp.float32(temps.shape[0] * temps.shape[1]))
    summed = jnp.einsum(
        "tsc,tsp->cp",
        lax.all_gather(readings, COL, axis=2, tiled=True),
        temps,
        preferred_element_type=jnp.float32,
    )
    rounded = (summed * scale_factor).astype(jnp.bfloat16)
    return lax.all_to_all(rounded, COL, split_axis=0, concat_axis=1, tiled=True)


def solution(mesh):
    torus = Mesh(mesh.devices.reshape(mesh.shape["row"], 8, 2), ("row", "col_0", "col_1"))
    in_specs = (P(None, None, ROW_COL), P())
    out_specs = P(COL, "row")
    return jax.shard_map(body, mesh=torus, in_specs=in_specs, out_specs=out_specs, check_vma=False)
```

profile of v0, /device:TPU:6, one launch (start us, length us, event | category | flops | bytes accessed | tf_op | source)
XLA Modules:
  0.0 315.3 jit_solution(11540507424467396206)
XLA Ops:
  6.5 0.9 broadcast_subtract_fusion
  7.5 29.7 %while.11 = (s32[]{:T(128)}, bf16[12,64,2048]{2,1,0:T(8,128)(2,1)}, bf16[12,64,512]{2,1,0:T(8,128)(2,1)}, s32[12,2048]{1,0:T(8,128)S(1)}, s32[]{:T(128)}) while((s32[]{:T(128)}, bf16[12,64,2048]{2,1,0:T(8,128)(2,1)}, bf16[12,64,512]{2,1,0:T(8,128)(2,1)}, s32[12,2048]{1,0:T(8,128)S(1)}, s32[]{:T(128)}) %tuple.21), condition=%wide.region_1.2_spmd.clone, body=%wide.region_0.1_spmd.clone.sunk | while | flops 135266304 | bytes 615489 | solution.py:70
  7.5 2.4 fusion.15
  9.9 2.5 fusion.15
  12.4 2.4 fusion.15
  14.9 2.5 fusion.15
  17.3 2.5 fusion.15
  19.8 2.5 fusion.15
  22.3 2.5 fusion.15
  24.7 2.4 fusion.15
  27.2 2.5 fusion.15
  29.7 2.5 fusion.15
  32.2 2.5 fusion.15
  34.6 2.5 fusion.15
  37.1 0.0 reduce-scatter.5.cloned.1.call-update
  37.1 0.0 copy-start
  37.1 0.0 reduce-scatter.7.cloned.1.call-start
  37.2 54.7 %reduce-scatter.5.cloned.1.call-done = bf16[12,64,256]{2,1,0:T(8,128)(2,1)} async-done(((bf16[12,64,2048]{2,1,0:T(8,128)(2,1)}), bf16[12,64,256]{2,1,0:T(8,128)(2,1)}) %reduce-scatter.5.cloned.1.call-update) | async-done | bytes 393232 | tf_op jit(solution)/shard_map/reduce_scatter | solution.py:13
  91.9 1.9 copy.5
  93.8 1.4 reshape.5
  95.2 0.0 reduce-scatter.7.cloned.1.call-update
  95.2 0.0 all-gather.2.cloned.1.call-start
  95.3 19.3 %reduce-scatter.7.cloned.1.call-done = bf16[128,768]{1,0:T(8,128)(2,1)} async-done(((bf16[256,768]{1,0:T(8,128)(2,1)}), bf16[128,768]{1,0:T(8,128)(2,1)}) %reduce-scatter.7.cloned.1.call-update) | async-done | bytes 196624
  114.5 1.3 reshape.6
  115.8 0.4 copy.6
  116.2 20.3 %all_to_all.29 = bf16[32,24,128]{2,1,0:T(8,128)(2,1)S(1)} all-to-all(bf16[32,24,128]{2,1,0:T(8,128)(2,1)S(1)} %bitcast.33), channel_id=1, replica_groups=mesh['row'=32,'col_0'=8,'col_1'=2] {'row'}, dimensions={0} | all-to-all | bytes 393216 | tf_op jit(solution)/shard_map/all_to_all | solution.py:49
  136.6 15.6 %all_to_all.30 = bf16[32,24,128]{2,1,0:T(8,128)(2,1)} all-to-all(bf16[32,24,128]{2,1,0:T(8,128)(2,1)S(1)} %broadcast_in_dim.15), channel_id=1, replica_groups=mesh['row'=32,'col_0'=8,'col_1'=2] {'row'}, dimensions={0} | all-to-all | bytes 393216 | tf_op jit(solution)/shard_map/all_to_all | solution.py:26
  152.2 0.0 all-gather.2.cloned.1.call-update
  152.3 101.0 %all-gather.2.cloned.1.call-done = bf16[12,64,2048]{2,1,0:T(8,128)(2,1)} async-done(((bf16[12,64,128]{2,1,0:T(8,128)(2,1)}), bf16[12,64,2048]{2,1,0:T(8,128)(2,1)}) %all-gather.2.cloned.1.call-update) | async-done | bytes 3145744 | tf_op jit(solution)/shard_map/all_gather | solution.py:86
  253.3 3.7 %fusion.9 = bf16[2048,512]{1,0:T(8,128)(2,1)S(1)} fusion(bf16[12,64,2048]{2,1,0:T(8,128)(2,1)} %all-gather.2.cloned.1.call-done, bf16[12,64,512]{2,1,0:T(8,128)(2,1)S(1)} %copy-done), kind=kOutput, calls=%fused_computation.11 | convolution fusion | flops 1612709888 | bytes 6029312 | tf_op jit(solution)/shard_map/tsc,tsp->cp/dot_general | solution.py:84
  257.0 50.2 %all_to_all.31 = bf16[16,128,512]{2,1,0:T(8,128)(2,1)S(1)} all-to-all(bf16[16,128,512]{2,1,0:T(8,128)(2,1)S(1)} %bitcast.30), channel_id=1, replica_groups=mesh['row'=32,'col_0'=8,'col_1'=2] {'col_0','col_1'}, dimensions={0} | all-to-all | bytes 4194304 | tf_op jit(solution)/shard_map/all_to_all | solution.py:91
  307.2 1.5 copy.7
  (17 shorter events, 0.2 us)
Async XLA Ops:
  6.5 85.3 %reduce-scatter.5.cloned.1.call-start = ((), (), s32[]{:S(2)}) async-start(), calls=%async_computation.5 | async-start | bytes 3538944 | tf_op jit(solution)/shard_map/reduce_scatter | solution.py:13
  37.1 216.2 %copy-start = (bf16[12,64,512]{2,1,0:T(8,128)(2,1)S(1)}, bf16[12,64,512]{2,1,0:T(8,128)(2,1)}, u32[]{:S(2)}) copy-start(bf16[12,64,512]{2,1,0:T(8,128)(2,1)} %get-tuple-element.103) | copy-start | bytes 2359300
  37.1 77.4 %reduce-scatter.7.cloned.1.call-start = ((), (), s32[]{:S(2)}) async-start(), calls=%async_computation.7 | async-start | bytes 589824
  95.2 158.1 %all-gather.2.cloned.1.call-start = ((), (), s32[]{:S(2)}) async-start(), calls=%async_computation.6 | async-start | bytes 3342336 | tf_op jit(solution)/shard_map/all_gather | solution.py:86
Sparse Core Ops, SparseCore 0:
  37.3 54.5 reduce-scatter.4
  95.3 19.1 reduce-scatter.6
  152.4 100.8 all-gather.1
where the time goes:
time: 317 us; the launch traced here: 315 us
  waiting for transfers between devices  175 us (55%)
  blocking collectives  86.2 us (27%)
  matrix products  33.2 us (10%)
  between operations  13.2 us (4%)
  local copies, waits for them, and re-layouts  6.65 us (2%)
    all_gather x1, waiting for transfers between devices, body(): lax.all_gather(readings, COL, axis=2, tiled=True)  101 us
    reduce_scatter x1, waiting for transfers between devices, scatter_axes(): value = lax.psum_scatter(value, axis, scatter_dimension=dim, tiled=True)  54.7 us
    all_to_all x1, blocking collectives, body(): return lax.all_to_all(rounded, COL, split_axis=0, concat_axis=1, tiled=True)  50.2 us
    dot_general x12, matrix products, one_tier(): return jnp.dot(tier_fields, selector, preferred_element_type=jnp.float32)  29.5 us
    all_to_all x1, blocking collectives, sent_and_summed(): lax.all_to_all(blocks, axis, split_axis=0, concat_axis=0, tiled=True)  20.3 us
    unnamed x4, waiting for transfers between devices  19.3 us
    all_to_all x1, blocking collectives, sent_to_all(): lax.all_to_all(jnp.broadcast_to(value[None], (length, *value.shape)), axi...  15.6 us
  transfers between devices with their start and end apart: 3, of which 3 were waited for; matrix products, arithmetic and copies ran while one was open for 0% of the time, Pallas kernels for 0%

commit v1 on v0

v1 whole, which is shorter than its diff:
```python
import jax
import jax.numpy as jnp
from jax import lax
from jax.experimental import pallas as pl
from jax.experimental.pallas import tpu as pltpu
from jax.sharding import Mesh
from jax.sharding import PartitionSpec as P

AXES = ("y", "xh", "core", "z", "xl")
X = ("xh", "xl")
PLANE = ("y", "xh", "xl", "core")
VMEM = pl.BlockSpec(memory_space=pltpu.VMEM)


def ring(value, axis, shift):
    size = lax.axis_size(axis)
    return lax.ppermute(value, axis, [(i, (i + shift) % size) for i in range(size)])


def select_kernel(tiers, snaps, idx_ref, temps_ref, *rest):
    out_ref = rest[-1]
    rows, width = idx_ref.shape[0], temps_ref.shape[2]
    lanes = lax.broadcasted_iota(jnp.int32, (rows, width), 1)

    def one(tier):
        chosen = (lanes == idx_ref[:, tier : tier + 1]).astype(jnp.float32).astype(jnp.bfloat16)
        return lax.dot_general(
            chosen, temps_ref[tier], (((1,), (1,)), ((), ())), preferred_element_type=jnp.float32
        )

    for tier in range(0, tiers, 2):
        found = jnp.concatenate([one(tier), one(tier + 1)], axis=1)
        spot = slice(tier * snaps, (tier + 2) * snaps)
        if len(rest) > 1:
            found = found + rest[0][:, spot].astype(jnp.float32)
        out_ref[:, spot] = found.astype(jnp.bfloat16)


def select(idx, temps, *added):
    rows, tiers = idx.shape
    _, snaps, width = temps.shape
    depth, block = tiers * snaps, 256
    spec = pl.BlockSpec((block, depth), lambda i: (i, 0))
    return pl.pallas_call(
        lambda *refs: select_kernel(tiers, snaps, *refs),
        grid=(rows // block,),
        in_specs=[
            pl.BlockSpec((block, tiers), lambda i: (i, 0)),
            pl.BlockSpec(temps.shape, lambda i: (0, 0, 0)),
        ]
        + [spec] * len(added),
        out_specs=spec,
        out_shape=jax.ShapeDtypeStruct((rows, depth), jnp.bfloat16),
        cost_estimate=pl.CostEstimate(
            flops=2 * rows * depth * width, bytes_accessed=2 * rows * depth, transcendentals=0
        ),
        name="select",
    )(idx, temps, *added)


def body(temps, sensors):
    tiers, snaps, width = temps.shape
    depth = tiers * snaps
    n_y, n_x, n_core, n_z = (lax.axis_size(a) for a in ("y", X, "core", "z"))
    n_xl = lax.axis_size("xl")
    per_z = sensors.shape[1] // n_z
    piece = per_z // (n_y * n_x * n_core)
    core = lax.axis_index("core")

    gathered = lax.all_gather(temps, "z")

    other_temps = ring(temps, "core", 1)
    order = sensors.reshape(tiers, n_z, n_y, n_x, n_core, piece)
    order = lax.dynamic_index_in_dim(order, core, 4, keepdims=False)
    order = order.transpose(3, 1, 2, 4, 0).reshape(-1, tiers)
    first = lax.axis_index(AXES) * width
    stride = n_z * n_xl * width
    other_first = first + jnp.where(core == 0, stride, -stride)
    part = select(order - first, temps)
    part = select(order - other_first, other_temps, part)

    part = part.reshape(n_x, per_z * n_z // (n_x * n_core), depth)
    part = lax.all_to_all(part, X, 0, 0, tiled=True)
    part = part.astype(jnp.float32).sum(axis=0).astype(jnp.bfloat16)
    part = part.reshape(n_z * n_y, piece, depth)
    part = lax.all_to_all(part, ("z", "y"), 0, 0, tiled=True)
    part = part.astype(jnp.float32).sum(axis=0).astype(jnp.bfloat16)
    part = jnp.broadcast_to(part[None], (n_y * n_x * n_core, piece, depth))
    readings = lax.all_to_all(part, PLANE, 0, 0, tiled=True).reshape(per_z, depth)

    scale = 1.0 / jnp.sqrt(jnp.float32(depth))
    summed = jnp.einsum(
        "hck,zkp->hzcp",
        readings.reshape(n_xl, per_z // n_xl, depth),
        gathered.reshape(n_z, depth, width),
        preferred_element_type=jnp.float32,
    )
    corr = (summed * scale).astype(jnp.bfloat16)
    corr = lax.all_to_all(corr, "xl", 0, 0, tiled=True)
    return corr.transpose(2, 1, 0, 3).reshape(per_z // n_xl, -1)


def solution(mesh):
    torus = Mesh(mesh.devices.reshape(8, 2, 2, 8, 2), AXES)
    return jax.shard_map(
        body,
        mesh=torus,
        in_specs=(P(None, None, AXES), P()),
        out_specs=P(("z", "xl"), ("y", "xh", "core")),
        check_vma=False,
    )
```

time: 317 us -> 154 us (0.49)
  waiting for transfers between devices: 175 us -> 0.73 us
  matrix products: 33.2 us -> 4.58 us
  blocking collectives: 86.2 us -> 106 us
  Pallas kernels: 0 us -> 13.1 us
  local copies, waits for them, and re-layouts: 6.65 us -> 10.9 us
    all_gather x1, waiting for transfers between devices: 101 us -> 0.02 us  [body(): gathered = lax.all_gather(temps, 'z')]
    reduce_scatter x1 -> x0, waiting for transfers between devices: 54.7 us -> none  [scatter_axes(): value = lax.psum_scatter(value, axis, scatter_dimension=dim, tiled=True)]
    dot_general x13 -> x1, matrix products: 33.2 us -> 4.58 us  [body(): jnp.einsum('hck,zkp->hzcp', readings.reshape(n_xl, per_z // n_xl, depth),...]
    all_to_all x3 -> x4, blocking collectives: 86.2 us -> 106 us  [the longest x1 29 us: body(): part = lax.all_to_all(part, X, 0, 0, tiled=True)]
    unnamed x4 -> x1, waiting for transfers between devices: 19.3 us -> 0.71 us
    pallas_call x0 -> x2, Pallas kernels: none -> 13.1 us  [select(): pl.pallas_call(lambda *refs: select_kernel(tiers, snaps, *refs), grid=(ro...]
    reshape x0 -> x2, local copies, waits for them, and re-layouts: none -> 4.16 us  [the longest x1 4.06 us: body(): return corr.transpose(2, 1, 0, 3).reshape(per_z // n_xl, -1)]
  transfers between devices with their start and end apart: 3 -> 2, of which waited for: 3 -> 0; matrix products, arithmetic and copies ran while one was open for 0% -> 3% of each run, Pallas kernels for 0% -> 9%
where the time goes in v1:
time: 154 us; the launch traced here: 151 us
  blocking collectives  106 us (69%)
  between operations  13.5 us (9%)
  Pallas kernels  13.1 us (9%)
  local copies, waits for them, and re-layouts  10.9 us (7%)
  matrix products  4.58 us (3%)
  starting transfers between devices  1.92 us (1%)
    all_to_all x1, blocking collectives, body(): part = lax.all_to_all(part, X, 0, 0, tiled=True)  29 us
    all_to_all x1, blocking collectives, body(): part = lax.all_to_all(part, ('z', 'y'), 0, 0, tiled=True)  28.6 us
    all_to_all x1, blocking collectives, body(): corr = lax.all_to_all(corr, 'xl', 0, 0, tiled=True)  26.5 us
    all_to_all x1, blocking collectives, body(): lax.all_to_all(part, PLANE, 0, 0, tiled=True).reshape(per_z, depth)  21.6 us
    pallas_call x2, Pallas kernels, select(): pl.pallas_call(lambda *refs: select_kernel(tiers, snaps, *refs), grid=(ro...  13.1 us
    dot_general x1, matrix products, body(): jnp.einsum('hck,zkp->hzcp', readings.reshape(n_xl, per_z // n_xl, depth),...  4.58 us
    reshape x1, local copies, waits for them, and re-layouts, body(): return corr.transpose(2, 1, 0, 3).reshape(per_z // n_xl, -1)  4.06 us
  transfers between devices with their start and end apart: 2, of which 0 were waited for; matrix products, arithmetic and copies ran while one was open for 3% of the time, Pallas kernels for 9%

profile of v1, /device:TPU:6, one launch (start us, length us, event | category | flops | bytes accessed | tf_op | source)
XLA Modules:
  0.0 151.1 jit_solution(6597144692057037397)
XLA Ops:
  6.5 0.0 all-gather.3.cloned.1.call-start
  6.5 0.7 all-gather.3.cloned.1.call-update
  7.3 1.9 %collective-permute-start = (bf16[12,64,512]{2,1,0:T(8,128)(2,1)}, bf16[12,64,512]{2,1,0:T(8,128)(2,1)S(1)}, u32[]{:S(2)}, u32[]{:S(2)}) collective-permute-start(bf16[12,64,512]{2,1,0:T(8,128)(2,1)} %refs_1_.1), channel_id=1, source_target_pairs={{0,16},{16,0},{1,17},{17,1},{2,18},{18,2},{3,19},{19,3},{4,20},{20... | collective-permute-start | bytes 2359304 | tf_op jit(solution)/shard_map/ppermute | solution.py:17
  9.2 1.3 copy.19
  10.5 0.2 subtract_bitcast_fusion
  10.7 0.9 copy.21
  11.6 1.0 copy.20
  12.6 6.5 %select.2.refs_2_ = bf16[1024,768]{1,0:T(8,128)(2,1)} custom-call(s32[1024,12]{1,0:T(8,128)} %bitcast.28, bf16[12,64,512]{2,1,0:T(8,128)(2,1)} %refs_1_.1), custom_call_target="tpu_custom_call" | custom-call | flops 805306368 | bytes 1572864 | tf_op jit(solution)/shard_map/select/pallas_call | solution.py:44
  19.1 0.0 collective-permute-done.refs_1_
  19.1 0.0 copy-start
  19.1 1.0 copy-done
  20.0 6.6 %select.3 = bf16[1024,768]{1,0:T(8,128)(2,1)} custom-call(s32[1024,12]{1,0:T(8,128)} %bitcast.27, bf16[12,64,512]{2,1,0:T(8,128)(2,1)} %copy-done, bf16[1024,768]{1,0:T(8,128)(2,1)} %select.2.refs_2_), custom_call_target="tpu_custom_call" | custom-call | flops 805306368 | bytes 1572864 | tf_op jit(solution)/shard_map/select/pallas_call | solution.py:44
  26.7 29.0 %all_to_all.20 = bf16[4,256,768]{2,1,0:T(8,128)(2,1)S(1)} all-to-all(bf16[4,256,768]{2,1,0:T(8,128)(2,1)} %bitcast.25), channel_id=1, replica_groups=mesh['y'=8,'xh'=2,'core'=2,'z'=8,'xl'=2] {'xh','xl'}, dimensions={0} | all-to-all | bytes 3145728 | tf_op jit(solution)/shard_map/all_to_all | solution.py:83
  55.7 0.4 reduce_sum.24
  56.1 0.1 reshape.27
  56.2 28.6 %all_to_all.21 = bf16[64,4,768]{2,1,0:T(4,128)(2,1)S(1)} all-to-all(bf16[64,4,768]{2,1,0:T(4,128)(2,1)S(1)} %reshape.27), channel_id=1, replica_groups=mesh['y'=8,'xh'=2,'core'=2,'z'=8,'xl'=2] {'z','y'}, dimensions={0} | all-to-all | bytes 786432 | tf_op jit(solution)/shard_map/all_to_all | solution.py:86
  84.7 0.2 reduce_sum.25
  84.9 0.1 broadcast_in_dim.2
  85.0 21.6 %all_to_all.22 = bf16[64,4,768]{2,1,0:T(4,128)(2,1)S(1)} all-to-all(bf16[64,4,768]{2,1,0:T(4,128)(2,1)S(1)} %broadcast_in_dim.2), channel_id=1, replica_groups=mesh['y'=8,'xh'=2,'core'=2,'z'=8,'xl'=2] {'y','xh','xl','core'}, dimensions={0} | all-to-all | bytes 786432 | tf_op jit(solution)/shard_map/all_to_all | solution.py:89
  106.6 0.1 reshape.32
  106.7 0.0 all-gather.3.cloned.1.call-done
  106.8 4.6 %fusion = bf16[2,8,128,512]{3,2,1,0:T(8,128)(2,1)S(1)} fusion(bf16[8,768,512,1]{2,1,0,3:T(8,128)(2,1)} %bitcast.29, bf16[2,128,768,1]{2,1,0,3:T(8,128)(2,1)S(1)} %reshape.32), kind=kOutput, calls=%fused_computation.1 | convolution fusion | flops 1612709888 | bytes 8781824 | tf_op jit(solution)/shard_map/hck,zkp->hzcp/dot_general | solution.py:92
  111.4 26.5 %all_to_all.23 = bf16[2,8,128,512]{3,2,1,0:T(8,128)(2,1)S(1)} all-to-all(bf16[2,8,128,512]{3,2,1,0:T(8,128)(2,1)S(1)} %fusion), channel_id=1, replica_groups=mesh['y'=8,'xh'=2,'core'=2,'z'=8,'xl'=2] {'xl'}, dimensions={0} | all-to-all | bytes 4194304 | tf_op jit(solution)/shard_map/all_to_all | solution.py:99
  137.8 2.4 %copy.23 = bf16[128,8,2,512]{0,3,2,1:T(8,128)(2,1)} copy(bf16[128,8,2,512]{3,0,1,2:T(8,128)(2,1)S(1)} %bitcast.23) | data formatting | bytes 4194304 | tf_op jit(solution)/shard_map/transpose | solution.py:100
  140.2 4.1 %copy.24 = bf16[128,8192]{1,0:T(8,128)(2,1)} copy(bf16[128,8192]{0,1:T(8,128)(2,1)} %bitcast.24) | data formatting | bytes 4194304 | tf_op jit(solution)/shard_map/reshape | solution.py:100
Async XLA Ops:
  6.5 100.2 %all-gather.3.cloned.1.call-start = ((), (), s32[]{:S(2)}) async-start(), calls=%async_computation.4 | async-start | bytes 7077888 | tf_op jit(solution)/shard_map/all_gather | solution.py:70
  7.3 11.8 %collective-permute-start = (bf16[12,64,512]{2,1,0:T(8,128)(2,1)}, bf16[12,64,512]{2,1,0:T(8,128)(2,1)S(1)}, u32[]{:S(2)}, u32[]{:S(2)}) collective-permute-start(bf16[12,64,512]{2,1,0:T(8,128)(2,1)} %refs_1_.1), channel_id=1, source_target_pairs={{0,16},{16,0},{1,17},{17,1},{2,18},{18,2},{3,19},{19,3},{4,20},{20... | collective-permute-start | bytes 2359304 | tf_op jit(solution)/shard_map/ppermute | solution.py:17
  19.1 1.0 copy-start
Sparse Core Ops, SparseCore 0:
  9.4 90.9 all-gather.2

commit v2 on v1

v2 whole, which is shorter than its diff:
```python
import functools
import math

import jax
import jax.numpy as jnp
from jax import lax
from jax.experimental import pallas as pl
from jax.experimental.pallas import tpu as pltpu
from jax.sharding import Mesh
from jax.sharding import PartitionSpec as P

AXES = ("y", "xh", "core", "z", "xl")
PLANE = ("y", "xh", "xl", "core")
SLOTS = 32
FIRST = 384
F32, BF16 = jnp.float32, jnp.bfloat16
PARAMS = pltpu.CompilerParams(vmem_limit_bytes=16 * 2**20)
NT = (((1,), (1,)), ((), ()))
VMEM = pl.BlockSpec(memory_space=pltpu.VMEM)
SMEM = pl.BlockSpec(memory_space=pltpu.SMEM)


def matmul(a, b, dims=(((1,), (0,)), ((), ()))):
    return lax.dot_general(a, b, dims, preferred_element_type=F32)


def ones(mask):
    return mask.astype(F32).astype(BF16)


def triangles(tiers, columns):
    upper = lax.broadcasted_iota(jnp.int32, (columns, columns), 0) < lax.broadcasted_iota(
        jnp.int32, (columns, columns), 1
    )
    lower = lax.broadcasted_iota(jnp.int32, (tiers, tiers), 0) > lax.broadcasted_iota(
        jnp.int32, (tiers, tiers), 1
    )
    return ones(upper), ones(lower)


def ranks(mask, upper, lower):
    mask = ones(mask)
    return matmul(mask, upper) + matmul(lower, mask).sum(axis=1, keepdims=True)


def compact_kernel(scalar_ref, sensors_ref, temps_ref, out_ref):
    n_z, half, _ = out_ref.shape
    tiers, _, width = temps_ref.shape
    slots, per_z = 2 * half, sensors_ref.shape[1] // n_z
    first, start = scalar_ref[0], scalar_ref[1]
    upper, lower = triangles(tiers, per_z)
    slot_ids = lax.broadcasted_iota(jnp.int32, (slots, per_z), 0)
    tier_ids = lax.broadcasted_iota(jnp.int32, (tiers, per_z), 0)
    spots = []
    for z in range(n_z):
        offset = sensors_ref[:, z * per_z : (z + 1) * per_z] - first
        mine = (offset >= 0) & (offset < width)
        slot = ranks(mine, upper, lower).astype(jnp.int32) - start
        slot = jnp.where(mine, slot, -1)
        spot = (offset + tier_ids * width + 1).astype(F32)
        found = jnp.zeros((slots, per_z), F32)
        for tier in range(tiers):
            row = slice(tier, tier + 1)
            found = found + jnp.where(slot[row] == slot_ids, spot[row], 0.0)
        spots.append(found.sum(axis=1, keepdims=True))
    spots = jnp.concatenate(spots, axis=0).astype(jnp.int32) - 1
    lanes = lax.broadcasted_iota(jnp.int32, (n_z * slots, width), 1)
    total = jnp.zeros((n_z * slots, temps_ref.shape[1]), F32)
    for tier in range(tiers):
        total = total + matmul(ones(spots - tier * width == lanes), temps_ref[tier], NT)
    for z in range(n_z):
        low = z * slots
        out_ref[z] = jnp.concatenate(
            [total[low : low + half], total[low + half : low + slots]], axis=1
        ).astype(BF16)


def compact(scalars, sensors, temps, n_z):
    return pl.pallas_call(
        compact_kernel,
        in_specs=[SMEM, VMEM, VMEM],
        out_specs=VMEM,
        out_shape=jax.ShapeDtypeStruct((n_z, SLOTS // 2, 2 * temps.shape[1]), BF16),
        compiler_params=PARAMS,
        name="compact",
    )(scalars, sensors, temps)


def expand_kernel(width, scalar_ref, sensors_ref, lists_ref, out_ref):
    n_z, half, wide = lists_ref.shape
    snaps = wide // 2
    tiers = sensors_ref.shape[0]
    per_z = out_ref.shape[0]
    first, start, stride = scalar_ref[0], scalar_ref[1], 2 * width
    own = pl.multiple_of(scalar_ref[2], per_z)
    upper, lower = triangles(tiers, per_z)
    offset = sensors_ref[:, pl.ds(own, per_z)] - first
    spot = jnp.full((tiers, per_z), -1, jnp.int32)
    for z in range(n_z):
        there = (offset >= z * stride) & (offset < z * stride + width)
        slot = ranks(there, upper, lower).astype(jnp.int32) - start
        code = jnp.where(slot < half, slot + z * half, slot + (n_z - 1 + z) * half)
        spot = jnp.where(there & (slot >= 0) & (slot < 2 * half), code, spot)
    eye = lax.broadcasted_iota(jnp.int32, (tiers, tiers), 0) == lax.broadcasted_iota(
        jnp.int32, (tiers, tiers), 1
    )
    column = lax.dot_general(
        spot.astype(F32).astype(BF16), ones(eye), (((0,), (0,)), ((), ())), preferred_element_type=F32
    ).astype(jnp.int32)
    lists = lists_ref[...].reshape(n_z * half, wide)
    lists = jnp.concatenate([lists[:, :snaps], lists[:, snaps:]], axis=0)
    lanes = lax.broadcasted_iota(jnp.int32, (per_z, 2 * n_z * half), 1)
    for tier in range(0, tiers, 2):
        pair = [matmul(ones(lanes == column[:, t : t + 1]), lists) for t in (tier, tier + 1)]
        out_ref[:, tier * snaps : (tier + 2) * snaps] = jnp.concatenate(pair, axis=1).astype(BF16)


def expand(scalars, sensors, lists, width):
    n_z, _, wide = lists.shape
    tiers, count = sensors.shape
    return pl.pallas_call(
        functools.partial(expand_kernel, width),
        in_specs=[SMEM, VMEM, VMEM],
        out_specs=VMEM,
        out_shape=jax.ShapeDtypeStruct((count // n_z, tiers * wide // 2), BF16),
        compiler_params=PARAMS,
        name="expand",
    )(scalars, sensors, lists)


def longest_kernel(n_z, devices, width, sensors_ref, out_ref):
    tiers, count = sensors_ref.shape
    per_z, low = count // n_z, 16
    high_ids = lax.broadcasted_iota(jnp.int32, (devices // low, per_z), 0)
    low_ids = lax.broadcasted_iota(jnp.int32, (low, per_z), 0)
    most = jnp.zeros((devices // low, low), F32)
    for z in range(n_z):
        owner = sensors_ref[:, z * per_z : (z + 1) * per_z] // width
        total = jnp.zeros_like(most)
        for tier in range(tiers):
            row = owner[tier : tier + 1]
            total = total + matmul(ones(row // low == high_ids), ones(row % low == low_ids), NT)
        most = jnp.maximum(most, total)
    out_ref[0, 0] = jnp.max(most).astype(jnp.int32)


def longest(sensors, n_z, devices, width):
    return pl.pallas_call(
        functools.partial(longest_kernel, n_z, devices, width),
        in_specs=[VMEM],
        out_specs=SMEM,
        out_shape=jax.ShapeDtypeStruct((1, 1), jnp.int32),
        compiler_params=PARAMS,
        cost_estimate=pl.CostEstimate(
            flops=2 * sensors.size * devices, bytes_accessed=4 * sensors.size, transcendentals=0
        ),
        name="longest",
    )(sensors)[0, 0]


def correlate_kernel(scale, scalar_ref, readings_ref, pixels_ref, *rest):
    summed = matmul(readings_ref[...], pixels_ref[...])
    rest[-1][...] = (summed * scale).astype(BF16)


def block_columns(rows, stride, skipped, width):
    def place_of(z, h):
        return 0, pl.multiple_of((2 * z + h[1]) * stride + skipped, 128)

    return pl.BlockSpec((pl.Element(rows), pl.Element(width)), place_of)


def correlate(half, readings, pixels, out_spec, out_shape, *whole):
    n_z, depth, width = pixels.shape
    rows = readings.shape[0] // 2
    return pl.pallas_call(
        functools.partial(correlate_kernel, 1.0 / math.sqrt(depth)),
        grid_spec=pltpu.PrefetchScalarGridSpec(
            num_scalar_prefetch=1,
            grid=(n_z,),
            in_specs=[
                pl.BlockSpec((rows, depth), lambda z, h: (h[0], 0)),
                pl.BlockSpec((None, depth, width), lambda z, h: (z, 0, 0)),
            ]
            + [pl.BlockSpec(memory_space=pl.ANY)] * len(whole),
            out_specs=out_spec,
        ),
        out_shape=jax.ShapeDtypeStruct(out_shape, BF16),
        input_output_aliases={3: 0} if whole else {},
        cost_estimate=pl.CostEstimate(
            flops=2 * rows * depth * width * n_z, bytes_accessed=pixels.size * 2, transcendentals=0
        ),
        compiler_params=pltpu.CompilerParams(vmem_limit_bytes=59 * 2**20),
        name="correlate",
    )(half, readings, pixels, *whole)


def place_kernel(scalar_ref, block_ref, whole_ref, out_ref):
    out_ref[...] = block_ref[...]


def place(side, blocks, out_spec, whole):
    n_z, rows, width = blocks.shape
    return pl.pallas_call(
        place_kernel,
        grid_spec=pltpu.PrefetchScalarGridSpec(
            num_scalar_prefetch=1,
            grid=(n_z,),
            in_specs=[
                pl.BlockSpec((None, rows, width), lambda z, h: (z, 0, 0)),
                pl.BlockSpec(memory_space=pl.ANY),
            ],
            out_specs=out_spec,
        ),
        out_shape=jax.ShapeDtypeStruct(whole.shape, BF16),
        input_output_aliases={2: 0},
        compiler_params=PARAMS,
        name="place",
    )(side, blocks, whole)


def body(temps, sensors):
    tiers, snaps, width = temps.shape
    depth = tiers * snaps
    n_z, n_plane, devices = (lax.axis_size(a) for a in ("z", PLANE, AXES))
    per_z = sensors.shape[1] // n_z
    piece = per_z // n_plane
    rows = per_z // 2
    z, xl = lax.axis_index("z"), lax.axis_index("xl")

    spans = [(0, FIRST), (FIRST, width - FIRST)]
    gathered = [
        lax.all_gather(lax.slice_in_dim(temps, low, low + size, axis=2), "z").reshape(
            n_z, depth, size
        )
        for low, size in spans
    ]

    first = lax.axis_index(AXES) * width
    column_first = first - z * lax.axis_size("xl") * width

    def one_round(number):
        start = number * SLOTS
        lists = compact(jnp.stack([first, start]), sensors, temps, n_z)
        lists = lax.all_to_all(lists, "z", 0, 0, tiled=True)
        part = expand(jnp.stack([column_first, start, z * per_z]), sensors, lists, width)
        seen, part = lax.optimization_barrier((sensors, part))
        part = lax.all_to_all(part.reshape(n_plane, piece, depth), PLANE, 0, 0, tiled=True)
        part = part.astype(F32).sum(axis=0).astype(BF16)
        part = jnp.broadcast_to(part[None], (n_plane, piece, depth))
        return seen, lax.all_to_all(part, PLANE, 0, 0, tiled=True).reshape(per_z, depth)

    seen, readings = one_round(jnp.int32(0))
    rounds = pl.cdiv(longest(seen, n_z, devices, width), SLOTS)
    _, readings = lax.while_loop(
        lambda state: state[0] < rounds,
        lambda state: (state[0] + 1, state[1] + one_round(state[0])[1]),
        (jnp.int32(1), readings),
    )

    theirs, mine = jnp.stack([1 - xl, xl]), jnp.stack([xl, xl])
    there = jnp.stack([xl, 1 - xl])
    whole, shape = (), (rows, 2 * n_z * width)
    for pixels, (low, size) in zip(gathered, spans, strict=True):
        pixels, *whole = lax.optimization_barrier((pixels, *whole))
        sent = correlate(
            theirs,
            readings,
            pixels,
            pl.BlockSpec((None, rows, size), lambda z, h: (z, 0, 0)),
            (n_z, rows, size),
        )
        arrived = lax.ppermute(sent, "xl", [(0, 1), (1, 0)])
        spec = block_columns(rows, width, low, size)
        own = correlate(mine, readings, pixels, spec, shape, *whole)
        whole = (place(there, arrived, spec, own),)
    return whole[0]


def solution(mesh):
    torus = Mesh(mesh.devices.reshape(8, 2, 2, 8, 2), AXES)
    return jax.shard_map(
        body,
        mesh=torus,
        in_specs=(P(None, None, AXES), P()),
        out_specs=P(("z", "xl"), ("y", "xh", "core")),
        check_vma=False,
    )
```

time: 154 us -> 148 us (0.961)
  blocking collectives: 106 us -> 0 us
  waiting for transfers between devices: 0.73 us -> 53.2 us
  starting transfers between devices: 1.92 us -> 32.3 us
  Pallas kernels: 13.1 us -> 40.7 us
  local copies, waits for them, and re-layouts: 10.9 us -> 4.58 us
  matrix products: 4.58 us -> 0 us
    all_to_all x4 -> x0, blocking collectives: 106 us -> none  [the longest x1 29 us: body(): part = lax.all_to_all(part, X, 0, 0, tiled=True)]
    all_to_all x0 -> x3, waiting for transfers between devices: none -> 34.1 us  [the longest x1 14 us: one_round(): lax.all_to_all(part.reshape(n_plane, piece, depth), PLANE, 0, 0, tiled=True)]
    pallas_call x2 -> x9, Pallas kernels: 13.1 us -> 40.7 us  [the longest x4 28 us: correlate(): pl.pallas_call(functools.partial(correlate_kernel, 1.0 / math.sqrt(depth)...]
    all_to_all x0 -> x3, starting transfers between devices: none -> 26.8 us  [the longest x1 10.6 us: one_round(): lax.all_to_all(part.reshape(n_plane, piece, depth), PLANE, 0, 0, tiled=True)]
    ppermute x1 -> x2, waiting for transfers between devices: 0.01 us -> 9.59 us  [body(): arrived = lax.ppermute(sent, 'xl', [(0, 1), (1, 0)])]
    all_gather x1 -> x2, waiting for transfers between devices: 0.02 us -> 9.46 us  [body(): lax.all_gather(lax.slice_in_dim(temps, low, low + size, axis=2), 'z')]
    dot_general x1 -> x0, matrix products: 4.58 us -> none  [body(): jnp.einsum('hck,zkp->hzcp', readings.reshape(n_xl, per_z // n_xl, depth),...]
    ppermute x1 -> x2, starting transfers between devices: 1.92 us -> 5.48 us  [body(): arrived = lax.ppermute(sent, 'xl', [(0, 1), (1, 0)])]
  transfers between devices with their start and end apart: 2 -> 7, of which waited for: 0 -> 5; matrix products, arithmetic and copies ran while one was open for 3% -> 3% of each run, Pallas kernels for 9% -> 21%
where the time goes in v2:
time: 148 us; the launch traced here: 147 us
  waiting for transfers between devices  53.2 us (36%)
  Pallas kernels  40.7 us (28%)
  starting transfers between devices  32.3 us (22%)
  between operations  14.1 us (10%)
  local copies, waits for them, and re-layouts  4.58 us (3%)
  other arithmetic  1.63 us (1%)
    pallas_call x4, Pallas kernels, correlate(): pl.pallas_call(functools.partial(correlate_kernel, 1.0 / math.sqrt(depth)...  28 us
    all_to_all x1, waiting for transfers between devices, one_round(): lax.all_to_all(part.reshape(n_plane, piece, depth), PLANE, 0, 0, tiled=True)  14 us
    all_to_all x1, waiting for transfers between devices, one_round(): lax.all_to_all(part, PLANE, 0, 0, tiled=True).reshape(per_z, depth)  12.2 us
    all_to_all x1, starting transfers between devices, one_round(): lax.all_to_all(part.reshape(n_plane, piece, depth), PLANE, 0, 0, tiled=True)  10.6 us
    all_to_all x1, starting transfers between devices, one_round(): lists = lax.all_to_all(lists, 'z', 0, 0, tiled=True)  10.3 us
    ppermute x2, waiting for transfers between devices, body(): arrived = lax.ppermute(sent, 'xl', [(0, 1), (1, 0)])  9.59 us
    all_gather x2, waiting for transfers between devices, body(): lax.all_gather(lax.slice_in_dim(temps, low, low + size, axis=2), 'z')  9.46 us
    all_to_all x1, waiting for transfers between devices, one_round(): lists = lax.all_to_all(lists, 'z', 0, 0, tiled=True)  7.95 us
  transfers between devices with their start and end apart: 7, of which 5 were waited for; matrix products, arithmetic and copies ran while one was open for 3% of the time, Pallas kernels for 21%

profile of v2, /device:TPU:6, one launch (start us, length us, event | category | flops | bytes accessed | tf_op | source)
XLA Modules:
  0.0 146.6 jit_solution(1399473983949042879)
XLA Ops:
  6.5 2.0 %slice.7 = bf16[12,64,384]{2,1,0:T(8,128)(2,1)} slice(bf16[12,64,512]{2,1,0:T(8,128)(2,1)} %temps_ref.1), slice={[0:12], [0:64], [0:384]} | slice | bytes 1179648 | tf_op jit(solution)/shard_map/slice | solution.py:233
  8.6 0.1 pad_add_fusion.5.scalar_ref
  8.7 3.3 %compact.5 = bf16[8,16,128]{2,1,0:T(8,128)(2,1)} custom-call(s32[2]{0:T(128)S(1)} %pad_add_fusion.5.scalar_ref, s32[12,2048]{1,0:T(8,128)} %sensors_ref.4, bf16[12,64,512]{2,1,0:T(8,128)(2,1)S(1)} %copy-done), custom_call_target="tpu_custom_call" | custom-call | tf_op jit(solution)/shard_map/compact/pallas_call | solution.py:79
  12.0 10.3 %all-to-all-start.3 = ((bf16[8,16,128]{2,1,0:T(8,128)(2,1)}), bf16[8,16,128]{2,1,0:T(8,128)(2,1)S(1)}, u32[]{:S(2)}, u32[]{:S(2)}) async-start(bf16[8,16,128]{2,1,0:T(8,128)(2,1)} %compact.5), calls=%async_computation.3 | async-start | bytes 65536 | tf_op jit(solution)/shard_map/all_to_all | solution.py:245
  22.3 0.1 pad_add_fusion.4.scalar_ref
  22.4 8.0 %all-to-all-done.3.lists_ref = bf16[8,16,128]{2,1,0:T(8,128)(2,1)S(1)} async-done(((bf16[8,16,128]{2,1,0:T(8,128)(2,1)}), bf16[8,16,128]{2,1,0:T(8,128)(2,1)S(1)}, u32[]{:S(2)}, u32[]{:S(2)}) %all-to-all-start.3) | async-done | bytes 32800 | tf_op jit(solution)/shard_map/all_to_all | solution.py:245
  30.3 1.8 %expand.5 = bf16[256,768]{1,0:T(8,128)(2,1)S(1)} custom-call(s32[3]{0:T(128)S(1)} %pad_add_fusion.4.scalar_ref, s32[12,2048]{1,0:T(8,128)S(1)} %copy-done.1, bf16[8,16,128]{2,1,0:T(8,128)(2,1)S(1)} %all-to-all-done.3.lists_ref), custom_call_target="tpu_custom_call" | custom-call | tf_op jit(solution)/shard_map/expand/pallas_call | solution.py:121
  32.2 0.9 reshape.28
  33.0 10.6 %all-to-all-start.4 = ((bf16[64,4,768]{2,1,0:T(4,128)(2,1)}), bf16[64,4,768]{2,1,0:T(4,128)(2,1)S(1)}, u32[]{:S(2)}, u32[]{:S(2)}) async-start(bf16[64,4,768]{2,1,0:T(4,128)(2,1)} %reshape.28), calls=%async_computation.4 | async-start | bytes 786432 | tf_op jit(solution)/shard_map/all_to_all | solution.py:248
  43.6 0.0 all-gather.5.cloned.1.call-start
  43.7 0.7 slice.6
  44.4 14.0 %all-to-all-done.4 = bf16[64,4,768]{2,1,0:T(4,128)(2,1)S(1)} async-done(((bf16[64,4,768]{2,1,0:T(4,128)(2,1)}), bf16[64,4,768]{2,1,0:T(4,128)(2,1)S(1)}, u32[]{:S(2)}, u32[]{:S(2)}) %all-to-all-start.4) | async-done | bytes 393248 | tf_op jit(solution)/shard_map/all_to_all | solution.py:248
  58.4 0.2 reduce_sum.24
  58.6 0.9 broadcast_in_dim.7
  59.5 5.9 %all-to-all-start.5 = ((bf16[64,4,768]{2,1,0:T(4,128)(2,1)}), bf16[64,4,768]{2,1,0:T(4,128)(2,1)S(1)}, u32[]{:S(2)}, u32[]{:S(2)}) async-start(bf16[64,4,768]{2,1,0:T(4,128)(2,1)} %broadcast_in_dim.7), calls=%async_computation.5 | async-start | bytes 786432 | tf_op jit(solution)/shard_map/all_to_all | solution.py:251
  65.4 0.6 pad_add_fusion.3.scalar_ref
  66.0 1.3 longest.1
  68.0 12.2 %all-to-all-done.5 = bf16[64,4,768]{2,1,0:T(4,128)(2,1)S(1)} async-done(((bf16[64,4,768]{2,1,0:T(4,128)(2,1)}), bf16[64,4,768]{2,1,0:T(4,128)(2,1)S(1)}, u32[]{:S(2)}, u32[]{:S(2)}) %all-to-all-start.5) | async-done | bytes 393248 | tf_op jit(solution)/shard_map/all_to_all | solution.py:251
  80.1 0.1 reshape.29
  80.2 0.0 all-gather.7.cloned.1.call-done
  80.3 7.5 %correlate.4 = bf16[8,128,384]{2,1,0:T(8,128)(2,1)} custom-call(s32[2]{0:T(128)} %pad_add_fusion.3.scalar_ref, bf16[256,768]{1,0:T(8,128)(2,1)S(1)} %get-tuple-element.116.readings_ref, bf16[8,768,384]{2,1,0:T(8,128)(2,1)} %bitcast.20), custom_call_target="tpu_custom_call" | custom-call | flops 603979776 | bytes 4718592 | tf_op jit(solution)/shard_map/correlate/pallas_call | solution.py:176
  87.8 2.7 %collective-permute-start = (bf16[8,128,384]{2,1,0:T(8,128)(2,1)}, bf16[8,128,384]{2,1,0:T(8,128)(2,1)S(1)}, u32[]{:S(2)}, u32[]{:S(2)}) collective-permute-start(bf16[8,128,384]{2,1,0:T(8,128)(2,1)} %correlate.4), channel_id=1, source_target_pairs={{0,1},{1,0},{2,3},{3,2},{4,5},{5,4},{6,7},{7,6},{8,9},{9,8},{10,11... | collective-permute-start | bytes 2359304 | tf_op jit(solution)/shard_map/ppermute | solution.py:273
  90.5 0.6 pad_add_fusion.6.scalar_ref
  91.1 0.1 pad_add_fusion.2.scalar_ref
  91.1 7.5 %correlate.5.whole_ref = bf16[128,8192]{1,0:T(8,128)(2,1)} custom-call(s32[2]{0:T(128)} %pad_add_fusion.6.scalar_ref, bf16[256,768]{1,0:T(8,128)(2,1)S(1)} %get-tuple-element.116.readings_ref, bf16[8,768,384]{2,1,0:T(8,128)(2,1)} %bitcast.21), custom_call_target="tpu_custom_call" | custom-call | flops 603979776 | bytes 4718592 | tf_op jit(solution)/shard_map/correlate/pallas_call | solution.py:176
  98.7 9.6 %collective-permute-done.block_ref = bf16[8,128,384]{2,1,0:T(8,128)(2,1)S(1)} collective-permute-done((bf16[8,128,384]{2,1,0:T(8,128)(2,1)}, bf16[8,128,384]{2,1,0:T(8,128)(2,1)S(1)}, u32[]{:S(2)}, u32[]{:S(2)}) %collective-permute-start) | collective-permute-done | bytes 786464 | tf_op jit(solution)/shard_map/ppermute | solution.py:273
  108.2 3.2 %place.2.rest_0_ = bf16[128,8192]{1,0:T(8,128)(2,1)} custom-call(s32[2]{0:T(128)S(1)} %pad_add_fusion.2.scalar_ref, bf16[8,128,384]{2,1,0:T(8,128)(2,1)S(1)} %collective-permute-done.block_ref, bf16[128,8192]{1,0:T(8,128)(2,1)} %correlate.5.whole_ref), custom_call_target="tpu_custom_call", output_to_operand_aliasing={{}: (2, {})} | custom-call | tf_op jit(solution)/shard_map/place/pallas_call | solution.py:204
  111.4 9.4 %all-gather.5.cloned.1.call-done = bf16[96,64,128]{2,1,0:T(8,128)(2,1)} async-done(((bf16[12,64,128]{2,1,0:T(8,128)(2,1)}), bf16[96,64,128]{2,1,0:T(8,128)(2,1)}) %all-gather.5.cloned.1.call-update) | async-done | bytes 1572880 | tf_op jit(solution)/shard_map/all_gather | solution.py:233
  120.9 6.5 %correlate.6 = bf16[8,128,128]{2,1,0:T(8,128)(2,1)} custom-call(s32[2]{0:T(128)} %pad_add_fusion.3.scalar_ref, bf16[256,768]{1,0:T(8,128)(2,1)S(1)} %get-tuple-element.116.readings_ref, bf16[8,768,128]{2,1,0:T(8,128)(2,1)} %bitcast.22), custom_call_target="tpu_custom_call" | custom-call | flops 201326592 | bytes 1572864 | tf_op jit(solution)/shard_map/correlate/pallas_call | solution.py:176
  127.4 2.7 %collective-permute-start.1 = (bf16[8,128,128]{2,1,0:T(8,128)(2,1)}, bf16[8,128,128]{2,1,0:T(8,128)(2,1)S(1)}, u32[]{:S(2)}, u32[]{:S(2)}) collective-permute-start(bf16[8,128,128]{2,1,0:T(8,128)(2,1)} %correlate.6), channel_id=1, source_target_pairs={{0,1},{1,0},{2,3},{3,2},{4,5},{5,4},{6,7},{7,6},{8,9},{9,8},{10,11... | collective-permute-start | bytes 786440 | tf_op jit(solution)/shard_map/ppermute | solution.py:273
  130.1 6.5 %correlate.7.whole_ref = bf16[128,8192]{1,0:T(8,128)(2,1)} custom-call(s32[2]{0:T(128)} %pad_add_fusion.6.scalar_ref, bf16[256,768]{1,0:T(8,128)(2,1)S(1)} %get-tuple-element.116.readings_ref, bf16[8,768,128]{2,1,0:T(8,128)(2,1)} %bitcast.23, bf16[128,8192]{1,0:T(8,128)(2,1)} %place.2.rest_0_), custom_call_target="tpu_custom_call", output_to_operand_aliasing={{}: (3, {})} | custom-call | flops 201326592 | bytes 1572864 | tf_op jit(solution)/shard_map/correlate/pallas_call | solution.py:176
  136.6 3.1 %place.3 = bf16[128,8192]{1,0:T(8,128)(2,1)} custom-call(s32[2]{0:T(128)S(1)} %pad_add_fusion.2.scalar_ref, bf16[8,128,128]{2,1,0:T(8,128)(2,1)S(1)} %collective-permute-done.1.block_ref, bf16[128,8192]{1,0:T(8,128)(2,1)} %correlate.7.whole_ref), custom_call_target="tpu_custom_call", output_to_operand_aliasing={{}: (2, {})} | custom-call | tf_op jit(solution)/shard_map/place/pallas_call | solution.py:204
  (9 shorter events, 0.1 us)
Async XLA Ops:
  6.5 2.1 %copy-start = (bf16[12,64,512]{2,1,0:T(8,128)(2,1)S(1)}, bf16[12,64,512]{2,1,0:T(8,128)(2,1)}, u32[]{:S(2)}) copy-start(bf16[12,64,512]{2,1,0:T(8,128)(2,1)} %temps_ref.1) | copy-start | bytes 2359300
  6.5 23.8 %copy-start.1 = (s32[12,2048]{1,0:T(8,128)S(1)}, s32[12,2048]{1,0:T(8,128)}, u32[]{:S(2)}) copy-start(s32[12,2048]{1,0:T(8,128)} %sensors_ref.4) | copy-start | bytes 294916
  6.5 73.7 %all-gather.7.cloned.1.call-start = ((), (), s32[]{:S(2)}) async-start(), calls=%async_computation.7 | async-start | bytes 5308416 | tf_op jit(solution)/shard_map/all_gather | solution.py:233
  12.0 18.3 %all-to-all-start.3 = ((bf16[8,16,128]{2,1,0:T(8,128)(2,1)}), bf16[8,16,128]{2,1,0:T(8,128)(2,1)S(1)}, u32[]{:S(2)}, u32[]{:S(2)}) async-start(bf16[8,16,128]{2,1,0:T(8,128)(2,1)} %compact.5), calls=%async_computation.3 | async-start | bytes 65536 | tf_op jit(solution)/shard_map/all_to_all | solution.py:245
  33.0 25.4 %all-to-all-start.4 = ((bf16[64,4,768]{2,1,0:T(4,128)(2,1)}), bf16[64,4,768]{2,1,0:T(4,128)(2,1)S(1)}, u32[]{:S(2)}, u32[]{:S(2)}) async-start(bf16[64,4,768]{2,1,0:T(4,128)(2,1)} %reshape.28), calls=%async_computation.4 | async-start | bytes 786432 | tf_op jit(solution)/shard_map/all_to_all | solution.py:248
  43.6 77.2 %all-gather.5.cloned.1.call-start = ((), (), s32[]{:S(2)}) async-start(), calls=%async_computation.6 | async-start | bytes 1769472 | tf_op jit(solution)/shard_map/all_gather | solution.py:233
  59.5 20.7 %all-to-all-start.5 = ((bf16[64,4,768]{2,1,0:T(4,128)(2,1)}), bf16[64,4,768]{2,1,0:T(4,128)(2,1)S(1)}, u32[]{:S(2)}, u32[]{:S(2)}) async-start(bf16[64,4,768]{2,1,0:T(4,128)(2,1)} %broadcast_in_dim.7), calls=%async_computation.5 | async-start | bytes 786432 | tf_op jit(solution)/shard_map/all_to_all | solution.py:251
  87.8 20.5 %collective-permute-start = (bf16[8,128,384]{2,1,0:T(8,128)(2,1)}, bf16[8,128,384]{2,1,0:T(8,128)(2,1)S(1)}, u32[]{:S(2)}, u32[]{:S(2)}) collective-permute-start(bf16[8,128,384]{2,1,0:T(8,128)(2,1)} %correlate.4), channel_id=1, source_target_pairs={{0,1},{1,0},{2,3},{3,2},{4,5},{5,4},{6,7},{7,6},{8,9},{9,8},{10,11... | collective-permute-start | bytes 2359304 | tf_op jit(solution)/shard_map/ppermute | solution.py:273
  127.4 9.3 %collective-permute-start.1 = (bf16[8,128,128]{2,1,0:T(8,128)(2,1)}, bf16[8,128,128]{2,1,0:T(8,128)(2,1)S(1)}, u32[]{:S(2)}, u32[]{:S(2)}) collective-permute-start(bf16[8,128,128]{2,1,0:T(8,128)(2,1)} %correlate.6), channel_id=1, source_target_pairs={{0,1},{1,0},{2,3},{3,2},{4,5},{5,4},{6,7},{7,6},{8,9},{9,8},{10,11... | collective-permute-start | bytes 786440 | tf_op jit(solution)/shard_map/ppermute | solution.py:273
Sparse Core Ops, SparseCore 0:
  9.4 67.7 all-gather.6
  79.3 41.5 all-gather.4

commit v3 on v2

--- a/solution.py
+++ b/solution.py
@@ -12,12 +12,12 @@
 AXES = ("y", "xh", "core", "z", "xl")
 PLANE = ("y", "xh", "xl", "core")
 SLOTS = 32
-FIRST = 384
 F32, BF16 = jnp.float32, jnp.bfloat16
 PARAMS = pltpu.CompilerParams(vmem_limit_bytes=16 * 2**20)
 NT = (((1,), (1,)), ((), ()))
 VMEM = pl.BlockSpec(memory_space=pltpu.VMEM)
 SMEM = pl.BlockSpec(memory_space=pltpu.SMEM)
+HBM = pl.BlockSpec(memory_space=pl.ANY)
 
 
 def matmul(a, b, dims=(((1,), (0,)), ((), ()))):
@@ -158,61 +158,72 @@
     )(sensors)[0, 0]
 
 
-def correlate_kernel(scale, scalar_ref, readings_ref, pixels_ref, *rest):
-    summed = matmul(readings_ref[...], pixels_ref[...])
-    rest[-1][...] = (summed * scale).astype(BF16)
-
-
-def block_columns(rows, stride, skipped, width):
-    def place_of(z, h):
-        return 0, pl.multiple_of((2 * z + h[1]) * stride + skipped, 128)
-
-    return pl.BlockSpec((pl.Element(rows), pl.Element(width)), place_of)
-
-
-def correlate(half, readings, pixels, out_spec, out_shape, *whole):
+def correlate_kernel(scale, scalar_ref, readings_ref, pixels_ref, out_ref, taken, done, *rest):
+    n_z, _, width = taken.shape
+    rows = readings_ref.shape[0] // 2
+    loads = [pltpu.make_async_copy(pixels_ref.at[z], taken.at[z], done.at[z]) for z in range(n_z)]
+    for load in loads:
+        load.start()
+    readings = readings_ref[pl.ds(pl.multiple_of(scalar_ref[0] * rows, rows), rows)]
+    stores = []
+    for z in range(n_z):
+        loads[z].wait()
+        summed = (matmul(readings, taken[z]) * scale).astype(BF16)
+        if not rest:
+            out_ref[z] = summed
+            continue
+        made, stored = rest
+        made[z] = summed
+        spot = pl.multiple_of((2 * z + scalar_ref[0]) * width, width)
+        stores.append(
+            pltpu.make_async_copy(made.at[z], out_ref.at[:, pl.ds(spot, width)], stored.at[z])
+        )
+        stores[-1].start()
+    for store in stores:
+        store.wait()
+
+
+def correlate(half, readings, pixels, placed):
     n_z, depth, width = pixels.shape
     rows = readings.shape[0] // 2
+    blocks = (n_z, rows, width)
+    scratch = [pltpu.VMEM(pixels.shape, BF16), pltpu.SemaphoreType.DMA((n_z,))]
+    if placed:
+        scratch += [pltpu.VMEM(blocks, BF16), pltpu.SemaphoreType.DMA((n_z,))]
     return pl.pallas_call(
         functools.partial(correlate_kernel, 1.0 / math.sqrt(depth)),
-        grid_spec=pltpu.PrefetchScalarGridSpec(
-            num_scalar_prefetch=1,
-            grid=(n_z,),
-            in_specs=[
-                pl.BlockSpec((rows, depth), lambda z, h: (h[0], 0)),
-                pl.BlockSpec((None, depth, width), lambda z, h: (z, 0, 0)),
-            ]
-            + [pl.BlockSpec(memory_space=pl.ANY)] * len(whole),
-            out_specs=out_spec,
-        ),
-        out_shape=jax.ShapeDtypeStruct(out_shape, BF16),
-        input_output_aliases={3: 0} if whole else {},
+        in_specs=[SMEM, VMEM, HBM],
+        out_specs=HBM if placed else VMEM,
+        out_shape=jax.ShapeDtypeStruct((rows, 2 * n_z * width) if placed else blocks, BF16),
+        scratch_shapes=scratch,
         cost_estimate=pl.CostEstimate(
             flops=2 * rows * depth * width * n_z, bytes_accessed=pixels.size * 2, transcendentals=0
         ),
-        compiler_params=pltpu.CompilerParams(vmem_limit_bytes=59 * 2**20),
+        compiler_params=pltpu.CompilerParams(vmem_limit_bytes=58 * 2**20),
         name="correlate",
-    )(half, readings, pixels, *whole)
-
-
-def place_kernel(scalar_ref, block_ref, whole_ref, out_ref):
-    out_ref[...] = block_ref[...]
-
-
-def place(side, blocks, out_spec, whole):
-    n_z, rows, width = blocks.shape
+    )(half, readings, pixels)
+
+
+def place_kernel(scalar_ref, blocks_ref, whole_ref, out_ref, done):
+    n_z, _, width = blocks_ref.shape
+    stores = []
+    for z in range(n_z):
+        spot = pl.multiple_of((2 * z + scalar_ref[0]) * width, width)
+        stores.append(
+            pltpu.make_async_copy(blocks_ref.at[z], out_ref.at[:, pl.ds(spot, width)], done.at[z])
+        )
+        stores[-1].start()
+    for store in stores:
+        store.wait()
+
+
+def place(side, blocks, whole):
     return pl.pallas_call(
         place_kernel,
-        grid_spec=pltpu.PrefetchScalarGridSpec(
-            num_scalar_prefetch=1,
-            grid=(n_z,),
-            in_specs=[
-                pl.BlockSpec((None, rows, width), lambda z, h: (z, 0, 0)),
-                pl.BlockSpec(memory_space=pl.ANY),
-            ],
-            out_specs=out_spec,
-        ),
+        in_specs=[SMEM, HBM, HBM],
+        out_specs=HBM,
         out_shape=jax.ShapeDtypeStruct(whole.shape, BF16),
+        scratch_shapes=[pltpu.SemaphoreType.DMA((blocks.shape[0],))],
         input_output_aliases={2: 0},
         compiler_params=PARAMS,
         name="place",
@@ -225,16 +236,9 @@
     n_z, n_plane, devices = (lax.axis_size(a) for a in ("z", PLANE, AXES))
     per_z = sensors.shape[1] // n_z
     piece = per_z // n_plane
-    rows = per_z // 2
     z, xl = lax.axis_index("z"), lax.axis_index("xl")
 
-    spans = [(0, FIRST), (FIRST, width - FIRST)]
-    gathered = [
-        lax.all_gather(lax.slice_in_dim(temps, low, low + size, axis=2), "z").reshape(
-            n_z, depth, size
-        )
-        for low, size in spans
-    ]
+    gathered = lax.all_gather(temps, "z").reshape(n_z, depth, width)
 
     first = lax.axis_index(AXES) * width
     column_first = first - z * lax.axis_size("xl") * width
@@ -258,23 +262,11 @@
         (jnp.int32(1), readings),
     )
 
-    theirs, mine = jnp.stack([1 - xl, xl]), jnp.stack([xl, xl])
-    there = jnp.stack([xl, 1 - xl])
-    whole, shape = (), (rows, 2 * n_z * width)
-    for pixels, (low, size) in zip(gathered, spans, strict=True):
-        pixels, *whole = lax.optimization_barrier((pixels, *whole))
-        sent = correlate(
-            theirs,
-            readings,
-            pixels,
-            pl.BlockSpec((None, rows, size), lambda z, h: (z, 0, 0)),
-            (n_z, rows, size),
-        )
-        arrived = lax.ppermute(sent, "xl", [(0, 1), (1, 0)])
-        spec = block_columns(rows, width, low, size)
-        own = correlate(mine, readings, pixels, spec, shape, *whole)
-        whole = (place(there, arrived, spec, own),)
-    return whole[0]
+    own, other = jnp.stack([xl]), jnp.stack([1 - xl])
+    sent = correlate(other, readings, gathered, False)
+    arrived = lax.ppermute(sent, "xl", [(0, 1), (1, 0)])
+    whole = correlate(own, readings, gathered, True)
+    return place(other, arrived, whole)
 
 
 def solution(mesh):

time: 148 us -> 132 us (0.89)
  blocking collectives: 0 us -> 25.3 us
  Pallas kernels: 40.7 us -> 16.7 us
  starting transfers between devices: 32.3 us -> 19.1 us
  local copies, waits for them, and re-layouts: 4.58 us -> 1.05 us
    all_to_all x0 -> x1, blocking collectives: none -> 25.3 us  [one_round(): lax.all_to_all(part.reshape(n_plane, piece, depth), PLANE, 0, 0, tiled=True)]
    pallas_call x4 -> x2, Pallas kernels: 28 us -> 8.54 us  [correlate(): pl.pallas_call(functools.partial(correlate_kernel, 1.0 / math.sqrt(depth)...]
    all_to_all x1 -> x0, waiting for transfers between devices: 14 us -> none  [one_round(): lax.all_to_all(part.reshape(n_plane, piece, depth), PLANE, 0, 0, tiled=True)]
    all_to_all x1 -> x0, starting transfers between devices: 10.6 us -> none  [one_round(): lax.all_to_all(part.reshape(n_plane, piece, depth), PLANE, 0, 0, tiled=True)]
    ppermute x2 -> x1, waiting for transfers between devices: 9.59 us -> 20.1 us  [body(): arrived = lax.ppermute(sent, 'xl', [(0, 1), (1, 0)])]
    pallas_call x2 -> x1, Pallas kernels: 6.27 us -> 1.02 us  [place(): pl.pallas_call(place_kernel, in_specs=[SMEM, HBM, HBM], out_specs=HBM, ou...]
    all_gather x2 -> x1, waiting for transfers between devices: 9.46 us -> 13.1 us  [body(): gathered = lax.all_gather(temps, 'z').reshape(n_z, depth, width)]
    slice x2 -> x0, local copies, waits for them, and re-layouts: 2.74 us -> none  [body(): lax.slice_in_dim(temps, low, low + size, axis=2)]
  transfers between devices with their start and end apart: 7 -> 4, of which waited for: 5 -> 4; matrix products, arithmetic and copies ran while one was open for 3% -> 1% of each run, Pallas kernels for 21% -> 9%
where the time goes in v3:
time: 132 us; the launch traced here: 131 us
  waiting for transfers between devices  54.6 us (41%)
  blocking collectives  25.3 us (19%)
  starting transfers between devices  19.1 us (14%)
  Pallas kernels  16.7 us (13%)
  between operations  14.2 us (11%)
    all_to_all x1, blocking collectives, one_round(): lax.all_to_all(part.reshape(n_plane, piece, depth), PLANE, 0, 0, tiled=True)  25.3 us
    ppermute x1, waiting for transfers between devices, body(): arrived = lax.ppermute(sent, 'xl', [(0, 1), (1, 0)])  20.1 us
    all_gather x1, waiting for transfers between devices, body(): gathered = lax.all_gather(temps, 'z').reshape(n_z, depth, width)  13.1 us
    all_to_all x1, waiting for transfers between devices, one_round(): lax.all_to_all(part, PLANE, 0, 0, tiled=True).reshape(per_z, depth)  12.8 us
    all_to_all x1, starting transfers between devices, one_round(): lists = lax.all_to_all(lists, 'z', 0, 0, tiled=True)  10.4 us
    pallas_call x2, Pallas kernels, correlate(): pl.pallas_call(functools.partial(correlate_kernel, 1.0 / math.sqrt(depth)...  8.54 us
    all_to_all x1, waiting for transfers between devices, one_round(): lists = lax.all_to_all(lists, 'z', 0, 0, tiled=True)  7.95 us
    all_to_all x1, starting transfers between devices, one_round(): lax.all_to_all(part, PLANE, 0, 0, tiled=True).reshape(per_z, depth)  5.89 us
  transfers between devices with their start and end apart: 4, of which 4 were waited for; matrix products, arithmetic and copies ran while one was open for 1% of the time, Pallas kernels for 9%

profile of v3, /device:TPU:6, one launch (start us, length us, event | category | flops | bytes accessed | tf_op | source)
XLA Modules:
  0.0 131.3 jit_solution(6693201194500816949)
XLA Ops:
  6.5 0.0 all-gather.3.cloned.1.call-start
  6.5 0.7 all-gather.3.cloned.1.call-update
  7.3 0.1 pad_add_fusion.3.scalar_ref
  7.4 3.6 %compact.5 = bf16[8,16,128]{2,1,0:T(8,128)(2,1)} custom-call(s32[2]{0:T(128)S(1)} %pad_add_fusion.3.scalar_ref, s32[12,2048]{1,0:T(8,128)} %sensors_ref.4, bf16[12,64,512]{2,1,0:T(8,128)(2,1)} %temps_ref.1), custom_call_target="tpu_custom_call" | custom-call | tf_op jit(solution)/shard_map/compact/pallas_call | solution.py:79
  11.0 0.0 copy-start.1
  11.0 10.4 %all-to-all-start.3 = ((bf16[8,16,128]{2,1,0:T(8,128)(2,1)}), bf16[8,16,128]{2,1,0:T(8,128)(2,1)S(1)}, u32[]{:S(2)}, u32[]{:S(2)}) async-start(bf16[8,16,128]{2,1,0:T(8,128)(2,1)} %compact.5), calls=%async_computation.3 | async-start | bytes 65536 | tf_op jit(solution)/shard_map/all_to_all | solution.py:249
  21.4 0.1 pad_add_fusion.2.scalar_ref
  21.5 8.0 %all-to-all-done.3.lists_ref = bf16[8,16,128]{2,1,0:T(8,128)(2,1)S(1)} async-done(((bf16[8,16,128]{2,1,0:T(8,128)(2,1)}), bf16[8,16,128]{2,1,0:T(8,128)(2,1)S(1)}, u32[]{:S(2)}, u32[]{:S(2)}) %all-to-all-start.3) | async-done | bytes 32800 | tf_op jit(solution)/shard_map/all_to_all | solution.py:249
  29.5 2.2 %expand.5 = bf16[256,768]{1,0:T(8,128)(2,1)S(1)} custom-call(s32[3]{0:T(128)S(1)} %pad_add_fusion.2.scalar_ref, s32[12,2048]{1,0:T(8,128)} %sensors_ref.4, bf16[8,16,128]{2,1,0:T(8,128)(2,1)S(1)} %all-to-all-done.3.lists_ref), custom_call_target="tpu_custom_call" | custom-call | tf_op jit(solution)/shard_map/expand/pallas_call | solution.py:121
  31.7 0.0 copy-start
  31.7 0.1 reshape.25
  31.8 25.3 %all_to_all.39 = bf16[64,4,768]{2,1,0:T(4,128)(2,1)S(1)} all-to-all(bf16[64,4,768]{2,1,0:T(4,128)(2,1)S(1)} %reshape.25), channel_id=1, replica_groups=mesh['y'=8,'xh'=2,'core'=2,'z'=8,'xl'=2] {'y','xh','xl','core'}, dimensions={0} | all-to-all | bytes 786432 | tf_op jit(solution)/shard_map/all_to_all | solution.py:252
  57.1 0.2 reduce_sum.24
  57.3 0.9 broadcast_in_dim.7
  58.1 5.9 %all-to-all-start.5 = ((bf16[64,4,768]{2,1,0:T(4,128)(2,1)}), bf16[64,4,768]{2,1,0:T(4,128)(2,1)S(1)}, u32[]{:S(2)}, u32[]{:S(2)}) async-start(bf16[64,4,768]{2,1,0:T(4,128)(2,1)} %broadcast_in_dim.7), calls=%async_computation.5 | async-start | bytes 786432 | tf_op jit(solution)/shard_map/all_to_all | solution.py:255
  64.0 0.0 copy-done.1
  64.0 1.3 %longest.1 = s32[1,1]{1,0:T(1,128)} custom-call(s32[12,2048]{1,0:T(8,128)S(1)} %copy-done.1), custom_call_target="tpu_custom_call" | custom-call | flops 25165824 | bytes 98304 | tf_op jit(solution)/shard_map/longest/pallas_call | solution.py:148
  66.0 12.8 %all-to-all-done.5 = bf16[64,4,768]{2,1,0:T(4,128)(2,1)S(1)} async-done(((bf16[64,4,768]{2,1,0:T(4,128)(2,1)}), bf16[64,4,768]{2,1,0:T(4,128)(2,1)S(1)}, u32[]{:S(2)}, u32[]{:S(2)}) %all-to-all-start.5) | async-done | bytes 393248 | tf_op jit(solution)/shard_map/all_to_all | solution.py:255
  78.8 0.1 reshape.26
  78.9 0.0 copy-done
  78.9 13.1 %all-gather.3.cloned.1.call-done = bf16[96,64,512]{2,1,0:T(8,128)(2,1)} async-done(((bf16[12,64,512]{2,1,0:T(8,128)(2,1)}), bf16[96,64,512]{2,1,0:T(8,128)(2,1)}) %all-gather.3.cloned.1.call-update) | async-done | bytes 6291472 | tf_op jit(solution)/shard_map/all_gather | solution.py:241
  92.0 4.4 %correlate.2 = bf16[8,128,512]{2,1,0:T(8,128)(2,1)} custom-call(s32[1]{0:T(128)} %bitcast.4.scalar_ref, bf16[256,768]{1,0:T(8,128)(2,1)S(1)} %get-tuple-element.114.readings_ref, bf16[8,768,512]{2,1,0:T(8,128)(2,1)} %bitcast.19), custom_call_target="tpu_custom_call" | custom-call | flops 805306368 | bytes 6291456 | tf_op jit(solution)/shard_map/correlate/pallas_call | solution.py:193
  96.4 2.8 %collective-permute-start = (bf16[8,128,512]{2,1,0:T(8,128)(2,1)}, bf16[8,128,512]{2,1,0:T(8,128)(2,1)S(1)}, u32[]{:S(2)}, u32[]{:S(2)}) collective-permute-start(bf16[8,128,512]{2,1,0:T(8,128)(2,1)} %correlate.2), channel_id=1, source_target_pairs={{0,1},{1,0},{2,3},{3,2},{4,5},{5,4},{6,7},{7,6},{8,9},{9,8},{10,11... | collective-permute-start | bytes 3145736 | tf_op jit(solution)/shard_map/ppermute | solution.py:267
  99.2 4.1 %correlate.3.whole_ref = bf16[128,8192]{1,0:T(8,128)(2,1)} custom-call(s32[1]{0:T(128)} %bitcast.10.scalar_ref, bf16[256,768]{1,0:T(8,128)(2,1)S(1)} %get-tuple-element.114.readings_ref, bf16[8,768,512]{2,1,0:T(8,128)(2,1)} %bitcast.20), custom_call_target="tpu_custom_call" | custom-call | flops 805306368 | bytes 6291456 | tf_op jit(solution)/shard_map/correlate/pallas_call | solution.py:193
  103.3 20.1 %collective-permute-done.blocks_ref = bf16[8,128,512]{2,1,0:T(8,128)(2,1)S(1)} collective-permute-done((bf16[8,128,512]{2,1,0:T(8,128)(2,1)}, bf16[8,128,512]{2,1,0:T(8,128)(2,1)S(1)}, u32[]{:S(2)}, u32[]{:S(2)}) %collective-permute-start) | collective-permute-done | bytes 1048608 | tf_op jit(solution)/shard_map/ppermute | solution.py:267
  123.4 1.0 place.1
  (1 shorter events, 0.0 us)
Async XLA Ops:
  6.5 85.4 %all-gather.3.cloned.1.call-start = ((), (), s32[]{:S(2)}) async-start(), calls=%async_computation.6 | async-start | bytes 7077888 | tf_op jit(solution)/shard_map/all_gather | solution.py:241
  11.0 53.0 %copy-start.1 = (s32[12,2048]{1,0:T(8,128)S(1)}, s32[12,2048]{1,0:T(8,128)}, u32[]{:S(2)}) copy-start(s32[12,2048]{1,0:T(8,128)} %sensors_ref.4) | copy-start | bytes 294916
  11.0 18.5 %all-to-all-start.3 = ((bf16[8,16,128]{2,1,0:T(8,128)(2,1)}), bf16[8,16,128]{2,1,0:T(8,128)(2,1)S(1)}, u32[]{:S(2)}, u32[]{:S(2)}) async-start(bf16[8,16,128]{2,1,0:T(8,128)(2,1)} %compact.5), calls=%async_computation.3 | async-start | bytes 65536 | tf_op jit(solution)/shard_map/all_to_all | solution.py:249
  31.7 47.2 %copy-start = (bf16[12,64,512]{2,1,0:T(8,128)(2,1)S(1)}, bf16[12,64,512]{2,1,0:T(8,128)(2,1)}, u32[]{:S(2)}) copy-start(bf16[12,64,512]{2,1,0:T(8,128)(2,1)} %temps_ref.1) | copy-start | bytes 2359300
  58.1 20.7 %all-to-all-start.5 = ((bf16[64,4,768]{2,1,0:T(4,128)(2,1)}), bf16[64,4,768]{2,1,0:T(4,128)(2,1)S(1)}, u32[]{:S(2)}, u32[]{:S(2)}) async-start(bf16[64,4,768]{2,1,0:T(4,128)(2,1)} %broadcast_in_dim.7), calls=%async_computation.5 | async-start | bytes 786432 | tf_op jit(solution)/shard_map/all_to_all | solution.py:255
  96.4 27.0 %collective-permute-start = (bf16[8,128,512]{2,1,0:T(8,128)(2,1)}, bf16[8,128,512]{2,1,0:T(8,128)(2,1)S(1)}, u32[]{:S(2)}, u32[]{:S(2)}) collective-permute-start(bf16[8,128,512]{2,1,0:T(8,128)(2,1)} %correlate.2), channel_id=1, source_target_pairs={{0,1},{1,0},{2,3},{3,2},{4,5},{5,4},{6,7},{7,6},{8,9},{9,8},{10,11... | collective-permute-start | bytes 3145736 | tf_op jit(solution)/shard_map/ppermute | solution.py:267
Sparse Core Ops, SparseCore 0:
  9.4 82.4 all-gather.2

commit v4 on v3

--- a/solution.py
+++ b/solution.py
@@ -158,76 +158,122 @@
     )(sensors)[0, 0]
 
 
-def correlate_kernel(scale, scalar_ref, readings_ref, pixels_ref, out_ref, taken, done, *rest):
-    n_z, _, width = taken.shape
+def correlation(scale, readings, block):
+    depth = readings.shape[1] // len(block)
+    parts = [
+        matmul(readings[:, i * depth : (i + 1) * depth], part[...]) for i, part in enumerate(block)
+    ]
+    return (sum(parts[1:], parts[0]) * scale).astype(BF16)
+
+
+def half_of(readings_ref, side):
     rows = readings_ref.shape[0] // 2
-    loads = [pltpu.make_async_copy(pixels_ref.at[z], taken.at[z], done.at[z]) for z in range(n_z)]
-    for load in loads:
-        load.start()
-    readings = readings_ref[pl.ds(pl.multiple_of(scalar_ref[0] * rows, rows), rows)]
+    return readings_ref[pl.ds(pl.multiple_of(side * rows, rows), rows)]
+
+
+def grouped(refs, sizes):
+    refs = iter(refs)
+    return [[next(refs) for _ in range(size)] for size in sizes]
+
+
+def send_kernel(scale, sizes, scalar_ref, readings_ref, *rest):
+    readings = half_of(readings_ref, 1 - scalar_ref[1])
+    for spot, block in enumerate(grouped(rest[:-1], sizes)):
+        rest[-1][spot] = correlation(scale, readings, block)
+
+
+def keep_kernel(scale, n_z, shifts, sizes, scalar_ref, readings_ref, *rest):
+    *refs, out_ref, made, stored = rest
+    readings = half_of(readings_ref, scalar_ref[1])
     stores = []
-    for z in range(n_z):
-        loads[z].wait()
-        summed = (matmul(readings, taken[z]) * scale).astype(BF16)
-        if not rest:
-            out_ref[z] = summed
-            continue
-        made, stored = rest
-        made[z] = summed
-        spot = pl.multiple_of((2 * z + scalar_ref[0]) * width, width)
+    for spot, block in enumerate(grouped(refs, sizes)):
+        made[spot] = correlation(scale, readings, block)
         stores.append(
-            pltpu.make_async_copy(made.at[z], out_ref.at[:, pl.ds(spot, width)], stored.at[z])
+            pltpu.make_async_copy(
+                made.at[spot], columns(out_ref, n_z, shifts[spot], scalar_ref, 0), stored.at[spot]
+            )
         )
         stores[-1].start()
     for store in stores:
         store.wait()
 
 
-def correlate(half, readings, pixels, placed):
-    n_z, depth, width = pixels.shape
-    rows = readings.shape[0] // 2
-    blocks = (n_z, rows, width)
-    scratch = [pltpu.VMEM(pixels.shape, BF16), pltpu.SemaphoreType.DMA((n_z,))]
-    if placed:
-        scratch += [pltpu.VMEM(blocks, BF16), pltpu.SemaphoreType.DMA((n_z,))]
-    return pl.pallas_call(
-        functools.partial(correlate_kernel, 1.0 / math.sqrt(depth)),
-        in_specs=[SMEM, VMEM, HBM],
-        out_specs=HBM if placed else VMEM,
-        out_shape=jax.ShapeDtypeStruct((rows, 2 * n_z * width) if placed else blocks, BF16),
-        scratch_shapes=scratch,
-        cost_estimate=pl.CostEstimate(
-            flops=2 * rows * depth * width * n_z, bytes_accessed=pixels.size * 2, transcendentals=0
-        ),
-        compiler_params=pltpu.CompilerParams(vmem_limit_bytes=58 * 2**20),
-        name="correlate",
-    )(half, readings, pixels)
-
-
-def place_kernel(scalar_ref, blocks_ref, whole_ref, out_ref, done):
-    n_z, _, width = blocks_ref.shape
+def columns(out_ref, n_z, shift, scalar_ref, other):
+    width = out_ref.shape[1] // (2 * n_z)
+    side = 1 - scalar_ref[1] if other else scalar_ref[1]
+    spot = (2 * lax.rem(scalar_ref[0] + shift + n_z, n_z) + side) * width
+    return out_ref.at[:, pl.ds(pl.multiple_of(spot, width), width)]
+
+
+def place_kernel(n_z, shifts, scalar_ref, *rest):
+    *pieces, _, out_ref, done = rest
     stores = []
-    for z in range(n_z):
-        spot = pl.multiple_of((2 * z + scalar_ref[0]) * width, width)
-        stores.append(
-            pltpu.make_async_copy(blocks_ref.at[z], out_ref.at[:, pl.ds(spot, width)], done.at[z])
-        )
-        stores[-1].start()
+    for piece in pieces:
+        for i in range(piece.shape[0]):
+            spot = len(stores)
+            stores.append(
+                pltpu.make_async_copy(
+                    piece.at[i], columns(out_ref, n_z, shifts[spot], scalar_ref, 1), done.at[spot]
+                )
+            )
+            stores[-1].start()
     for store in stores:
         store.wait()
 
 
-def place(side, blocks, whole):
-    return pl.pallas_call(
-        place_kernel,
-        in_specs=[SMEM, HBM, HBM],
+def cost(blocks, rows):
+    pixels = sum(part.size for block in blocks for part in block)
+    return pl.CostEstimate(flops=2 * rows * pixels, bytes_accessed=2 * pixels, transcendentals=0)
+
+
+def send(here, readings, blocks):
+    rows, depth = readings.shape[0] // 2, readings.shape[1]
+    parts = [part for block in blocks for part in block]
+    return pl.pallas_call(
+        functools.partial(send_kernel, 1.0 / math.sqrt(depth), [len(block) for block in blocks]),
+        in_specs=[SMEM, VMEM] + [VMEM] * len(parts),
+        out_specs=VMEM,
+        out_shape=jax.ShapeDtypeStruct((len(blocks), rows, parts[0].shape[1]), BF16),
+        cost_estimate=cost(blocks, rows),
+        compiler_params=PARAMS,
+        name="send",
+    )(here, readings, *parts)
+
+
+def keep(here, readings, blocks, shifts):
+    rows, depth = readings.shape[0] // 2, readings.shape[1]
+    parts = [part for block in blocks for part in block]
+    count, width = len(blocks), parts[0].shape[1]
+    return pl.pallas_call(
+        functools.partial(
+            keep_kernel, 1.0 / math.sqrt(depth), count, shifts, [len(block) for block in blocks]
+        ),
+        in_specs=[SMEM, VMEM] + [VMEM] * len(parts),
+        out_specs=HBM,
+        out_shape=jax.ShapeDtypeStruct((rows, 2 * count * width), BF16),
+        scratch_shapes=[pltpu.VMEM((count, rows, width), BF16), pltpu.SemaphoreType.DMA((count,))],
+        cost_estimate=cost(blocks, rows),
+        compiler_params=PARAMS,
+        name="keep",
+    )(here, readings, *parts)
+
+
+def place(here, pieces, shifts, whole):
+    return pl.pallas_call(
+        functools.partial(place_kernel, len(shifts), shifts),
+        in_specs=[SMEM] + [HBM] * (len(pieces) + 1),
         out_specs=HBM,
         out_shape=jax.ShapeDtypeStruct(whole.shape, BF16),
-        scratch_shapes=[pltpu.SemaphoreType.DMA((blocks.shape[0],))],
-        input_output_aliases={2: 0},
+        scratch_shapes=[pltpu.SemaphoreType.DMA((len(shifts),))],
+        input_output_aliases={len(pieces) + 1: 0},
         compiler_params=PARAMS,
         name="place",
-    )(side, blocks, whole)
+    )(here, *pieces, whole)
+
+
+def ring(value, shift):
+    size = lax.axis_size("z")
+    return lax.ppermute(value, "z", [(i, (i + shift) % size) for i in range(size)])
 
 
 def body(temps, sensors):
@@ -238,35 +284,58 @@
     piece = per_z // n_plane
     z, xl = lax.axis_index("z"), lax.axis_index("xl")
 
-    gathered = lax.all_gather(temps, "z").reshape(n_z, depth, width)
+    pixels = temps.reshape(depth, width)
+    up, down = [pixels, ring(pixels, 1)], [pixels, ring(pixels, -1)]
+
+    def go_on(ready):
+        above, below, _ = lax.optimization_barrier((up[-1], down[-1], ready))
+        up.append(ring(above, 1))
+        down.append(ring(below, -1))
 
     first = lax.axis_index(AXES) * width
     column_first = first - z * lax.axis_size("xl") * width
 
-    def one_round(number):
+    def part_of(number):
         start = number * SLOTS
         lists = compact(jnp.stack([first, start]), sensors, temps, n_z)
         lists = lax.all_to_all(lists, "z", 0, 0, tiled=True)
-        part = expand(jnp.stack([column_first, start, z * per_z]), sensors, lists, width)
-        seen, part = lax.optimization_barrier((sensors, part))
+        return expand(jnp.stack([column_first, start, z * per_z]), sensors, lists, width)
+
+    def summed_of(part):
         part = lax.all_to_all(part.reshape(n_plane, piece, depth), PLANE, 0, 0, tiled=True)
         part = part.astype(F32).sum(axis=0).astype(BF16)
-        part = jnp.broadcast_to(part[None], (n_plane, piece, depth))
-        return seen, lax.all_to_all(part, PLANE, 0, 0, tiled=True).reshape(per_z, depth)
-
-    seen, readings = one_round(jnp.int32(0))
+        return jnp.broadcast_to(part[None], (n_plane, piece, depth))
+
+    def handed_out(part):
+        return lax.all_to_all(part, PLANE, 0, 0, tiled=True).reshape(per_z, depth)
+
+    part = part_of(jnp.int32(0))
+    go_on(part)
+    seen, part = lax.optimization_barrier((sensors, part))
+    part = summed_of(part)
+    go_on(part)
+    readings = handed_out(part)
     rounds = pl.cdiv(longest(seen, n_z, devices, width), SLOTS)
     _, readings = lax.while_loop(
         lambda state: state[0] < rounds,
-        lambda state: (state[0] + 1, state[1] + one_round(state[0])[1]),
+        lambda state: (state[0] + 1, state[1] + handed_out(summed_of(part_of(state[0])))),
         (jnp.int32(1), readings),
     )
 
-    own, other = jnp.stack([xl]), jnp.stack([1 - xl])
-    sent = correlate(other, readings, gathered, False)
-    arrived = lax.ppermute(sent, "xl", [(0, 1), (1, 0)])
-    whole = correlate(own, readings, gathered, True)
-    return place(other, arrived, whole)
+    here = jnp.stack([z, xl])
+
+    def swapped(sent):
+        return lax.ppermute(sent, "xl", [(0, 1), (1, 0)])
+
+    near = [(block,) for block in (pixels, up[1], down[1], up[2], down[2])]
+    late = [(up[3],), (down[3],)]
+    shifts = [0, -1, 1, -2, 2, -3, 3, 4]
+    sent = send(here, readings, near)
+    above, below, _ = lax.optimization_barrier((up[3], down[3], sent))
+    middle = depth // 2
+    far = [(ring(above[:middle], 1), ring(below[middle:], -1))]
+    pieces = [swapped(sent), swapped(send(here, readings, late)), swapped(send(here, readings, far))]
+    return place(here, pieces, shifts, keep(here, readings, near + late + far, shifts))
 
 
 def solution(mesh):

time: 132 us -> 121 us (0.917)
  starting transfers between devices: 19.1 us -> 63.4 us
  blocking collectives: 25.3 us -> 0 us
  waiting for transfers between devices: 54.6 us -> 34.7 us
  between operations: 14.2 us -> 1.13 us
  local copies, waits for them, and re-layouts: 1.05 us -> 3.78 us
    ppermute x1 -> x11, starting transfers between devices: 2.76 us -> 42.4 us  [the longest x8 34.2 us: ring(): lax.ppermute(value, 'z', [(i, (i + shift) % size) for i in range(size)])]
    all_to_all x1 -> x0, blocking collectives: 25.3 us -> none  [one_round(): lax.all_to_all(part.reshape(n_plane, piece, depth), PLANE, 0, 0, tiled=True)]
    all_gather x1 -> x0, waiting for transfers between devices: 13.1 us -> none  [body(): gathered = lax.all_gather(temps, 'z').reshape(n_z, depth, width)]
    ppermute x1 -> x11, waiting for transfers between devices: 20.1 us -> 14.1 us  [the longest x8 13.2 us: ring(): lax.ppermute(value, 'z', [(i, (i + shift) % size) for i in range(size)])]
    all_to_all x2 -> x3, starting transfers between devices: 16.3 us -> 21 us  [the longest x1 10.6 us: summed_of(): lax.all_to_all(part.reshape(n_plane, piece, depth), PLANE, 0, 0, tiled=True)]
    reshape x2, local copies, waits for them, and re-layouts: 0.19 us -> 1.71 us  [the longest x1 0.85 us: summed_of(): part.reshape(n_plane, piece, depth)]
    pallas_call x3 -> x5, Pallas kernels: 9.57 us -> 8.68 us  [the longest x3 3.98 us: send(): pl.pallas_call(functools.partial(send_kernel, 1.0 / math.sqrt(depth), [le...]
    all_to_all x2 -> x3, waiting for transfers between devices: 20.7 us -> 20.5 us  [the longest x1 10 us: part_of(): lists = lax.all_to_all(lists, 'z', 0, 0, tiled=True)]
  transfers between devices with their start and end apart: 4 -> 14, of which waited for: 4 -> 9; matrix products, arithmetic and copies ran while one was open for 1% -> 3% of each run, Pallas kernels for 9% -> 9%
where the time goes in v4:
time: 121 us; the launch traced here: 120 us
  starting transfers between devices  63.4 us (52%)
  waiting for transfers between devices  34.7 us (29%)
  Pallas kernels  16.7 us (14%)
  local copies, waits for them, and re-layouts  3.78 us (3%)
    ppermute x8, starting transfers between devices, ring(): lax.ppermute(value, 'z', [(i, (i + shift) % size) for i in range(size)])  34.2 us
    ppermute x8, waiting for transfers between devices, ring(): lax.ppermute(value, 'z', [(i, (i + shift) % size) for i in range(size)])  13.2 us
    all_to_all x1, starting transfers between devices, summed_of(): lax.all_to_all(part.reshape(n_plane, piece, depth), PLANE, 0, 0, tiled=True)  10.6 us
    all_to_all x1, waiting for transfers between devices, part_of(): lists = lax.all_to_all(lists, 'z', 0, 0, tiled=True)  10 us
    ppermute x3, starting transfers between devices, swapped(): return lax.ppermute(sent, 'xl', [(0, 1), (1, 0)])  8.28 us
    all_to_all x1, waiting for transfers between devices, summed_of(): lax.all_to_all(part.reshape(n_plane, piece, depth), PLANE, 0, 0, tiled=True)  7.63 us
    all_to_all x1, starting transfers between devices, handed_out(): return lax.all_to_all(part, PLANE, 0, 0, tiled=True).reshape(per_z, depth)  5.89 us
    all_to_all x1, starting transfers between devices, part_of(): lists = lax.all_to_all(lists, 'z', 0, 0, tiled=True)  4.47 us
  transfers between devices with their start and end apart: 14, of which 9 were waited for; matrix products, arithmetic and copies ran while one was open for 3% of the time, Pallas kernels for 9%

profile of v4, /device:TPU:6, one launch (start us, length us, event | category | flops | bytes accessed | tf_op | source)
XLA Modules:
  0.0 120.1 jit_solution(15615400473651945183)
XLA Ops:
  0.0 4.3 %collective-permute-start = (bf16[768,512]{1,0:T(8,128)(2,1)}, bf16[768,512]{1,0:T(8,128)(2,1)S(1)}, u32[]{:S(2)}, u32[]{:S(2)}) collective-permute-start(bf16[768,512]{1,0:T(8,128)(2,1)} %bitcast.19), channel_id=1, source_target_pairs={{0,2},{2,4},{4,6},{6,8},{8,10},{10,12},{12,14},{14,0},{1,3},{3,5},... | collective-permute-start | bytes 2359304 | tf_op jit(solution)/shard_map/ppermute | solution.py:276
  4.3 8.6 %collective-permute-start.1 = (bf16[768,512]{1,0:T(8,128)(2,1)}, bf16[768,512]{1,0:T(8,128)(2,1)S(1)}, u32[]{:S(2)}, u32[]{:S(2)}) collective-permute-start(bf16[768,512]{1,0:T(8,128)(2,1)} %bitcast.20), channel_id=1, source_target_pairs={{0,14},{2,0},{4,2},{6,4},{8,6},{10,8},{12,10},{14,12},{1,15},{3,1}... | collective-permute-start | bytes 2359304 | tf_op jit(solution)/shard_map/ppermute | solution.py:276
  13.0 3.6 %compact.5 = bf16[8,16,128]{2,1,0:T(8,128)(2,1)} custom-call(s32[2]{0:T(128)S(1)} %pad_add_fusion.4.scalar_ref, s32[12,2048]{1,0:T(8,128)} %sensors_ref.4, bf16[12,64,512]{2,1,0:T(8,128)(2,1)} %temps_ref.1), custom_call_target="tpu_custom_call" | custom-call | tf_op jit(solution)/shard_map/compact/pallas_call | solution.py:79
  16.6 4.5 %all-to-all-start.3 = ((bf16[8,16,128]{2,1,0:T(8,128)(2,1)}), bf16[8,16,128]{2,1,0:T(8,128)(2,1)S(1)}, u32[]{:S(2)}, u32[]{:S(2)}) async-start(bf16[8,16,128]{2,1,0:T(8,128)(2,1)} %compact.5), calls=%async_computation.3 | async-start | bytes 65536 | tf_op jit(solution)/shard_map/all_to_all | solution.py:301
  21.2 10.0 %all-to-all-done.3.lists_ref = bf16[8,16,128]{2,1,0:T(8,128)(2,1)S(1)} async-done(((bf16[8,16,128]{2,1,0:T(8,128)(2,1)}), bf16[8,16,128]{2,1,0:T(8,128)(2,1)S(1)}, u32[]{:S(2)}, u32[]{:S(2)}) %all-to-all-start.3) | async-done | bytes 32800 | tf_op jit(solution)/shard_map/all_to_all | solution.py:301
  31.2 2.2 %expand.5 = bf16[256,768]{1,0:T(8,128)(2,1)S(1)} custom-call(s32[3]{0:T(128)S(1)} %pad_add_fusion.3.scalar_ref, s32[12,2048]{1,0:T(8,128)} %sensors_ref.4, bf16[8,16,128]{2,1,0:T(8,128)(2,1)S(1)} %all-to-all-done.3.lists_ref), custom_call_target="tpu_custom_call" | custom-call | tf_op jit(solution)/shard_map/expand/pallas_call | solution.py:121
  34.2 10.6 %all-to-all-start.4 = ((bf16[64,4,768]{2,1,0:T(4,128)(2,1)}), bf16[64,4,768]{2,1,0:T(4,128)(2,1)S(1)}, u32[]{:S(2)}, u32[]{:S(2)}) async-start(bf16[64,4,768]{2,1,0:T(4,128)(2,1)} %reshape.25), calls=%async_computation.4 | async-start | bytes 786432 | tf_op jit(solution)/shard_map/all_to_all | solution.py:305
  44.9 5.2 %collective-permute-start.2 = (bf16[768,512]{1,0:T(8,128)(2,1)S(1)}, bf16[768,512]{1,0:T(8,128)(2,1)}, u32[]{:S(2)}, u32[]{:S(2)}) collective-permute-start(bf16[768,512]{1,0:T(8,128)(2,1)S(1)} %collective-permute-done.rest_1_), channel_id=1, source_target_pairs={{0,2},{2,4},{4,6},{6,8},{8,10},{10,12},{12,14},{14,0},{1,3},{3,5},... | collective-permute-start | bytes 2359304 | tf_op jit(solution)/shard_map/ppermute | solution.py:276
  50.0 1.9 %collective-permute-start.3 = (bf16[768,512]{1,0:T(8,128)(2,1)S(1)}, bf16[768,512]{1,0:T(8,128)(2,1)}, u32[]{:S(2)}, u32[]{:S(2)}) collective-permute-start(bf16[768,512]{1,0:T(8,128)(2,1)S(1)} %collective-permute-done.1.rest_2_), channel_id=1, source_target_pairs={{0,14},{2,0},{4,2},{6,4},{8,6},{10,8},{12,10},{14,12},{1,15},{3,1}... | collective-permute-start | bytes 2359304 | tf_op jit(solution)/shard_map/ppermute | solution.py:276
  52.0 7.6 %all-to-all-done.4 = bf16[64,4,768]{2,1,0:T(4,128)(2,1)S(1)} async-done(((bf16[64,4,768]{2,1,0:T(4,128)(2,1)}), bf16[64,4,768]{2,1,0:T(4,128)(2,1)S(1)}, u32[]{:S(2)}, u32[]{:S(2)}) %all-to-all-start.4) | async-done | bytes 393248 | tf_op jit(solution)/shard_map/all_to_all | solution.py:305
  59.8 0.9 broadcast_in_dim.7
  60.7 5.9 %all-to-all-start.5 = ((bf16[64,4,768]{2,1,0:T(4,128)(2,1)}), bf16[64,4,768]{2,1,0:T(4,128)(2,1)S(1)}, u32[]{:S(2)}, u32[]{:S(2)}) async-start(bf16[64,4,768]{2,1,0:T(4,128)(2,1)} %broadcast_in_dim.7), calls=%async_computation.5 | async-start | bytes 786432 | tf_op jit(solution)/shard_map/all_to_all | solution.py:310
  66.6 2.2 %longest.1 = s32[1,1]{1,0:T(1,128)} custom-call(s32[12,2048]{1,0:T(8,128)} %sensors_ref.4), custom_call_target="tpu_custom_call" | custom-call | flops 25165824 | bytes 98304 | tf_op jit(solution)/shard_map/longest/pallas_call | solution.py:148
  69.5 1.8 %collective-permute-done.3.rest_4_ = bf16[768,512]{1,0:T(8,128)(2,1)} collective-permute-done((bf16[768,512]{1,0:T(8,128)(2,1)S(1)}, bf16[768,512]{1,0:T(8,128)(2,1)}, u32[]{:S(2)}, u32[]{:S(2)}) %collective-permute-start.3) | collective-permute-done | bytes 786464 | tf_op jit(solution)/shard_map/ppermute | solution.py:276
  71.3 3.4 %collective-permute-start.5 = (bf16[768,512]{1,0:T(8,128)(2,1)}, bf16[768,512]{1,0:T(8,128)(2,1)S(1)}, u32[]{:S(2)}, u32[]{:S(2)}) collective-permute-start(bf16[768,512]{1,0:T(8,128)(2,1)} %collective-permute-done.2.rest_3_), channel_id=1, source_target_pairs={{0,2},{2,4},{4,6},{6,8},{8,10},{10,12},{12,14},{14,0},{1,3},{3,5},... | collective-permute-start | bytes 2359304 | tf_op jit(solution)/shard_map/ppermute | solution.py:276
  74.7 3.7 %collective-permute-start.6 = (bf16[768,512]{1,0:T(8,128)(2,1)}, bf16[768,512]{1,0:T(8,128)(2,1)S(1)}, u32[]{:S(2)}, u32[]{:S(2)}) collective-permute-start(bf16[768,512]{1,0:T(8,128)(2,1)} %collective-permute-done.3.rest_4_), channel_id=1, source_target_pairs={{0,14},{2,0},{4,2},{6,4},{8,6},{10,8},{12,10},{14,12},{1,15},{3,1}... | collective-permute-start | bytes 2359304 | tf_op jit(solution)/shard_map/ppermute | solution.py:276
  78.4 2.9 %all-to-all-done.5 = bf16[64,4,768]{2,1,0:T(4,128)(2,1)S(1)} async-done(((bf16[64,4,768]{2,1,0:T(4,128)(2,1)}), bf16[64,4,768]{2,1,0:T(4,128)(2,1)S(1)}, u32[]{:S(2)}, u32[]{:S(2)}) %all-to-all-start.5) | async-done | bytes 393248 | tf_op jit(solution)/shard_map/all_to_all | solution.py:310
  82.2 1.1 copy-done.1
  83.3 2.2 %send.3 = bf16[5,128,512]{2,1,0:T(8,128)(2,1)S(1)} custom-call(s32[2]{0:T(128)S(1)} %pad_add_fusion.2.scalar_ref, bf16[256,768]{1,0:T(8,128)(2,1)} %get-tuple-element.244, bf16[768,512]{1,0:T(8,128)(2,1)S(1)} %bitcast.21, bf16[768,512]{1,0:T(8,128)(2,1)S(1)} %collective-permute-done.rest_1_, bf16[768,512]{1,0:T(8,128)(2,1)S(1)} %copy-done.1, ...), custom_call_target="tpu_custom_call" | custom-call | flops 503316480 | bytes 3932160 | tf_op jit(solution)/shard_map/send/pallas_call | solution.py:232
  85.5 2.8 %collective-permute-start.4 = (bf16[5,128,512]{2,1,0:T(8,128)(2,1)S(1)}, bf16[5,128,512]{2,1,0:T(8,128)(2,1)S(1)}, u32[]{:S(2)}, u32[]{:S(2)}) collective-permute-start(bf16[5,128,512]{2,1,0:T(8,128)(2,1)S(1)} %send.3), channel_id=1, source_target_pairs={{0,1},{1,0},{2,3},{3,2},{4,5},{5,4},{6,7},{7,6},{8,9},{9,8},{10,11... | collective-permute-start | bytes 1966088 | tf_op jit(solution)/shard_map/ppermute | solution.py:328
  88.3 4.8 %collective-permute-done.5.rest_0_.rest_5_ = bf16[768,512]{1,0:T(8,128)(2,1)S(1)} collective-permute-done((bf16[768,512]{1,0:T(8,128)(2,1)}, bf16[768,512]{1,0:T(8,128)(2,1)S(1)}, u32[]{:S(2)}, u32[]{:S(2)}) %collective-permute-start.5) | collective-permute-done | bytes 786464 | tf_op jit(solution)/shard_map/ppermute | solution.py:276
  93.1 3.0 %collective-permute-done.6.rest_1_.rest_6_ = bf16[768,512]{1,0:T(8,128)(2,1)S(1)} collective-permute-done((bf16[768,512]{1,0:T(8,128)(2,1)}, bf16[768,512]{1,0:T(8,128)(2,1)S(1)}, u32[]{:S(2)}, u32[]{:S(2)}) %collective-permute-start.6) | collective-permute-done | bytes 786464 | tf_op jit(solution)/shard_map/ppermute | solution.py:276
  96.2 3.0 %collective-permute-start.8 = (bf16[384,512]{1,0:T(8,128)(2,1)S(1)}, bf16[384,512]{1,0:T(8,128)(2,1)S(1)}, u32[]{:S(2)}, u32[]{:S(2)}) collective-permute-start(bf16[384,512]{1,0:T(8,128)(2,1)S(1)} %slice.6), channel_id=1, source_target_pairs={{0,2},{2,4},{4,6},{6,8},{8,10},{10,12},{12,14},{14,0},{1,3},{3,5},... | collective-permute-start | bytes 1179656 | tf_op jit(solution)/shard_map/ppermute | solution.py:276
  99.2 4.2 %collective-permute-start.9 = (bf16[384,512]{1,0:T(8,128)(2,1)S(1)}, bf16[384,512]{1,0:T(8,128)(2,1)S(1)}, u32[]{:S(2)}, u32[]{:S(2)}) collective-permute-start(bf16[384,512]{1,0:T(8,128)(2,1)S(1)} %slice.7), channel_id=1, source_target_pairs={{0,14},{2,0},{4,2},{6,4},{8,6},{10,8},{12,10},{14,12},{1,15},{3,1}... | collective-permute-start | bytes 1179656 | tf_op jit(solution)/shard_map/ppermute | solution.py:276
  103.4 0.9 send.4
  104.3 2.8 %collective-permute-start.7 = (bf16[2,128,512]{2,1,0:T(8,128)(2,1)S(1)}, bf16[2,128,512]{2,1,0:T(8,128)(2,1)S(1)}, u32[]{:S(2)}, u32[]{:S(2)}) collective-permute-start(bf16[2,128,512]{2,1,0:T(8,128)(2,1)S(1)} %send.4), channel_id=1, source_target_pairs={{0,1},{1,0},{2,3},{3,2},{4,5},{5,4},{6,7},{7,6},{8,9},{9,8},{10,11... | collective-permute-start | bytes 786440 | tf_op jit(solution)/shard_map/ppermute | solution.py:328
  107.1 2.3 %collective-permute-done.8.rest_0_.rest_7_ = bf16[384,512]{1,0:T(8,128)(2,1)S(1)} collective-permute-done((bf16[384,512]{1,0:T(8,128)(2,1)S(1)}, bf16[384,512]{1,0:T(8,128)(2,1)S(1)}, u32[]{:S(2)}, u32[]{:S(2)}) %collective-permute-start.8) | collective-permute-done | bytes 393248 | tf_op jit(solution)/shard_map/ppermute | solution.py:276
  109.4 1.2 %collective-permute-done.9.rest_1_.rest_8_ = bf16[384,512]{1,0:T(8,128)(2,1)S(1)} collective-permute-done((bf16[384,512]{1,0:T(8,128)(2,1)S(1)}, bf16[384,512]{1,0:T(8,128)(2,1)S(1)}, u32[]{:S(2)}, u32[]{:S(2)}) %collective-permute-start.9) | collective-permute-done | bytes 393248 | tf_op jit(solution)/shard_map/ppermute | solution.py:276
  111.5 2.8 %collective-permute-start.10 = (bf16[1,128,512]{2,1,0:T(8,128)(2,1)S(1)}, bf16[1,128,512]{2,1,0:T(8,128)(2,1)S(1)}, u32[]{:S(2)}, u32[]{:S(2)}) collective-permute-start(bf16[1,128,512]{2,1,0:T(8,128)(2,1)S(1)} %send.5), channel_id=1, source_target_pairs={{0,1},{1,0},{2,3},{3,2},{4,5},{5,4},{6,7},{7,6},{8,9},{9,8},{10,11... | collective-permute-start | bytes 393224 | tf_op jit(solution)/shard_map/ppermute | solution.py:328
  114.3 3.1 %keep.1.rest_3_ = bf16[128,8192]{1,0:T(8,128)(2,1)} custom-call(s32[2]{0:T(128)S(1)} %pad_add_fusion.2.scalar_ref, bf16[256,768]{1,0:T(8,128)(2,1)S(1)} %copy-done.5, bf16[768,512]{1,0:T(8,128)(2,1)S(1)} %bitcast.22, bf16[768,512]{1,0:T(8,128)(2,1)S(1)} %collective-permute-done.rest_1_, bf16[768,512]{1,0:T(8,128)(2,1)S(1)} %copy-done.2, ...), custom_call_target="tpu_custom_call" | custom-call | flops 805306368 | bytes 6291456 | tf_op jit(solution)/shard_map/keep/pallas_call | solution.py:247
  117.4 0.9 collective-permute-done.10.rest_2_
  118.4 1.6 %place.1 = bf16[128,8192]{1,0:T(8,128)(2,1)} custom-call(s32[2]{0:T(128)S(1)} %pad_add_fusion.2.scalar_ref, bf16[5,128,512]{2,1,0:T(8,128)(2,1)S(1)} %collective-permute-done.4.rest_0_, bf16[2,128,512]{2,1,0:T(8,128)(2,1)S(1)} %collective-permute-done.7.rest_1_, ...), custom_call_target="tpu_custom_call", output_to_operand_aliasing={{}: (4, {})} | custom-call | tf_op jit(solution)/shard_map/place/pallas_call | solution.py:262
  (24 shorter events, 3.1 us)
Async XLA Ops:
  0.0 44.8 %collective-permute-start = (bf16[768,512]{1,0:T(8,128)(2,1)}, bf16[768,512]{1,0:T(8,128)(2,1)S(1)}, u32[]{:S(2)}, u32[]{:S(2)}) collective-permute-start(bf16[768,512]{1,0:T(8,128)(2,1)} %bitcast.19), channel_id=1, source_target_pairs={{0,2},{2,4},{4,6},{6,8},{8,10},{10,12},{12,14},{14,0},{1,3},{3,5},... | collective-permute-start | bytes 2359304 | tf_op jit(solution)/shard_map/ppermute | solution.py:276
  4.3 40.6 %collective-permute-start.1 = (bf16[768,512]{1,0:T(8,128)(2,1)}, bf16[768,512]{1,0:T(8,128)(2,1)S(1)}, u32[]{:S(2)}, u32[]{:S(2)}) collective-permute-start(bf16[768,512]{1,0:T(8,128)(2,1)} %bitcast.20), channel_id=1, source_target_pairs={{0,14},{2,0},{4,2},{6,4},{8,6},{10,8},{12,10},{14,12},{1,15},{3,1}... | collective-permute-start | bytes 2359304 | tf_op jit(solution)/shard_map/ppermute | solution.py:276
  16.6 14.5 %all-to-all-start.3 = ((bf16[8,16,128]{2,1,0:T(8,128)(2,1)}), bf16[8,16,128]{2,1,0:T(8,128)(2,1)S(1)}, u32[]{:S(2)}, u32[]{:S(2)}) async-start(bf16[8,16,128]{2,1,0:T(8,128)(2,1)} %compact.5), calls=%async_computation.3 | async-start | bytes 65536 | tf_op jit(solution)/shard_map/all_to_all | solution.py:301
  33.4 48.8 %copy-start.3 = (bf16[12,64,512]{2,1,0:T(8,128)(2,1)S(1)}, bf16[12,64,512]{2,1,0:T(8,128)(2,1)}, u32[]{:S(2)}) copy-start(bf16[12,64,512]{2,1,0:T(8,128)(2,1)} %temps_ref.1) | copy-start | bytes 2359300
  34.2 25.4 %all-to-all-start.4 = ((bf16[64,4,768]{2,1,0:T(4,128)(2,1)}), bf16[64,4,768]{2,1,0:T(4,128)(2,1)S(1)}, u32[]{:S(2)}, u32[]{:S(2)}) async-start(bf16[64,4,768]{2,1,0:T(4,128)(2,1)} %reshape.25), calls=%async_computation.4 | async-start | bytes 786432 | tf_op jit(solution)/shard_map/all_to_all | solution.py:305
  44.9 24.7 %copy-start = (bf16[768,512]{1,0:T(8,128)(2,1)}, bf16[768,512]{1,0:T(8,128)(2,1)S(1)}, u32[]{:S(2)}) copy-start(bf16[768,512]{1,0:T(8,128)(2,1)S(1)} %collective-permute-done.1.rest_2_) | copy-start | bytes 2359300
  44.9 24.7 %collective-permute-start.2 = (bf16[768,512]{1,0:T(8,128)(2,1)S(1)}, bf16[768,512]{1,0:T(8,128)(2,1)}, u32[]{:S(2)}, u32[]{:S(2)}) collective-permute-start(bf16[768,512]{1,0:T(8,128)(2,1)S(1)} %collective-permute-done.rest_1_), channel_id=1, source_target_pairs={{0,2},{2,4},{4,6},{6,8},{8,10},{10,12},{12,14},{14,0},{1,3},{3,5},... | collective-permute-start | bytes 2359304 | tf_op jit(solution)/shard_map/ppermute | solution.py:276
  50.0 21.3 %collective-permute-start.3 = (bf16[768,512]{1,0:T(8,128)(2,1)S(1)}, bf16[768,512]{1,0:T(8,128)(2,1)}, u32[]{:S(2)}, u32[]{:S(2)}) collective-permute-start(bf16[768,512]{1,0:T(8,128)(2,1)S(1)} %collective-permute-done.1.rest_2_), channel_id=1, source_target_pairs={{0,14},{2,0},{4,2},{6,4},{8,6},{10,8},{12,10},{14,12},{1,15},{3,1}... | collective-permute-start | bytes 2359304 | tf_op jit(solution)/shard_map/ppermute | solution.py:276
  60.7 20.7 %all-to-all-start.5 = ((bf16[64,4,768]{2,1,0:T(4,128)(2,1)}), bf16[64,4,768]{2,1,0:T(4,128)(2,1)S(1)}, u32[]{:S(2)}, u32[]{:S(2)}) async-start(bf16[64,4,768]{2,1,0:T(4,128)(2,1)} %broadcast_in_dim.7), calls=%async_computation.5 | async-start | bytes 786432 | tf_op jit(solution)/shard_map/all_to_all | solution.py:310
  71.3 21.8 %collective-permute-start.5 = (bf16[768,512]{1,0:T(8,128)(2,1)}, bf16[768,512]{1,0:T(8,128)(2,1)S(1)}, u32[]{:S(2)}, u32[]{:S(2)}) collective-permute-start(bf16[768,512]{1,0:T(8,128)(2,1)} %collective-permute-done.2.rest_3_), channel_id=1, source_target_pairs={{0,2},{2,4},{4,6},{6,8},{8,10},{10,12},{12,14},{14,0},{1,3},{3,5},... | collective-permute-start | bytes 2359304 | tf_op jit(solution)/shard_map/ppermute | solution.py:276
  74.7 21.4 %collective-permute-start.6 = (bf16[768,512]{1,0:T(8,128)(2,1)}, bf16[768,512]{1,0:T(8,128)(2,1)S(1)}, u32[]{:S(2)}, u32[]{:S(2)}) collective-permute-start(bf16[768,512]{1,0:T(8,128)(2,1)} %collective-permute-done.3.rest_4_), channel_id=1, source_target_pairs={{0,14},{2,0},{4,2},{6,4},{8,6},{10,8},{12,10},{14,12},{1,15},{3,1}... | collective-permute-start | bytes 2359304 | tf_op jit(solution)/shard_map/ppermute | solution.py:276
  82.2 1.1 copy-start.1
  83.3 20.1 %copy-start.5 = (bf16[256,768]{1,0:T(8,128)(2,1)S(1)}, bf16[256,768]{1,0:T(8,128)(2,1)}, u32[]{:S(2)}) copy-start(bf16[256,768]{1,0:T(8,128)(2,1)} %get-tuple-element.244) | copy-start | bytes 1179652
  85.5 31.9 %collective-permute-start.4 = (bf16[5,128,512]{2,1,0:T(8,128)(2,1)S(1)}, bf16[5,128,512]{2,1,0:T(8,128)(2,1)S(1)}, u32[]{:S(2)}, u32[]{:S(2)}) collective-permute-start(bf16[5,128,512]{2,1,0:T(8,128)(2,1)S(1)} %send.3), channel_id=1, source_target_pairs={{0,1},{1,0},{2,3},{3,2},{4,5},{5,4},{6,7},{7,6},{8,9},{9,8},{10,11... | collective-permute-start | bytes 1966088 | tf_op jit(solution)/shard_map/ppermute | solution.py:328
  96.2 18.1 %copy-start.2 = (bf16[768,512]{1,0:T(8,128)(2,1)S(1)}, bf16[768,512]{1,0:T(8,128)(2,1)}, u32[]{:S(2)}) copy-start(bf16[768,512]{1,0:T(8,128)(2,1)} %copy-done) | copy-start | bytes 2359300
  96.2 13.3 %collective-permute-start.8 = (bf16[384,512]{1,0:T(8,128)(2,1)S(1)}, bf16[384,512]{1,0:T(8,128)(2,1)S(1)}, u32[]{:S(2)}, u32[]{:S(2)}) collective-permute-start(bf16[384,512]{1,0:T(8,128)(2,1)S(1)} %slice.6), channel_id=1, source_target_pairs={{0,2},{2,4},{4,6},{6,8},{8,10},{10,12},{12,14},{14,0},{1,3},{3,5},... | collective-permute-start | bytes 1179656 | tf_op jit(solution)/shard_map/ppermute | solution.py:276
  99.2 11.5 %collective-permute-start.9 = (bf16[384,512]{1,0:T(8,128)(2,1)S(1)}, bf16[384,512]{1,0:T(8,128)(2,1)S(1)}, u32[]{:S(2)}, u32[]{:S(2)}) collective-permute-start(bf16[384,512]{1,0:T(8,128)(2,1)S(1)} %slice.7), channel_id=1, source_target_pairs={{0,14},{2,0},{4,2},{6,4},{8,6},{10,8},{12,10},{14,12},{1,15},{3,1}... | collective-permute-start | bytes 1179656 | tf_op jit(solution)/shard_map/ppermute | solution.py:276
  104.3 13.1 %collective-permute-start.7 = (bf16[2,128,512]{2,1,0:T(8,128)(2,1)S(1)}, bf16[2,128,512]{2,1,0:T(8,128)(2,1)S(1)}, u32[]{:S(2)}, u32[]{:S(2)}) collective-permute-start(bf16[2,128,512]{2,1,0:T(8,128)(2,1)S(1)} %send.4), channel_id=1, source_target_pairs={{0,1},{1,0},{2,3},{3,2},{4,5},{5,4},{6,7},{7,6},{8,9},{9,8},{10,11... | collective-permute-start | bytes 786440 | tf_op jit(solution)/shard_map/ppermute | solution.py:328
  111.5 6.9 %collective-permute-start.10 = (bf16[1,128,512]{2,1,0:T(8,128)(2,1)S(1)}, bf16[1,128,512]{2,1,0:T(8,128)(2,1)S(1)}, u32[]{:S(2)}, u32[]{:S(2)}) collective-permute-start(bf16[1,128,512]{2,1,0:T(8,128)(2,1)S(1)} %send.5), channel_id=1, source_target_pairs={{0,1},{1,0},{2,3},{3,2},{4,5},{5,4},{6,7},{7,6},{8,9},{9,8},{10,11... | collective-permute-start | bytes 393224 | tf_op jit(solution)/shard_map/ppermute | solution.py:328

commit v5 on v4

--- a/solution.py
+++ b/solution.py
@@ -285,21 +285,24 @@
     z, xl = lax.axis_index("z"), lax.axis_index("xl")
 
     pixels = temps.reshape(depth, width)
-    up, down = [pixels, ring(pixels, 1)], [pixels, ring(pixels, -1)]
-
-    def go_on(ready):
-        above, below, _ = lax.optimization_barrier((up[-1], down[-1], ready))
-        up.append(ring(above, 1))
-        down.append(ring(below, -1))
+    up, down = [pixels, ring(pixels, 1)], [pixels]
+
+    def go_on(blocks, shift, ready):
+        block, _ = lax.optimization_barrier((blocks[-1], ready))
+        blocks.append(ring(block, shift))
 
     first = lax.axis_index(AXES) * width
     column_first = first - z * lax.axis_size("xl") * width
 
-    def part_of(number):
-        start = number * SLOTS
-        lists = compact(jnp.stack([first, start]), sensors, temps, n_z)
-        lists = lax.all_to_all(lists, "z", 0, 0, tiled=True)
-        return expand(jnp.stack([column_first, start, z * per_z]), sensors, lists, width)
+    def listed(number):
+        return compact(jnp.stack([first, number * SLOTS]), sensors, temps, n_z)
+
+    def exchanged(lists):
+        return lax.all_to_all(lists, "z", 0, 0, tiled=True)
+
+    def part_of(number, lists):
+        scalars = jnp.stack([column_first, number * SLOTS, z * per_z])
+        return expand(scalars, sensors, lists, width)
 
     def summed_of(part):
         part = lax.all_to_all(part.reshape(n_plane, piece, depth), PLANE, 0, 0, tiled=True)
@@ -309,16 +312,25 @@
     def handed_out(part):
         return lax.all_to_all(part, PLANE, 0, 0, tiled=True).reshape(per_z, depth)
 
-    part = part_of(jnp.int32(0))
-    go_on(part)
+    def one_round(number):
+        return handed_out(summed_of(part_of(number, exchanged(listed(number)))))
+
+    lists = listed(jnp.int32(0))
+    go_on(down, -1, lists)
+    lists = exchanged(lists)
+    go_on(up, 1, lists)
+    part = part_of(jnp.int32(0), lists)
+    go_on(down, -1, part)
+    go_on(up, 1, part)
     seen, part = lax.optimization_barrier((sensors, part))
     part = summed_of(part)
-    go_on(part)
+    go_on(down, -1, part)
+    go_on(up, 1, part)
     readings = handed_out(part)
     rounds = pl.cdiv(longest(seen, n_z, devices, width), SLOTS)
     _, readings = lax.while_loop(
         lambda state: state[0] < rounds,
-        lambda state: (state[0] + 1, state[1] + handed_out(summed_of(part_of(state[0])))),
+        lambda state: (state[0] + 1, state[1] + one_round(state[0])),
         (jnp.int32(1), readings),
     )
 
@@ -327,15 +339,10 @@
     def swapped(sent):
         return lax.ppermute(sent, "xl", [(0, 1), (1, 0)])
 
-    near = [(block,) for block in (pixels, up[1], down[1], up[2], down[2])]
-    late = [(up[3],), (down[3],)]
+    blocks = [(block,) for block in (*up[:2], down[1], up[2], down[2], up[3], down[3], up[4])]
     shifts = [0, -1, 1, -2, 2, -3, 3, 4]
-    sent = send(here, readings, near)
-    above, below, _ = lax.optimization_barrier((up[3], down[3], sent))
-    middle = depth // 2
-    far = [(ring(above[:middle], 1), ring(below[middle:], -1))]
-    pieces = [swapped(sent), swapped(send(here, readings, late)), swapped(send(here, readings, far))]
-    return place(here, pieces, shifts, keep(here, readings, near + late + far, shifts))
+    pieces = [swapped(send(here, readings, blocks[low:high])) for low, high in ((0, 6), (6, 8))]
+    return place(here, pieces, shifts, keep(here, readings, blocks, shifts))
 
 
 def solution(mesh):

time: 121 us -> 122 us (level)
  the two profiles are of different devices: /device:TPU:6 before, /device:TPU:8 now
where the time goes in v5:
time: 122 us; the launch traced here: 121 us
  starting transfers between devices  59.1 us (48%)
  waiting for transfers between devices  40.6 us (33%)
  Pallas kernels  17.2 us (14%)
  local copies, waits for them, and re-layouts  2.55 us (2%)
    ppermute x7, starting transfers between devices, ring(): lax.ppermute(value, 'z', [(i, (i + shift) % size) for i in range(size)])  25.9 us
    ppermute x7, waiting for transfers between devices, ring(): lax.ppermute(value, 'z', [(i, (i + shift) % size) for i in range(size)])  14 us
    all_to_all x1, starting transfers between devices, summed_of(): lax.all_to_all(part.reshape(n_plane, piece, depth), PLANE, 0, 0, tiled=True)  10.7 us
    all_to_all x1, starting transfers between devices, exchanged(): return lax.all_to_all(lists, 'z', 0, 0, tiled=True)  9.41 us
    all_to_all x1, waiting for transfers between devices, summed_of(): lax.all_to_all(part.reshape(n_plane, piece, depth), PLANE, 0, 0, tiled=True)  8.15 us
    all_to_all x1, waiting for transfers between devices, exchanged(): return lax.all_to_all(lists, 'z', 0, 0, tiled=True)  7.91 us
    all_to_all x1, waiting for transfers between devices, handed_out(): return lax.all_to_all(part, PLANE, 0, 0, tiled=True).reshape(per_z, depth)  7.36 us
    all_to_all x1, starting transfers between devices, handed_out(): return lax.all_to_all(part, PLANE, 0, 0, tiled=True).reshape(per_z, depth)  6.55 us
  transfers between devices with their start and end apart: 12, of which 7 were waited for; matrix products, arithmetic and copies ran while one was open for 2% of the time, Pallas kernels for 10%

profile of v5, /device:TPU:8, one launch (start us, length us, event | category | flops | bytes accessed | tf_op | source)
XLA Modules:
  0.0 121.0 jit_solution(12597502115858229421)
XLA Ops:
  0.0 4.3 %collective-permute-start = (bf16[768,512]{1,0:T(8,128)(2,1)}, bf16[768,512]{1,0:T(8,128)(2,1)S(1)}, u32[]{:S(2)}, u32[]{:S(2)}) collective-permute-start(bf16[768,512]{1,0:T(8,128)(2,1)} %bitcast.19), channel_id=1, source_target_pairs={{0,2},{2,4},{4,6},{6,8},{8,10},{10,12},{12,14},{14,0},{1,3},{3,5},... | collective-permute-start | bytes 2359304 | tf_op jit(solution)/shard_map/ppermute | solution.py:276
  4.4 3.6 %compact.5 = bf16[8,16,128]{2,1,0:T(8,128)(2,1)} custom-call(s32[2]{0:T(128)S(1)} %pad_add_fusion.4.scalar_ref, s32[12,2048]{1,0:T(8,128)} %sensors_ref.4, bf16[12,64,512]{2,1,0:T(8,128)(2,1)} %temps_ref.1), custom_call_target="tpu_custom_call" | custom-call | tf_op jit(solution)/shard_map/compact/pallas_call | solution.py:79
  8.0 9.4 %all-to-all-start.3 = ((bf16[8,16,128]{2,1,0:T(8,128)(2,1)}), bf16[8,16,128]{2,1,0:T(8,128)(2,1)S(1)}, u32[]{:S(2)}, u32[]{:S(2)}) async-start(bf16[8,16,128]{2,1,0:T(8,128)(2,1)} %compact.5), calls=%async_computation.3 | async-start | bytes 65536 | tf_op jit(solution)/shard_map/all_to_all | solution.py:301
  17.4 5.1 %collective-permute-start.1 = (bf16[768,512]{1,0:T(8,128)(2,1)}, bf16[768,512]{1,0:T(8,128)(2,1)S(1)}, u32[]{:S(2)}, u32[]{:S(2)}) collective-permute-start(bf16[768,512]{1,0:T(8,128)(2,1)} %bitcast.20), channel_id=1, source_target_pairs={{0,14},{2,0},{4,2},{6,4},{8,6},{10,8},{12,10},{14,12},{1,15},{3,1}... | collective-permute-start | bytes 2359304 | tf_op jit(solution)/shard_map/ppermute | solution.py:276
  22.6 7.9 %all-to-all-done.3.lists_ref = bf16[8,16,128]{2,1,0:T(8,128)(2,1)S(1)} async-done(((bf16[8,16,128]{2,1,0:T(8,128)(2,1)}), bf16[8,16,128]{2,1,0:T(8,128)(2,1)S(1)}, u32[]{:S(2)}, u32[]{:S(2)}) %all-to-all-start.3) | async-done | bytes 32800 | tf_op jit(solution)/shard_map/all_to_all | solution.py:301
  30.5 3.1 %collective-permute-start.2 = (bf16[768,512]{1,0:T(8,128)(2,1)S(1)}, bf16[768,512]{1,0:T(8,128)(2,1)S(1)}, u32[]{:S(2)}, u32[]{:S(2)}) collective-permute-start(bf16[768,512]{1,0:T(8,128)(2,1)S(1)} %collective-permute-done.rest_1_), channel_id=1, source_target_pairs={{0,2},{2,4},{4,6},{6,8},{8,10},{10,12},{12,14},{14,0},{1,3},{3,5},... | collective-permute-start | bytes 2359304 | tf_op jit(solution)/shard_map/ppermute | solution.py:276
  33.6 0.1 pad_add_fusion.3.scalar_ref
  33.7 2.2 %expand.5 = bf16[256,768]{1,0:T(8,128)(2,1)S(1)} custom-call(s32[3]{0:T(128)S(1)} %pad_add_fusion.3.scalar_ref, s32[12,2048]{1,0:T(8,128)} %sensors_ref.4, bf16[8,16,128]{2,1,0:T(8,128)(2,1)S(1)} %all-to-all-done.3.lists_ref), custom_call_target="tpu_custom_call" | custom-call | tf_op jit(solution)/shard_map/expand/pallas_call | solution.py:121
  35.9 0.8 reshape.25
  36.8 10.7 %all-to-all-start.4 = ((bf16[64,4,768]{2,1,0:T(4,128)(2,1)}), bf16[64,4,768]{2,1,0:T(4,128)(2,1)S(1)}, u32[]{:S(2)}, u32[]{:S(2)}) async-start(bf16[64,4,768]{2,1,0:T(4,128)(2,1)} %reshape.25), calls=%async_computation.4 | async-start | bytes 786432 | tf_op jit(solution)/shard_map/all_to_all | solution.py:308
  47.5 3.9 %collective-permute-start.3 = (bf16[768,512]{1,0:T(8,128)(2,1)S(1)}, bf16[768,512]{1,0:T(8,128)(2,1)}, u32[]{:S(2)}, u32[]{:S(2)}) collective-permute-start(bf16[768,512]{1,0:T(8,128)(2,1)S(1)} %collective-permute-done.1.rest_2_), channel_id=1, source_target_pairs={{0,14},{2,0},{4,2},{6,4},{8,6},{10,8},{12,10},{14,12},{1,15},{3,1}... | collective-permute-start | bytes 2359304 | tf_op jit(solution)/shard_map/ppermute | solution.py:276
  51.4 0.1 collective-permute-done.2.rest_3_
  51.5 1.9 %collective-permute-start.4 = (bf16[768,512]{1,0:T(8,128)(2,1)S(1)}, bf16[768,512]{1,0:T(8,128)(2,1)}, u32[]{:S(2)}, u32[]{:S(2)}) collective-permute-start(bf16[768,512]{1,0:T(8,128)(2,1)S(1)} %collective-permute-done.2.rest_3_), channel_id=1, source_target_pairs={{0,2},{2,4},{4,6},{6,8},{8,10},{10,12},{12,14},{14,0},{1,3},{3,5},... | collective-permute-start | bytes 2359304 | tf_op jit(solution)/shard_map/ppermute | solution.py:276
  53.4 8.2 %all-to-all-done.4 = bf16[64,4,768]{2,1,0:T(4,128)(2,1)S(1)} async-done(((bf16[64,4,768]{2,1,0:T(4,128)(2,1)}), bf16[64,4,768]{2,1,0:T(4,128)(2,1)S(1)}, u32[]{:S(2)}, u32[]{:S(2)}) %all-to-all-start.4) | async-done | bytes 393248 | tf_op jit(solution)/shard_map/all_to_all | solution.py:308
  61.6 0.2 reduce_sum.24
  61.8 0.9 broadcast_in_dim.7
  62.6 6.6 %all-to-all-start.5 = ((bf16[64,4,768]{2,1,0:T(4,128)(2,1)}), bf16[64,4,768]{2,1,0:T(4,128)(2,1)S(1)}, u32[]{:S(2)}, u32[]{:S(2)}) async-start(bf16[64,4,768]{2,1,0:T(4,128)(2,1)} %broadcast_in_dim.7), calls=%async_computation.5 | async-start | bytes 786432 | tf_op jit(solution)/shard_map/all_to_all | solution.py:313
  69.3 2.2 %longest.1 = s32[1,1]{1,0:T(1,128)} custom-call(s32[12,2048]{1,0:T(8,128)} %sensors_ref.4), custom_call_target="tpu_custom_call" | custom-call | flops 25165824 | bytes 98304 | tf_op jit(solution)/shard_map/longest/pallas_call | solution.py:148
  72.0 3.9 %collective-permute-start.6 = (bf16[768,512]{1,0:T(8,128)(2,1)}, bf16[768,512]{1,0:T(8,128)(2,1)}, u32[]{:S(2)}, u32[]{:S(2)}) collective-permute-start(bf16[768,512]{1,0:T(8,128)(2,1)} %collective-permute-done.3.rest_4_), channel_id=1, source_target_pairs={{0,14},{2,0},{4,2},{6,4},{8,6},{10,8},{12,10},{14,12},{1,15},{3,1}... | collective-permute-start | bytes 2359304 | tf_op jit(solution)/shard_map/ppermute | solution.py:276
  75.9 7.4 %all-to-all-done.5 = bf16[64,4,768]{2,1,0:T(4,128)(2,1)S(1)} async-done(((bf16[64,4,768]{2,1,0:T(4,128)(2,1)}), bf16[64,4,768]{2,1,0:T(4,128)(2,1)S(1)}, u32[]{:S(2)}, u32[]{:S(2)}) %all-to-all-start.5) | async-done | bytes 393248 | tf_op jit(solution)/shard_map/all_to_all | solution.py:313
  83.3 0.8 reshape.26
  84.1 3.7 %collective-permute-start.7 = (bf16[768,512]{1,0:T(8,128)(2,1)}, bf16[768,512]{1,0:T(8,128)(2,1)}, u32[]{:S(2)}, u32[]{:S(2)}) collective-permute-start(bf16[768,512]{1,0:T(8,128)(2,1)} %collective-permute-done.4.rest_5_), channel_id=1, source_target_pairs={{0,2},{2,4},{4,6},{6,8},{8,10},{10,12},{12,14},{14,0},{1,3},{3,5},... | collective-permute-start | bytes 2359304 | tf_op jit(solution)/shard_map/ppermute | solution.py:276
  87.8 0.2 while.12
  88.0 2.3 %send.2 = bf16[6,128,512]{2,1,0:T(8,128)(2,1)S(1)} custom-call(s32[2]{0:T(128)S(1)} %pad_add_fusion.2.scalar_ref, bf16[256,768]{1,0:T(8,128)(2,1)} %get-tuple-element.240, bf16[768,512]{1,0:T(8,128)(2,1)S(1)} %bitcast.21, bf16[768,512]{1,0:T(8,128)(2,1)S(1)} %collective-permute-done.rest_1_, bf16[768,512]{1,0:T(8,128)(2,1)S(1)} %collective-permute-done.1.rest_2_, ...), custom_call_target="tpu_custom_call" | custom-call | flops 603979776 | bytes 4718592 | tf_op jit(solution)/shard_map/send/pallas_call | solution.py:232
  90.3 3.4 %collective-permute-start.5 = (bf16[6,128,512]{2,1,0:T(8,128)(2,1)S(1)}, bf16[6,128,512]{2,1,0:T(8,128)(2,1)S(1)}, u32[]{:S(2)}, u32[]{:S(2)}) collective-permute-start(bf16[6,128,512]{2,1,0:T(8,128)(2,1)S(1)} %send.2), channel_id=1, source_target_pairs={{0,1},{1,0},{2,3},{3,2},{4,5},{5,4},{6,7},{7,6},{8,9},{9,8},{10,11... | collective-permute-start | bytes 2359304 | tf_op jit(solution)/shard_map/ppermute | solution.py:340
  93.7 0.1 collective-permute-done.6.rest_0_.rest_6_
  93.8 13.7 %collective-permute-done.7.rest_1_.rest_7_ = bf16[768,512]{1,0:T(8,128)(2,1)} collective-permute-done((bf16[768,512]{1,0:T(8,128)(2,1)}, bf16[768,512]{1,0:T(8,128)(2,1)}, u32[]{:S(2)}, u32[]{:S(2)}) %collective-permute-start.7) | collective-permute-done | bytes 786464 | tf_op jit(solution)/shard_map/ppermute | solution.py:276
  107.6 1.8 %send.3 = bf16[2,128,512]{2,1,0:T(8,128)(2,1)S(1)} custom-call(s32[2]{0:T(128)S(1)} %pad_add_fusion.2.scalar_ref, bf16[256,768]{1,0:T(8,128)(2,1)S(1)} %copy-done.2, bf16[768,512]{1,0:T(8,128)(2,1)} %collective-permute-done.6.rest_0_.rest_6_, bf16[768,512]{1,0:T(8,128)(2,1)} %collective-permute-done.7.rest_1_.rest_7_), custom_call_target="tpu_custom_call" | custom-call | flops 201326592 | bytes 1572864 | tf_op jit(solution)/shard_map/send/pallas_call | solution.py:232
  109.3 3.1 %collective-permute-start.8 = (bf16[2,128,512]{2,1,0:T(8,128)(2,1)S(1)}, bf16[2,128,512]{2,1,0:T(8,128)(2,1)S(1)}, u32[]{:S(2)}, u32[]{:S(2)}) collective-permute-start(bf16[2,128,512]{2,1,0:T(8,128)(2,1)S(1)} %send.3), channel_id=1, source_target_pairs={{0,1},{1,0},{2,3},{3,2},{4,5},{5,4},{6,7},{7,6},{8,9},{9,8},{10,11... | collective-permute-start | bytes 786440 | tf_op jit(solution)/shard_map/ppermute | solution.py:340
  112.5 3.6 %keep.1.rest_2_ = bf16[128,8192]{1,0:T(8,128)(2,1)} custom-call(s32[2]{0:T(128)S(1)} %pad_add_fusion.2.scalar_ref, bf16[256,768]{1,0:T(8,128)(2,1)S(1)} %copy-done.2, bf16[768,512]{1,0:T(8,128)(2,1)S(1)} %bitcast.22, bf16[768,512]{1,0:T(8,128)(2,1)S(1)} %collective-permute-done.rest_1_, bf16[768,512]{1,0:T(8,128)(2,1)S(1)} %collective-permute-done.1.rest_2_, ...), custom_call_target="tpu_custom_call" | custom-call | flops 805306368 | bytes 6291456 | tf_op jit(solution)/shard_map/keep/pallas_call | solution.py:247
  116.0 3.2 %collective-permute-done.8.rest_1_ = bf16[2,128,512]{2,1,0:T(8,128)(2,1)S(1)} collective-permute-done((bf16[2,128,512]{2,1,0:T(8,128)(2,1)S(1)}, bf16[2,128,512]{2,1,0:T(8,128)(2,1)S(1)}, u32[]{:S(2)}, u32[]{:S(2)}) %collective-permute-start.8) | collective-permute-done | bytes 262176 | tf_op jit(solution)/shard_map/ppermute | solution.py:340
  119.3 1.6 %place.1 = bf16[128,8192]{1,0:T(8,128)(2,1)} custom-call(s32[2]{0:T(128)S(1)} %pad_add_fusion.2.scalar_ref, bf16[6,128,512]{2,1,0:T(8,128)(2,1)S(1)} %collective-permute-done.5.rest_0_, bf16[2,128,512]{2,1,0:T(8,128)(2,1)S(1)} %collective-permute-done.8.rest_1_, bf16[128,8192]{1,0:T(8,128)(2,1)} %keep.1.rest_2_), custom_call_target="tpu_custom_call", output_to_operand_aliasing={{}: (3, {})} | custom-call | tf_op jit(solution)/shard_map/place/pallas_call | solution.py:262
  (11 shorter events, 0.2 us)
Async XLA Ops:
  0.0 30.5 %collective-permute-start = (bf16[768,512]{1,0:T(8,128)(2,1)}, bf16[768,512]{1,0:T(8,128)(2,1)S(1)}, u32[]{:S(2)}, u32[]{:S(2)}) collective-permute-start(bf16[768,512]{1,0:T(8,128)(2,1)} %bitcast.19), channel_id=1, source_target_pairs={{0,2},{2,4},{4,6},{6,8},{8,10},{10,12},{12,14},{14,0},{1,3},{3,5},... | collective-permute-start | bytes 2359304 | tf_op jit(solution)/shard_map/ppermute | solution.py:276
  8.0 22.5 %all-to-all-start.3 = ((bf16[8,16,128]{2,1,0:T(8,128)(2,1)}), bf16[8,16,128]{2,1,0:T(8,128)(2,1)S(1)}, u32[]{:S(2)}, u32[]{:S(2)}) async-start(bf16[8,16,128]{2,1,0:T(8,128)(2,1)} %compact.5), calls=%async_computation.3 | async-start | bytes 65536 | tf_op jit(solution)/shard_map/all_to_all | solution.py:301
  17.4 30.1 %collective-permute-start.1 = (bf16[768,512]{1,0:T(8,128)(2,1)}, bf16[768,512]{1,0:T(8,128)(2,1)S(1)}, u32[]{:S(2)}, u32[]{:S(2)}) collective-permute-start(bf16[768,512]{1,0:T(8,128)(2,1)} %bitcast.20), channel_id=1, source_target_pairs={{0,14},{2,0},{4,2},{6,4},{8,6},{10,8},{12,10},{14,12},{1,15},{3,1}... | collective-permute-start | bytes 2359304 | tf_op jit(solution)/shard_map/ppermute | solution.py:276
  30.5 21.0 %collective-permute-start.2 = (bf16[768,512]{1,0:T(8,128)(2,1)S(1)}, bf16[768,512]{1,0:T(8,128)(2,1)S(1)}, u32[]{:S(2)}, u32[]{:S(2)}) collective-permute-start(bf16[768,512]{1,0:T(8,128)(2,1)S(1)} %collective-permute-done.rest_1_), channel_id=1, source_target_pairs={{0,2},{2,4},{4,6},{6,8},{8,10},{10,12},{12,14},{14,0},{1,3},{3,5},... | collective-permute-start | bytes 2359304 | tf_op jit(solution)/shard_map/ppermute | solution.py:276
  36.8 51.0 %copy-start = (bf16[12,64,512]{2,1,0:T(8,128)(2,1)S(1)}, bf16[12,64,512]{2,1,0:T(8,128)(2,1)}, u32[]{:S(2)}) copy-start(bf16[12,64,512]{2,1,0:T(8,128)(2,1)} %temps_ref.1) | copy-start | bytes 2359300
  36.8 24.8 %all-to-all-start.4 = ((bf16[64,4,768]{2,1,0:T(4,128)(2,1)}), bf16[64,4,768]{2,1,0:T(4,128)(2,1)S(1)}, u32[]{:S(2)}, u32[]{:S(2)}) async-start(bf16[64,4,768]{2,1,0:T(4,128)(2,1)} %reshape.25), calls=%async_computation.4 | async-start | bytes 786432 | tf_op jit(solution)/shard_map/all_to_all | solution.py:308
  47.5 24.5 %collective-permute-start.3 = (bf16[768,512]{1,0:T(8,128)(2,1)S(1)}, bf16[768,512]{1,0:T(8,128)(2,1)}, u32[]{:S(2)}, u32[]{:S(2)}) collective-permute-start(bf16[768,512]{1,0:T(8,128)(2,1)S(1)} %collective-permute-done.1.rest_2_), channel_id=1, source_target_pairs={{0,14},{2,0},{4,2},{6,4},{8,6},{10,8},{12,10},{14,12},{1,15},{3,1}... | collective-permute-start | bytes 2359304 | tf_op jit(solution)/shard_map/ppermute | solution.py:276
  51.5 32.6 %collective-permute-start.4 = (bf16[768,512]{1,0:T(8,128)(2,1)S(1)}, bf16[768,512]{1,0:T(8,128)(2,1)}, u32[]{:S(2)}, u32[]{:S(2)}) collective-permute-start(bf16[768,512]{1,0:T(8,128)(2,1)S(1)} %collective-permute-done.2.rest_3_), channel_id=1, source_target_pairs={{0,2},{2,4},{4,6},{6,8},{8,10},{10,12},{12,14},{14,0},{1,3},{3,5},... | collective-permute-start | bytes 2359304 | tf_op jit(solution)/shard_map/ppermute | solution.py:276
  62.6 20.7 %all-to-all-start.5 = ((bf16[64,4,768]{2,1,0:T(4,128)(2,1)}), bf16[64,4,768]{2,1,0:T(4,128)(2,1)S(1)}, u32[]{:S(2)}, u32[]{:S(2)}) async-start(bf16[64,4,768]{2,1,0:T(4,128)(2,1)} %broadcast_in_dim.7), calls=%async_computation.5 | async-start | bytes 786432 | tf_op jit(solution)/shard_map/all_to_all | solution.py:313
  72.0 21.8 %collective-permute-start.6 = (bf16[768,512]{1,0:T(8,128)(2,1)}, bf16[768,512]{1,0:T(8,128)(2,1)}, u32[]{:S(2)}, u32[]{:S(2)}) collective-permute-start(bf16[768,512]{1,0:T(8,128)(2,1)} %collective-permute-done.3.rest_4_), channel_id=1, source_target_pairs={{0,14},{2,0},{4,2},{6,4},{8,6},{10,8},{12,10},{14,12},{1,15},{3,1}... | collective-permute-start | bytes 2359304 | tf_op jit(solution)/shard_map/ppermute | solution.py:276
  84.1 23.5 %collective-permute-start.7 = (bf16[768,512]{1,0:T(8,128)(2,1)}, bf16[768,512]{1,0:T(8,128)(2,1)}, u32[]{:S(2)}, u32[]{:S(2)}) collective-permute-start(bf16[768,512]{1,0:T(8,128)(2,1)} %collective-permute-done.4.rest_5_), channel_id=1, source_target_pairs={{0,2},{2,4},{4,6},{6,8},{8,10},{10,12},{12,14},{14,0},{1,3},{3,5},... | collective-permute-start | bytes 2359304 | tf_op jit(solution)/shard_map/ppermute | solution.py:276
  88.0 19.6 %copy-start.2 = (bf16[256,768]{1,0:T(8,128)(2,1)S(1)}, bf16[256,768]{1,0:T(8,128)(2,1)}, u32[]{:S(2)}) copy-start(bf16[256,768]{1,0:T(8,128)(2,1)} %get-tuple-element.240) | copy-start | bytes 1179652
  90.3 25.7 %collective-permute-start.5 = (bf16[6,128,512]{2,1,0:T(8,128)(2,1)S(1)}, bf16[6,128,512]{2,1,0:T(8,128)(2,1)S(1)}, u32[]{:S(2)}, u32[]{:S(2)}) collective-permute-start(bf16[6,128,512]{2,1,0:T(8,128)(2,1)S(1)} %send.2), channel_id=1, source_target_pairs={{0,1},{1,0},{2,3},{3,2},{4,5},{5,4},{6,7},{7,6},{8,9},{9,8},{10,11... | collective-permute-start | bytes 2359304 | tf_op jit(solution)/shard_map/ppermute | solution.py:340
  109.3 9.9 %collective-permute-start.8 = (bf16[2,128,512]{2,1,0:T(8,128)(2,1)S(1)}, bf16[2,128,512]{2,1,0:T(8,128)(2,1)S(1)}, u32[]{:S(2)}, u32[]{:S(2)}) collective-permute-start(bf16[2,128,512]{2,1,0:T(8,128)(2,1)S(1)} %send.3), channel_id=1, source_target_pairs={{0,1},{1,0},{2,3},{3,2},{4,5},{5,4},{6,7},{7,6},{8,9},{9,8},{10,11... | collective-permute-start | bytes 786440 | tf_op jit(solution)/shard_map/ppermute | solution.py:340

commit v6 on v5

v6 whole, which is shorter than its diff:
```python
import functools
import math

import jax
import jax.numpy as jnp
from jax import lax
from jax.experimental import pallas as pl
from jax.experimental.pallas import tpu as pltpu
from jax.sharding import Mesh
from jax.sharding import PartitionSpec as P

AXES = ("y", "xh", "core", "z", "xl")
LISTS = ("z", "xh", "xl", "core")
PLANE = ("xh", "xl", "core", "y")
SLOTS = 8
F32, BF16 = jnp.float32, jnp.bfloat16
PARAMS = pltpu.CompilerParams(vmem_limit_bytes=16 * 2**20)
NT = (((1,), (1,)), ((), ()))
VMEM = pl.BlockSpec(memory_space=pltpu.VMEM)
SMEM = pl.BlockSpec(memory_space=pltpu.SMEM)
HBM = pl.BlockSpec(memory_space=pl.ANY)


def matmul(a, b, dims=(((1,), (0,)), ((), ()))):
    return lax.dot_general(a, b, dims, preferred_element_type=F32)


def ones(mask):
    return mask.astype(F32).astype(BF16)


def compact_kernel(scalar_ref, sensors_ref, temps_ref, out_ref):
    tiers, snaps, width = temps_ref.shape
    count, rows = sensors_ref.shape[1], out_ref.shape[0]
    span = 256
    group = count * SLOTS // rows
    first, start = scalar_ref[0], scalar_ref[1]
    before = lax.broadcasted_iota(jnp.int32, (span, span), 0)
    after = lax.broadcasted_iota(jnp.int32, (span, span), 1)
    together = before // group == after // group
    ahead, together = ones(together & (before < after)), ones(together)
    lower = ones(
        lax.broadcasted_iota(jnp.int32, (tiers, tiers), 0)
        > lax.broadcasted_iota(jnp.int32, (tiers, tiers), 1)
    )
    made = span * SLOTS // group
    row_ids = lax.broadcasted_iota(jnp.int32, (made, span), 0)
    tier_ids = lax.broadcasted_iota(jnp.int32, (tiers, span), 0)
    list_ids = lax.broadcasted_iota(jnp.int32, (tiers, span), 1) // group
    spots = []
    for low in range(0, count, span):
        offset = sensors_ref[:, low : low + span] - first
        mine = (offset >= 0) & (offset < width)
        held = ones(mine)
        slot = matmul(held, ahead) + matmul(matmul(lower, held).astype(BF16), together)
        slot = slot.astype(jnp.int32) - start
        slot = jnp.where(mine & (slot >= 0) & (slot < SLOTS), slot + list_ids * SLOTS, -1)
        spot = (offset + tier_ids * width + 1).astype(F32)
        found = jnp.zeros((made, span), F32)
        for tier in range(tiers):
            row = slice(tier, tier + 1)
            found = found + jnp.where(slot[row] == row_ids, spot[row], 0.0)
        spots.append(found.sum(axis=1, keepdims=True))
    spots = jnp.concatenate(spots, axis=0).astype(jnp.int32) - 1
    lanes = lax.broadcasted_iota(jnp.int32, (rows, width), 1)
    total = jnp.zeros((rows, snaps), F32)
    for tier in range(tiers):
        total = total + matmul(ones(spots - tier * width == lanes), temps_ref[tier], NT)
    out_ref[...] = jnp.concatenate([total, jnp.zeros_like(total)], axis=1).astype(BF16)


def compact(scalars, sensors, temps, lists):
    snaps = temps.shape[1]
    return pl.pallas_call(
        compact_kernel,
        in_specs=[SMEM, VMEM, VMEM],
        out_specs=VMEM,
        out_shape=jax.ShapeDtypeStruct((lists * SLOTS, 2 * snaps), BF16),
        compiler_params=PARAMS,
        name="compact",
    )(scalars, sensors, temps).reshape(lists, SLOTS, 2 * snaps)


def expand_kernel(shift, scalar_ref, rows_ref, columns_ref, lists_ref, out_ref):
    tiers, group = rows_ref.shape
    n_lists, slots, wide = lists_ref.shape
    y, start = scalar_ref[0], scalar_ref[1]
    rows, owners = rows_ref[...] >> shift, columns_ref[...] >> shift
    later = lax.broadcasted_iota(jnp.int32, (group, group), 0) > lax.broadcasted_iota(
        jnp.int32, (group, group), 1
    )
    lists = lists_ref[...].reshape(n_lists * slots, wide)
    lanes = lax.broadcasted_iota(jnp.int32, (group, n_lists * slots), 1)
    found = []
    for tier in range(tiers):
        owner = owners[:, tier : tier + 1]
        same = [(owner == rows[t : t + 1]).astype(F32) for t in range(tier + 1)]
        same[-1] = jnp.where(later, same[-1], 0.0)
        slot = sum(same[1:], same[0]).sum(axis=1, keepdims=True).astype(jnp.int32) - start
        sender = (owner >> 1 & 7) * 8 + (owner >> 5 & 1) * 4 + (owner & 1) * 2 + (owner >> 4 & 1)
        there = (owner >> 6 == y) & (slot >= 0) & (slot < slots)
        spot = jnp.where(there, sender * slots + slot, -1)
        found.append(matmul(ones(spot == lanes), lists)[:, : wide // 2])
    for tier in range(0, tiers, 2):
        pair = jnp.concatenate(found[tier : tier + 2], axis=1)
        out_ref[:, tier * wide // 2 : (tier + 2) * wide // 2] = pair.astype(BF16)


def expand(scalars, chosen, lists, width):
    tiers, group = chosen.shape
    return pl.pallas_call(
        functools.partial(expand_kernel, width.bit_length() - 1),
        in_specs=[SMEM, VMEM, VMEM, VMEM],
        out_specs=VMEM,
        out_shape=jax.ShapeDtypeStruct((group, tiers * lists.shape[2] // 2), BF16),
        compiler_params=PARAMS,
        name="expand",
    )(scalars, chosen, chosen.T, lists)


def longest_kernel(group, devices, shift, sensors_ref, out_ref):
    tiers, count = sensors_ref.shape
    span, low = 256, 16
    lists = span // group
    high_ids = lax.broadcasted_iota(jnp.int32, (devices // low, span), 0)
    low_ids = lax.broadcasted_iota(jnp.int32, (low * lists, span), 0)
    list_ids = lax.broadcasted_iota(jnp.int32, (1, span), 1) // group
    most = jnp.zeros((devices // low, low * lists), F32)
    for at in range(0, count, span):
        owner = sensors_ref[:, at : at + span] >> shift
        total = jnp.zeros_like(most)
        for tier in range(tiers):
            row = owner[tier : tier + 1]
            lows = (row & low - 1) + list_ids * low
            total = total + matmul(ones(row >> 4 == high_ids), ones(lows == low_ids), NT)
        most = jnp.maximum(most, total)
    out_ref[0, 0] = jnp.max(most).astype(jnp.int32)


def longest(sensors, group, devices, width):
    return pl.pallas_call(
        functools.partial(longest_kernel, group, devices, width.bit_length() - 1),
        in_specs=[VMEM],
        out_specs=SMEM,
        out_shape=jax.ShapeDtypeStruct((1, 1), jnp.int32),
        cost_estimate=pl.CostEstimate(
            flops=2 * sensors.size * devices, bytes_accessed=4 * sensors.size, transcendentals=0
        ),
        compiler_params=PARAMS,
        name="longest",
    )(sensors)[0, 0]


def correlation(scale, readings, block):
    depth = readings.shape[1] // len(block)
    parts = [
        matmul(readings[:, i * depth : (i + 1) * depth], part[...]) for i, part in enumerate(block)
    ]
    return (sum(parts[1:], parts[0]) * scale).astype(BF16)


def half_of(readings_ref, side):
    rows = readings_ref.shape[0] // 2
    return readings_ref[pl.ds(pl.multiple_of(side * rows, rows), rows)]


def grouped(refs, sizes):
    refs = iter(refs)
    return [[next(refs) for _ in range(size)] for size in sizes]


def send_kernel(scale, sizes, scalar_ref, readings_ref, *rest):
    readings = half_of(readings_ref, 1 - scalar_ref[1])
    for spot, block in enumerate(grouped(rest[:-1], sizes)):
        rest[-1][spot] = correlation(scale, readings, block)


def keep_kernel(scale, n_z, shifts, sizes, scalar_ref, readings_ref, *rest):
    *refs, out_ref, made, stored = rest
    readings = half_of(readings_ref, scalar_ref[1])
    stores = []
    for spot, block in enumerate(grouped(refs, sizes)):
        made[spot] = correlation(scale, readings, block)
        stores.append(
            pltpu.make_async_copy(
                made.at[spot], columns(out_ref, n_z, shifts[spot], scalar_ref, 0), stored.at[spot]
            )
        )
        stores[-1].start()
    for store in stores:
        store.wait()


def columns(out_ref, n_z, shift, scalar_ref, other):
    width = out_ref.shape[1] // (2 * n_z)
    side = 1 - scalar_ref[1] if other else scalar_ref[1]
    spot = (2 * lax.rem(scalar_ref[0] + shift + n_z, n_z) + side) * width
    return out_ref.at[:, pl.ds(pl.multiple_of(spot, width), width)]


def place_kernel(n_z, shifts, scalar_ref, *rest):
    *pieces, _, out_ref, done = rest
    stores = []
    for piece in pieces:
        for i in range(piece.shape[0]):
            spot = len(stores)
            stores.append(
                pltpu.make_async_copy(
                    piece.at[i], columns(out_ref, n_z, shifts[spot], scalar_ref, 1), done.at[spot]
                )
            )
            stores[-1].start()
    for store in stores:
        store.wait()


def cost(blocks, rows):
    pixels = sum(part.size for block in blocks for part in block)
    return pl.CostEstimate(flops=2 * rows * pixels, bytes_accessed=2 * pixels, transcendentals=0)


def send(here, readings, blocks):
    rows, depth = readings.shape[0] // 2, readings.shape[1]
    parts = [part for block in blocks for part in block]
    return pl.pallas_call(
        functools.partial(send_kernel, 1.0 / math.sqrt(depth), [len(block) for block in blocks]),
        in_specs=[SMEM, VMEM] + [VMEM] * len(parts),
        out_specs=VMEM,
        out_shape=jax.ShapeDtypeStruct((len(blocks), rows, parts[0].shape[1]), BF16),
        cost_estimate=cost(blocks, rows),
        compiler_params=PARAMS,
        name="send",
    )(here, readings, *parts)


def keep(here, readings, blocks, shifts):
    rows, depth = readings.shape[0] // 2, readings.shape[1]
    parts = [part for block in blocks for part in block]
    count, width = len(blocks), parts[0].shape[1]
    return pl.pallas_call(
        functools.partial(
            keep_kernel, 1.0 / math.sqrt(depth), count, shifts, [len(block) for block in blocks]
        ),
        in_specs=[SMEM, VMEM] + [VMEM] * len(parts),
        out_specs=HBM,
        out_shape=jax.ShapeDtypeStruct((rows, 2 * count * width), BF16),
        scratch_shapes=[pltpu.VMEM((count, rows, width), BF16), pltpu.SemaphoreType.DMA((count,))],
        cost_estimate=cost(blocks, rows),
        compiler_params=PARAMS,
        name="keep",
    )(here, readings, *parts)


def place(here, pieces, shifts, whole):
    return pl.pallas_call(
        functools.partial(place_kernel, len(shifts), shifts),
        in_specs=[SMEM] + [HBM] * (len(pieces) + 1),
        out_specs=HBM,
        out_shape=jax.ShapeDtypeStruct(whole.shape, BF16),
        scratch_shapes=[pltpu.SemaphoreType.DMA((len(shifts),))],
        input_output_aliases={len(pieces) + 1: 0},
        compiler_params=PARAMS,
        name="place",
    )(here, *pieces, whole)


def ring(value, shift):
    size = lax.axis_size("z")
    return lax.ppermute(value, "z", [(i, (i + shift) % size) for i in range(size)])


def body(temps, sensors):
    tiers, snaps, width = temps.shape
    depth = tiers * snaps
    n_z, n_y, n_lists, n_plane, devices = (lax.axis_size(a) for a in ("z", "y", LISTS, PLANE, AXES))
    group = sensors.shape[1] // n_lists
    z, xl = lax.axis_index("z"), lax.axis_index("xl")

    pixels = temps.reshape(depth, width)
    up, down = [pixels, ring(pixels, 1)], [pixels, ring(pixels, -1)]

    def go_on(blocks, shift, ready):
        block, _ = lax.optimization_barrier((blocks[-1], ready))
        blocks.append(ring(block, shift))

    first = lax.axis_index(AXES) * width
    def listed(number):
        return compact(jnp.stack([first, number * SLOTS]), sensors, temps, n_lists)

    def exchanged(lists):
        return lax.all_to_all(lists, LISTS, 0, 0, tiled=True)

    chosen = lax.dynamic_slice_in_dim(sensors, lax.axis_index(LISTS) * group, group, axis=1)

    def part_of(number, lists):
        return expand(jnp.stack([lax.axis_index("y"), number * SLOTS]), chosen, lists, width)

    def summed_of(part):
        part = lax.all_to_all(part.reshape(n_y, group // n_y, depth), "y", 0, 0, tiled=True)
        part = part.astype(F32).sum(axis=0).astype(BF16)
        return jnp.broadcast_to(part[None], (n_plane, *part.shape))

    def handed_out(part):
        return lax.all_to_all(part, PLANE, 0, 0, tiled=True).reshape(-1, depth)

    def one_round(number):
        return handed_out(summed_of(part_of(number, exchanged(listed(number)))))

    part = part_of(jnp.int32(0), exchanged(listed(jnp.int32(0))))
    go_on(up, 1, part)
    go_on(down, -1, part)
    part = summed_of(part)
    seen, _ = lax.optimization_barrier((sensors, part))
    rounds = pl.cdiv(longest(seen, group, devices, width), SLOTS)
    go_on(up, 1, part)
    go_on(down, -1, part)
    readings = handed_out(part)
    _, readings = lax.while_loop(
        lambda state: state[0] < rounds,
        lambda state: (state[0] + 1, state[1] + one_round(state[0])),
        (jnp.int32(1), readings),
    )

    here = jnp.stack([z, xl])

    def swapped(sent):
        return lax.ppermute(sent, "xl", [(0, 1), (1, 0)])

    sent = send(here, readings, [(block,) for block in (pixels, up[1], down[1], up[2], down[2])])
    above, below, _ = lax.optimization_barrier((up[3], down[3], sent))
    middle = depth // 2
    far = (ring(above[:middle], 1), ring(below[middle:], -1))
    blocks = [(block,) for block in (*up[:2], down[1], up[2], down[2], up[3], down[3])] + [far]
    shifts = [0, -1, 1, -2, 2, -3, 3, 4]
    pieces = [swapped(sent)]
    pieces += [swapped(send(here, readings, blocks[low:high])) for low, high in ((5, 7), (7, 8))]
    return place(here, pieces, shifts, keep(here, readings, blocks, shifts))


def solution(mesh):
    torus = Mesh(mesh.devices.reshape(8, 2, 2, 8, 2), AXES)
    return jax.shard_map(
        body,
        mesh=torus,
        in_specs=(P(None, None, AXES), P()),
        out_specs=P(("z", "xl"), ("y", "xh", "core")),
        check_vma=False,
    )
```

time: 122 us -> 128 us (1.049)
  the two profiles are of different devices: /device:TPU:8 before, /device:TPU:6 now
where the time goes in v6:
time: 128 us; the launch traced here: 126 us
  starting transfers between devices  69.7 us (54%)
  waiting for transfers between devices  31.1 us (24%)
  Pallas kernels  19.4 us (15%)
  local copies, waits for them, and re-layouts  3.86 us (3%)
    ppermute x8, starting transfers between devices, ring(): lax.ppermute(value, 'z', [(i, (i + shift) % size) for i in range(size)])  34.5 us
    ppermute x8, waiting for transfers between devices, ring(): lax.ppermute(value, 'z', [(i, (i + shift) % size) for i in range(size)])  12.2 us
    all_to_all x1, starting transfers between devices, handed_out(): return lax.all_to_all(part, PLANE, 0, 0, tiled=True).reshape(-1, depth)  10.1 us
    ppermute x3, starting transfers between devices, swapped(): return lax.ppermute(sent, 'xl', [(0, 1), (1, 0)])  10 us
    all_to_all x1, waiting for transfers between devices, handed_out(): return lax.all_to_all(part, PLANE, 0, 0, tiled=True).reshape(-1, depth)  9.62 us
    all_to_all x1, starting transfers between devices, exchanged(): return lax.all_to_all(lists, LISTS, 0, 0, tiled=True)  7.96 us
    all_to_all x1, waiting for transfers between devices, exchanged(): return lax.all_to_all(lists, LISTS, 0, 0, tiled=True)  7.6 us
    all_to_all x1, starting transfers between devices, summed_of(): lax.all_to_all(part.reshape(n_y, group // n_y, depth), 'y', 0, 0, tiled=T...  7.1 us
  transfers between devices with their start and end apart: 14, of which 8 were waited for; matrix products, arithmetic and copies ran while one was open for 3% of the time, Pallas kernels for 11%

profile of v6, /device:TPU:6, one launch (start us, length us, event | category | flops | bytes accessed | tf_op | source)
XLA Modules:
  0.0 125.6 jit_solution(12111889545544490084)
XLA Ops:
  0.0 4.3 %collective-permute-start = (bf16[768,512]{1,0:T(8,128)(2,1)}, bf16[768,512]{1,0:T(8,128)(2,1)S(1)}, u32[]{:S(2)}, u32[]{:S(2)}) collective-permute-start(bf16[768,512]{1,0:T(8,128)(2,1)} %bitcast.23), channel_id=1, source_target_pairs={{0,2},{2,4},{4,6},{6,8},{8,10},{10,12},{12,14},{14,0},{1,3},{3,5},... | collective-permute-start | bytes 2359304 | tf_op jit(solution)/shard_map/ppermute | solution.py:269
  4.3 8.6 %collective-permute-start.1 = (bf16[768,512]{1,0:T(8,128)(2,1)}, bf16[768,512]{1,0:T(8,128)(2,1)S(1)}, u32[]{:S(2)}, u32[]{:S(2)}) collective-permute-start(bf16[768,512]{1,0:T(8,128)(2,1)} %bitcast.24), channel_id=1, source_target_pairs={{0,14},{2,0},{4,2},{6,4},{8,6},{10,8},{12,10},{14,12},{1,15},{3,1}... | collective-permute-start | bytes 2359304 | tf_op jit(solution)/shard_map/ppermute | solution.py:269
  13.0 5.0 %compact.5 = bf16[512,128]{1,0:T(8,128)(2,1)} custom-call(s32[2]{0:T(128)S(1)} %pad_add_fusion.2.scalar_ref, s32[12,2048]{1,0:T(8,128)} %sensors_ref.2, bf16[12,64,512]{2,1,0:T(8,128)(2,1)} %temps_ref.1), custom_call_target="tpu_custom_call" | custom-call | tf_op jit(solution)/shard_map/compact/pallas_call | solution.py:74
  18.0 8.0 %all-to-all-start.3 = ((bf16[64,8,128]{2,1,0:T(8,128)(2,1)}), bf16[64,8,128]{2,1,0:T(8,128)(2,1)S(1)}, u32[]{:S(2)}, u32[]{:S(2)}) async-start(bf16[64,8,128]{2,1,0:T(8,128)(2,1)} %bitcast.10), calls=%async_computation.3 | async-start | bytes 262144 | tf_op jit(solution)/shard_map/all_to_all | solution.py:291
  26.0 0.8 constant_dynamic-slice_fusion.rows_ref
  27.5 7.6 %all-to-all-done.3.lists_ref = bf16[64,8,128]{2,1,0:T(8,128)(2,1)S(1)} async-done(((bf16[64,8,128]{2,1,0:T(8,128)(2,1)}), bf16[64,8,128]{2,1,0:T(8,128)(2,1)S(1)}, u32[]{:S(2)}, u32[]{:S(2)}) %all-to-all-start.3) | async-done | bytes 131104 | tf_op jit(solution)/shard_map/all_to_all | solution.py:291
  35.1 1.7 %expand.5 = bf16[32,768]{1,0:T(8,128)(2,1)S(1)} custom-call(s32[2]{0:T(128)S(1)} %pad_add_fusion.3.scalar_ref, s32[12,32]{1,0:T(8,128)S(1)} %constant_dynamic-slice_fusion.rows_ref, s32[32,12]{1,0:T(8,128)} %bitcast.8.columns_ref, bf16[64,8,128]{2,1,0:T(8,128)(2,1)S(1)} %all-to-all-done.3.lists_ref), custom_call_target="tpu_custom_call" | custom-call | tf_op jit(solution)/shard_map/expand/pallas_call | solution.py:111
  37.4 7.1 %all-to-all-start.4 = ((bf16[8,4,768]{2,1,0:T(4,128)(2,1)}), bf16[8,4,768]{2,1,0:T(4,128)(2,1)S(1)}, u32[]{:S(2)}, u32[]{:S(2)}) async-start(bf16[8,4,768]{2,1,0:T(4,128)(2,1)} %reshape.35), calls=%async_computation.4 | async-start | bytes 98304 | tf_op jit(solution)/shard_map/all_to_all | solution.py:299
  44.5 4.0 %collective-permute-start.2 = (bf16[768,512]{1,0:T(8,128)(2,1)S(1)}, bf16[768,512]{1,0:T(8,128)(2,1)}, u32[]{:S(2)}, u32[]{:S(2)}) collective-permute-start(bf16[768,512]{1,0:T(8,128)(2,1)S(1)} %collective-permute-done.rest_1_), channel_id=1, source_target_pairs={{0,2},{2,4},{4,6},{6,8},{8,10},{10,12},{12,14},{14,0},{1,3},{3,5},... | collective-permute-start | bytes 2359304 | tf_op jit(solution)/shard_map/ppermute | solution.py:269
  48.6 3.0 %collective-permute-start.3 = (bf16[768,512]{1,0:T(8,128)(2,1)S(1)}, bf16[768,512]{1,0:T(8,128)(2,1)}, u32[]{:S(2)}, u32[]{:S(2)}) collective-permute-start(bf16[768,512]{1,0:T(8,128)(2,1)S(1)} %collective-permute-done.1.rest_2_), channel_id=1, source_target_pairs={{0,14},{2,0},{4,2},{6,4},{8,6},{10,8},{12,10},{14,12},{1,15},{3,1}... | collective-permute-start | bytes 2359304 | tf_op jit(solution)/shard_map/ppermute | solution.py:269
  51.6 1.1 all-to-all-done.4
  52.8 0.9 broadcast_in_dim.7
  53.6 10.1 %all-to-all-start.5 = ((bf16[64,4,768]{2,1,0:T(4,128)(2,1)}), bf16[64,4,768]{2,1,0:T(4,128)(2,1)S(1)}, u32[]{:S(2)}, u32[]{:S(2)}) async-start(bf16[64,4,768]{2,1,0:T(4,128)(2,1)} %broadcast_in_dim.7), calls=%async_computation.5 | async-start | bytes 786432 | tf_op jit(solution)/shard_map/all_to_all | solution.py:304
  63.9 3.8 %longest.1 = s32[1,1]{1,0:T(1,128)} custom-call(s32[12,2048]{1,0:T(8,128)} %sensors_ref.2), custom_call_target="tpu_custom_call" | custom-call | flops 25165824 | bytes 98304 | tf_op jit(solution)/shard_map/longest/pallas_call | solution.py:141
  68.3 9.6 %all-to-all-done.5 = bf16[64,4,768]{2,1,0:T(4,128)(2,1)S(1)} async-done(((bf16[64,4,768]{2,1,0:T(4,128)(2,1)}), bf16[64,4,768]{2,1,0:T(4,128)(2,1)S(1)}, u32[]{:S(2)}, u32[]{:S(2)}) %all-to-all-start.5) | async-done | bytes 393248 | tf_op jit(solution)/shard_map/all_to_all | solution.py:304
  77.9 0.8 reshape.36
  78.8 2.2 %collective-permute-start.5 = (bf16[768,512]{1,0:T(8,128)(2,1)}, bf16[768,512]{1,0:T(8,128)(2,1)S(1)}, u32[]{:S(2)}, u32[]{:S(2)}) collective-permute-start(bf16[768,512]{1,0:T(8,128)(2,1)} %collective-permute-done.2.rest_3_), channel_id=1, source_target_pairs={{0,2},{2,4},{4,6},{6,8},{8,10},{10,12},{12,14},{14,0},{1,3},{3,5},... | collective-permute-start | bytes 2359304 | tf_op jit(solution)/shard_map/ppermute | solution.py:269
  81.0 4.9 %collective-permute-start.6 = (bf16[768,512]{1,0:T(8,128)(2,1)}, bf16[768,512]{1,0:T(8,128)(2,1)S(1)}, u32[]{:S(2)}, u32[]{:S(2)}) collective-permute-start(bf16[768,512]{1,0:T(8,128)(2,1)} %collective-permute-done.3.rest_4_), channel_id=1, source_target_pairs={{0,14},{2,0},{4,2},{6,4},{8,6},{10,8},{12,10},{14,12},{1,15},{3,1}... | collective-permute-start | bytes 2359304 | tf_op jit(solution)/shard_map/ppermute | solution.py:269
  86.1 2.5 %send.3 = bf16[5,128,512]{2,1,0:T(8,128)(2,1)S(1)} custom-call(s32[2]{0:T(128)S(1)} %pad_add_fusion.4.scalar_ref, bf16[256,768]{1,0:T(8,128)(2,1)} %get-tuple-element.102.readings_ref, bf16[768,512]{1,0:T(8,128)(2,1)} %bitcast.25, bf16[768,512]{1,0:T(8,128)(2,1)S(1)} %collective-permute-done.rest_1_, bf16[768,512]{1,0:T(8,128)(2,1)S(1)} %collective-permute-done.1.rest_2_, ...), custom_call_target="tpu_custom_call" | custom-call | flops 503316480 | bytes 3932160 | tf_op jit(solution)/shard_map/send/pallas_call | solution.py:225
  88.5 3.6 %collective-permute-start.4 = (bf16[5,128,512]{2,1,0:T(8,128)(2,1)S(1)}, bf16[5,128,512]{2,1,0:T(8,128)(2,1)S(1)}, u32[]{:S(2)}, u32[]{:S(2)}) collective-permute-start(bf16[5,128,512]{2,1,0:T(8,128)(2,1)S(1)} %send.3), channel_id=1, source_target_pairs={{0,1},{1,0},{2,3},{3,2},{4,5},{5,4},{6,7},{7,6},{8,9},{9,8},{10,11... | collective-permute-start | bytes 1966088 | tf_op jit(solution)/shard_map/ppermute | solution.py:327
  92.1 8.6 %collective-permute-done.5.rest_0_.rest_5_ = bf16[768,512]{1,0:T(8,128)(2,1)S(1)} collective-permute-done((bf16[768,512]{1,0:T(8,128)(2,1)}, bf16[768,512]{1,0:T(8,128)(2,1)S(1)}, u32[]{:S(2)}, u32[]{:S(2)}) %collective-permute-start.5) | collective-permute-done | bytes 786464 | tf_op jit(solution)/shard_map/ppermute | solution.py:269
  100.7 1.3 %collective-permute-done.6.rest_1_.rest_6_ = bf16[768,512]{1,0:T(8,128)(2,1)S(1)} collective-permute-done((bf16[768,512]{1,0:T(8,128)(2,1)}, bf16[768,512]{1,0:T(8,128)(2,1)S(1)}, u32[]{:S(2)}, u32[]{:S(2)}) %collective-permute-start.6) | collective-permute-done | bytes 786464 | tf_op jit(solution)/shard_map/ppermute | solution.py:269
  102.1 2.1 %collective-permute-start.8 = (bf16[384,512]{1,0:T(8,128)(2,1)S(1)}, bf16[384,512]{1,0:T(8,128)(2,1)S(1)}, u32[]{:S(2)}, u32[]{:S(2)}) collective-permute-start(bf16[384,512]{1,0:T(8,128)(2,1)S(1)} %slice.6), channel_id=1, source_target_pairs={{0,2},{2,4},{4,6},{6,8},{8,10},{10,12},{12,14},{14,0},{1,3},{3,5},... | collective-permute-start | bytes 1179656 | tf_op jit(solution)/shard_map/ppermute | solution.py:269
  104.2 5.5 %collective-permute-start.9 = (bf16[384,512]{1,0:T(8,128)(2,1)S(1)}, bf16[384,512]{1,0:T(8,128)(2,1)S(1)}, u32[]{:S(2)}, u32[]{:S(2)}) collective-permute-start(bf16[384,512]{1,0:T(8,128)(2,1)S(1)} %slice.7), channel_id=1, source_target_pairs={{0,14},{2,0},{4,2},{6,4},{8,6},{10,8},{12,10},{14,12},{1,15},{3,1}... | collective-permute-start | bytes 1179656 | tf_op jit(solution)/shard_map/ppermute | solution.py:269
  109.7 0.9 send.4
  110.6 3.3 %collective-permute-start.7 = (bf16[2,128,512]{2,1,0:T(8,128)(2,1)S(1)}, bf16[2,128,512]{2,1,0:T(8,128)(2,1)S(1)}, u32[]{:S(2)}, u32[]{:S(2)}) collective-permute-start(bf16[2,128,512]{2,1,0:T(8,128)(2,1)S(1)} %send.4), channel_id=1, source_target_pairs={{0,1},{1,0},{2,3},{3,2},{4,5},{5,4},{6,7},{7,6},{8,9},{9,8},{10,11... | collective-permute-start | bytes 786440 | tf_op jit(solution)/shard_map/ppermute | solution.py:327
  113.9 1.0 collective-permute-done.8.rest_0_.rest_7_
  115.0 1.2 collective-permute-done.9.rest_1_.rest_8_
  116.2 0.8 send.5
  117.0 3.1 %collective-permute-start.10 = (bf16[1,128,512]{2,1,0:T(8,128)(2,1)S(1)}, bf16[1,128,512]{2,1,0:T(8,128)(2,1)S(1)}, u32[]{:S(2)}, u32[]{:S(2)}) collective-permute-start(bf16[1,128,512]{2,1,0:T(8,128)(2,1)S(1)} %send.5), channel_id=1, source_target_pairs={{0,1},{1,0},{2,3},{3,2},{4,5},{5,4},{6,7},{7,6},{8,9},{9,8},{10,11... | collective-permute-start | bytes 393224 | tf_op jit(solution)/shard_map/ppermute | solution.py:327
  120.1 3.1 %keep.1.rest_3_ = bf16[128,8192]{1,0:T(8,128)(2,1)} custom-call(s32[2]{0:T(128)S(1)} %pad_add_fusion.4.scalar_ref, bf16[256,768]{1,0:T(8,128)(2,1)S(1)} %copy-done.3, bf16[768,512]{1,0:T(8,128)(2,1)S(1)} %bitcast.26, bf16[768,512]{1,0:T(8,128)(2,1)S(1)} %collective-permute-done.rest_1_, bf16[768,512]{1,0:T(8,128)(2,1)S(1)} %collective-permute-done.1.rest_2_, ...), custom_call_target="tpu_custom_call" | custom-call | flops 805306368 | bytes 6291456 | tf_op jit(solution)/shard_map/keep/pallas_call | solution.py:240
  123.9 1.6 %place.1 = bf16[128,8192]{1,0:T(8,128)(2,1)} custom-call(s32[2]{0:T(128)S(1)} %pad_add_fusion.4.scalar_ref, bf16[5,128,512]{2,1,0:T(8,128)(2,1)S(1)} %collective-permute-done.4.rest_0_, bf16[2,128,512]{2,1,0:T(8,128)(2,1)S(1)} %collective-permute-done.7.rest_1_, ...), custom_call_target="tpu_custom_call", output_to_operand_aliasing={{}: (4, {})} | custom-call | tf_op jit(solution)/shard_map/place/pallas_call | solution.py:255
  (20 shorter events, 2.5 us)
Async XLA Ops:
  0.0 44.5 %collective-permute-start = (bf16[768,512]{1,0:T(8,128)(2,1)}, bf16[768,512]{1,0:T(8,128)(2,1)S(1)}, u32[]{:S(2)}, u32[]{:S(2)}) collective-permute-start(bf16[768,512]{1,0:T(8,128)(2,1)} %bitcast.23), channel_id=1, source_target_pairs={{0,2},{2,4},{4,6},{6,8},{8,10},{10,12},{12,14},{14,0},{1,3},{3,5},... | collective-permute-start | bytes 2359304 | tf_op jit(solution)/shard_map/ppermute | solution.py:269
  4.3 44.3 %collective-permute-start.1 = (bf16[768,512]{1,0:T(8,128)(2,1)}, bf16[768,512]{1,0:T(8,128)(2,1)S(1)}, u32[]{:S(2)}, u32[]{:S(2)}) collective-permute-start(bf16[768,512]{1,0:T(8,128)(2,1)} %bitcast.24), channel_id=1, source_target_pairs={{0,14},{2,0},{4,2},{6,4},{8,6},{10,8},{12,10},{14,12},{1,15},{3,1}... | collective-permute-start | bytes 2359304 | tf_op jit(solution)/shard_map/ppermute | solution.py:269
  18.0 17.1 %all-to-all-start.3 = ((bf16[64,8,128]{2,1,0:T(8,128)(2,1)}), bf16[64,8,128]{2,1,0:T(8,128)(2,1)S(1)}, u32[]{:S(2)}, u32[]{:S(2)}) async-start(bf16[64,8,128]{2,1,0:T(8,128)(2,1)} %bitcast.10), calls=%async_computation.3 | async-start | bytes 262144 | tf_op jit(solution)/shard_map/all_to_all | solution.py:291
  37.4 15.3 %all-to-all-start.4 = ((bf16[8,4,768]{2,1,0:T(4,128)(2,1)}), bf16[8,4,768]{2,1,0:T(4,128)(2,1)S(1)}, u32[]{:S(2)}, u32[]{:S(2)}) async-start(bf16[8,4,768]{2,1,0:T(4,128)(2,1)} %reshape.35), calls=%async_computation.4 | async-start | bytes 98304 | tf_op jit(solution)/shard_map/all_to_all | solution.py:299
  44.5 34.2 %collective-permute-start.2 = (bf16[768,512]{1,0:T(8,128)(2,1)S(1)}, bf16[768,512]{1,0:T(8,128)(2,1)}, u32[]{:S(2)}, u32[]{:S(2)}) collective-permute-start(bf16[768,512]{1,0:T(8,128)(2,1)S(1)} %collective-permute-done.rest_1_), channel_id=1, source_target_pairs={{0,2},{2,4},{4,6},{6,8},{8,10},{10,12},{12,14},{14,0},{1,3},{3,5},... | collective-permute-start | bytes 2359304 | tf_op jit(solution)/shard_map/ppermute | solution.py:269
  48.6 32.4 %collective-permute-start.3 = (bf16[768,512]{1,0:T(8,128)(2,1)S(1)}, bf16[768,512]{1,0:T(8,128)(2,1)}, u32[]{:S(2)}, u32[]{:S(2)}) collective-permute-start(bf16[768,512]{1,0:T(8,128)(2,1)S(1)} %collective-permute-done.1.rest_2_), channel_id=1, source_target_pairs={{0,14},{2,0},{4,2},{6,4},{8,6},{10,8},{12,10},{14,12},{1,15},{3,1}... | collective-permute-start | bytes 2359304 | tf_op jit(solution)/shard_map/ppermute | solution.py:269
  53.6 24.3 %all-to-all-start.5 = ((bf16[64,4,768]{2,1,0:T(4,128)(2,1)}), bf16[64,4,768]{2,1,0:T(4,128)(2,1)S(1)}, u32[]{:S(2)}, u32[]{:S(2)}) async-start(bf16[64,4,768]{2,1,0:T(4,128)(2,1)} %broadcast_in_dim.7), calls=%async_computation.5 | async-start | bytes 786432 | tf_op jit(solution)/shard_map/all_to_all | solution.py:304
  78.8 21.9 %collective-permute-start.5 = (bf16[768,512]{1,0:T(8,128)(2,1)}, bf16[768,512]{1,0:T(8,128)(2,1)S(1)}, u32[]{:S(2)}, u32[]{:S(2)}) collective-permute-start(bf16[768,512]{1,0:T(8,128)(2,1)} %collective-permute-done.2.rest_3_), channel_id=1, source_target_pairs={{0,2},{2,4},{4,6},{6,8},{8,10},{10,12},{12,14},{14,0},{1,3},{3,5},... | collective-permute-start | bytes 2359304 | tf_op jit(solution)/shard_map/ppermute | solution.py:269
  81.0 21.0 %collective-permute-start.6 = (bf16[768,512]{1,0:T(8,128)(2,1)}, bf16[768,512]{1,0:T(8,128)(2,1)S(1)}, u32[]{:S(2)}, u32[]{:S(2)}) collective-permute-start(bf16[768,512]{1,0:T(8,128)(2,1)} %collective-permute-done.3.rest_4_), channel_id=1, source_target_pairs={{0,14},{2,0},{4,2},{6,4},{8,6},{10,8},{12,10},{14,12},{1,15},{3,1}... | collective-permute-start | bytes 2359304 | tf_op jit(solution)/shard_map/ppermute | solution.py:269
  86.0 23.6 %copy-start.3 = (bf16[256,768]{1,0:T(8,128)(2,1)S(1)}, bf16[256,768]{1,0:T(8,128)(2,1)}, u32[]{:S(2)}) copy-start(bf16[256,768]{1,0:T(8,128)(2,1)} %get-tuple-element.102.readings_ref) | copy-start | bytes 1179652
  88.5 34.7 %collective-permute-start.4 = (bf16[5,128,512]{2,1,0:T(8,128)(2,1)S(1)}, bf16[5,128,512]{2,1,0:T(8,128)(2,1)S(1)}, u32[]{:S(2)}, u32[]{:S(2)}) collective-permute-start(bf16[5,128,512]{2,1,0:T(8,128)(2,1)S(1)} %send.3), channel_id=1, source_target_pairs={{0,1},{1,0},{2,3},{3,2},{4,5},{5,4},{6,7},{7,6},{8,9},{9,8},{10,11... | collective-permute-start | bytes 1966088 | tf_op jit(solution)/shard_map/ppermute | solution.py:327
  102.1 18.1 %copy-start = (bf16[12,64,512]{2,1,0:T(8,128)(2,1)S(1)}, bf16[12,64,512]{2,1,0:T(8,128)(2,1)}, u32[]{:S(2)}) copy-start(bf16[12,64,512]{2,1,0:T(8,128)(2,1)} %get-tuple-element.221) | copy-start | bytes 2359300
  102.1 12.9 %collective-permute-start.8 = (bf16[384,512]{1,0:T(8,128)(2,1)S(1)}, bf16[384,512]{1,0:T(8,128)(2,1)S(1)}, u32[]{:S(2)}, u32[]{:S(2)}) collective-permute-start(bf16[384,512]{1,0:T(8,128)(2,1)S(1)} %slice.6), channel_id=1, source_target_pairs={{0,2},{2,4},{4,6},{6,8},{8,10},{10,12},{12,14},{14,0},{1,3},{3,5},... | collective-permute-start | bytes 1179656 | tf_op jit(solution)/shard_map/ppermute | solution.py:269
  104.2 12.0 %collective-permute-start.9 = (bf16[384,512]{1,0:T(8,128)(2,1)S(1)}, bf16[384,512]{1,0:T(8,128)(2,1)S(1)}, u32[]{:S(2)}, u32[]{:S(2)}) collective-permute-start(bf16[384,512]{1,0:T(8,128)(2,1)S(1)} %slice.7), channel_id=1, source_target_pairs={{0,14},{2,0},{4,2},{6,4},{8,6},{10,8},{12,10},{14,12},{1,15},{3,1}... | collective-permute-start | bytes 1179656 | tf_op jit(solution)/shard_map/ppermute | solution.py:269
  110.6 12.7 %collective-permute-start.7 = (bf16[2,128,512]{2,1,0:T(8,128)(2,1)S(1)}, bf16[2,128,512]{2,1,0:T(8,128)(2,1)S(1)}, u32[]{:S(2)}, u32[]{:S(2)}) collective-permute-start(bf16[2,128,512]{2,1,0:T(8,128)(2,1)S(1)} %send.4), channel_id=1, source_target_pairs={{0,1},{1,0},{2,3},{3,2},{4,5},{5,4},{6,7},{7,6},{8,9},{9,8},{10,11... | collective-permute-start | bytes 786440 | tf_op jit(solution)/shard_map/ppermute | solution.py:327
  117.0 6.9 %collective-permute-start.10 = (bf16[1,128,512]{2,1,0:T(8,128)(2,1)S(1)}, bf16[1,128,512]{2,1,0:T(8,128)(2,1)S(1)}, u32[]{:S(2)}, u32[]{:S(2)}) collective-permute-start(bf16[1,128,512]{2,1,0:T(8,128)(2,1)S(1)} %send.5), channel_id=1, source_target_pairs={{0,1},{1,0},{2,3},{3,2},{4,5},{5,4},{6,7},{7,6},{8,9},{9,8},{10,11... | collective-permute-start | bytes 393224 | tf_op jit(solution)/shard_map/ppermute | solution.py:327

commit v7 on v6

--- a/solution.py
+++ b/solution.py
@@ -106,7 +106,7 @@
         out_ref[:, tier * wide // 2 : (tier + 2) * wide // 2] = pair.astype(BF16)
 
 
-def expand(scalars, chosen, lists, width):
+def expand(scalars, chosen, turned, lists, width):
     tiers, group = chosen.shape
     return pl.pallas_call(
         functools.partial(expand_kernel, width.bit_length() - 1),
@@ -115,7 +115,7 @@
         out_shape=jax.ShapeDtypeStruct((group, tiers * lists.shape[2] // 2), BF16),
         compiler_params=PARAMS,
         name="expand",
-    )(scalars, chosen, chosen.T, lists)
+    )(scalars, chosen, turned, lists)
 
 
 def longest_kernel(group, devices, shift, sensors_ref, out_ref):
@@ -144,7 +144,7 @@
         out_specs=SMEM,
         out_shape=jax.ShapeDtypeStruct((1, 1), jnp.int32),
         cost_estimate=pl.CostEstimate(
-            flops=2 * sensors.size * devices, bytes_accessed=4 * sensors.size, transcendentals=0
+            flops=100 * sensors.size * devices, bytes_accessed=4 * sensors.size, transcendentals=0
         ),
         compiler_params=PARAMS,
         name="longest",
@@ -277,23 +277,23 @@
     z, xl = lax.axis_index("z"), lax.axis_index("xl")
 
     pixels = temps.reshape(depth, width)
-    up, down = [pixels, ring(pixels, 1)], [pixels, ring(pixels, -1)]
-
-    def go_on(blocks, shift, ready):
-        block, _ = lax.optimization_barrier((blocks[-1], ready))
-        blocks.append(ring(block, shift))
+    near = [ring(pixels, shift) for shift in (1, -1)]
+
+    def after(ready, *values):
+        return lax.optimization_barrier((*values, ready))[:-1]
 
     first = lax.axis_index(AXES) * width
+    chosen = lax.dynamic_slice_in_dim(sensors, lax.axis_index(LISTS) * group, group, axis=1)
+    chosen, turned, sensors = lax.optimization_barrier((chosen, chosen.T, sensors))
+
     def listed(number):
         return compact(jnp.stack([first, number * SLOTS]), sensors, temps, n_lists)
 
     def exchanged(lists):
         return lax.all_to_all(lists, LISTS, 0, 0, tiled=True)
 
-    chosen = lax.dynamic_slice_in_dim(sensors, lax.axis_index(LISTS) * group, group, axis=1)
-
     def part_of(number, lists):
-        return expand(jnp.stack([lax.axis_index("y"), number * SLOTS]), chosen, lists, width)
+        return expand(jnp.stack([lax.axis_index("y"), number * SLOTS]), chosen, turned, lists, width)
 
     def summed_of(part):
         part = lax.all_to_all(part.reshape(n_y, group // n_y, depth), "y", 0, 0, tiled=True)
@@ -306,15 +306,16 @@
     def one_round(number):
         return handed_out(summed_of(part_of(number, exchanged(listed(number)))))
 
-    part = part_of(jnp.int32(0), exchanged(listed(jnp.int32(0))))
-    go_on(up, 1, part)
-    go_on(down, -1, part)
-    part = summed_of(part)
-    seen, _ = lax.optimization_barrier((sensors, part))
+    lists = listed(jnp.int32(0))
+    (again,) = after(lists, pixels)
+    second = [ring(again, shift) for shift in (2, -2)]
+    part = summed_of(part_of(jnp.int32(0), exchanged(lists)))
+    above, below, seen = after(part, *second, sensors)
+    third = [ring(above, 1), ring(below, -1)]
+    middle = depth // 2
+    far = (ring(above[:middle], 2), ring(below[middle:], -2))
+    readings = handed_out(part)
     rounds = pl.cdiv(longest(seen, group, devices, width), SLOTS)
-    go_on(up, 1, part)
-    go_on(down, -1, part)
-    readings = handed_out(part)
     _, readings = lax.while_loop(
         lambda state: state[0] < rounds,
         lambda state: (state[0] + 1, state[1] + one_round(state[0])),
@@ -326,14 +327,11 @@
     def swapped(sent):
         return lax.ppermute(sent, "xl", [(0, 1), (1, 0)])
 
-    sent = send(here, readings, [(block,) for block in (pixels, up[1], down[1], up[2], down[2])])
-    above, below, _ = lax.optimization_barrier((up[3], down[3], sent))
-    middle = depth // 2
-    far = (ring(above[:middle], 1), ring(below[middle:], -1))
-    blocks = [(block,) for block in (*up[:2], down[1], up[2], down[2], up[3], down[3])] + [far]
+    blocks = [(block,) for block in (pixels, *near, *second, *third)] + [far]
     shifts = [0, -1, 1, -2, 2, -3, 3, 4]
-    pieces = [swapped(sent)]
-    pieces += [swapped(send(here, readings, blocks[low:high])) for low, high in ((5, 7), (7, 8))]
+    pieces = [
+        swapped(send(here, readings, blocks[low:high])) for low, high in ((0, 5), (5, 7), (7, 8))
+    ]
     return place(here, pieces, shifts, keep(here, readings, blocks, shifts))
 
 

time: 128 us -> 126 us (0.984); the launches traced: 126 us -> 125 us
    ppermute x8, waiting for transfers between devices: 12.2 us -> 27.8 us  [ring(): lax.ppermute(value, 'z', [(i, (i + shift) % size) for i in range(size)])]
    all_to_all x1, waiting for transfers between devices: 9.62 us -> 0.01 us  [handed_out(): return lax.all_to_all(part, PLANE, 0, 0, tiled=True).reshape(-1, depth)]
    all_to_all x1, waiting for transfers between devices: 7.6 us -> 1.04 us  [exchanged(): return lax.all_to_all(lists, LISTS, 0, 0, tiled=True)]
    all_to_all x1, starting transfers between devices: 7.96 us -> 13.8 us  [exchanged(): return lax.all_to_all(lists, LISTS, 0, 0, tiled=True)]
    ppermute x8, starting transfers between devices: 34.5 us -> 30.1 us  [ring(): lax.ppermute(value, 'z', [(i, (i + shift) % size) for i in range(size)])]
    ppermute x3, starting transfers between devices: 10 us -> 8.27 us  [swapped(): return lax.ppermute(sent, 'xl', [(0, 1), (1, 0)])]
  transfers between devices with their start and end apart: 14 -> 14, of which waited for: 8 -> 10; matrix products, arithmetic and copies ran while one was open for 3% -> 2% of each run, Pallas kernels for 11% -> 7%
where the time goes in v7:
time: 126 us; the launch traced here: 125 us
  starting transfers between devices  69.4 us (55%)
  waiting for transfers between devices  31.3 us (25%)
  Pallas kernels  19.6 us (16%)
  local copies, waits for them, and re-layouts  3.34 us (3%)
    ppermute x8, starting transfers between devices, ring(): lax.ppermute(value, 'z', [(i, (i + shift) % size) for i in range(size)])  30.1 us
    ppermute x8, waiting for transfers between devices, ring(): lax.ppermute(value, 'z', [(i, (i + shift) % size) for i in range(size)])  27.8 us
    all_to_all x1, starting transfers between devices, exchanged(): return lax.all_to_all(lists, LISTS, 0, 0, tiled=True)  13.8 us
    all_to_all x1, starting transfers between devices, handed_out(): return lax.all_to_all(part, PLANE, 0, 0, tiled=True).reshape(-1, depth)  10.1 us
    ppermute x3, starting transfers between devices, swapped(): return lax.ppermute(sent, 'xl', [(0, 1), (1, 0)])  8.27 us
    all_to_all x1, starting transfers between devices, summed_of(): lax.all_to_all(part.reshape(n_y, group // n_y, depth), 'y', 0, 0, tiled=T...  7.1 us
    pallas_call x1, Pallas kernels, compact(): pl.pallas_call(compact_kernel, in_specs=[SMEM, VMEM, VMEM], out_specs=VME...  5.04 us
    pallas_call x3, Pallas kernels, send(): pl.pallas_call(functools.partial(send_kernel, 1.0 / math.sqrt(depth), [le...  4.58 us
  transfers between devices with their start and end apart: 14, of which 10 were waited for; matrix products, arithmetic and copies ran while one was open for 2% of the time, Pallas kernels for 7%

profile of v7, /device:TPU:6, one launch (start us, length us, event | category | flops | bytes accessed | tf_op | source)
XLA Modules:
  0.0 124.9 jit_solution(1443163723602360539)
XLA Ops:
  0.9 5.0 %compact.5 = bf16[512,128]{1,0:T(8,128)(2,1)} custom-call(s32[2]{0:T(128)S(1)} %pad_add_fusion.2.scalar_ref, s32[12,2048]{1,0:T(8,128)} %sensors_ref.1, bf16[12,64,512]{2,1,0:T(8,128)(2,1)} %temps_ref.1), custom_call_target="tpu_custom_call" | custom-call | tf_op jit(solution)/shard_map/compact/pallas_call | solution.py:74
  6.0 13.8 %all-to-all-start.3 = ((bf16[64,8,128]{2,1,0:T(8,128)(2,1)}), bf16[64,8,128]{2,1,0:T(8,128)(2,1)S(1)}, u32[]{:S(2)}, u32[]{:S(2)}) async-start(bf16[64,8,128]{2,1,0:T(8,128)(2,1)} %bitcast.9), calls=%async_computation.3 | async-start | bytes 262144 | tf_op jit(solution)/shard_map/all_to_all | solution.py:293
  19.8 4.3 %collective-permute-start = (bf16[768,512]{1,0:T(8,128)(2,1)}, bf16[768,512]{1,0:T(8,128)(2,1)S(1)}, u32[]{:S(2)}, u32[]{:S(2)}) collective-permute-start(bf16[768,512]{1,0:T(8,128)(2,1)} %bitcast.20), channel_id=1, source_target_pairs={{0,4},{2,6},{4,8},{6,10},{8,12},{10,14},{12,0},{14,2},{1,5},{3,7},... | collective-permute-start | bytes 2359304 | tf_op jit(solution)/shard_map/ppermute | solution.py:269
  24.1 3.7 %collective-permute-start.1 = (bf16[768,512]{1,0:T(8,128)(2,1)}, bf16[768,512]{1,0:T(8,128)(2,1)S(1)}, u32[]{:S(2)}, u32[]{:S(2)}) collective-permute-start(bf16[768,512]{1,0:T(8,128)(2,1)} %bitcast.21), channel_id=1, source_target_pairs={{0,12},{2,14},{4,0},{6,2},{8,4},{10,6},{12,8},{14,10},{1,13},{3,15... | collective-permute-start | bytes 2359304 | tf_op jit(solution)/shard_map/ppermute | solution.py:269
  27.9 1.0 all-to-all-done.3.lists_ref
  29.0 1.5 %expand.5 = bf16[32,768]{1,0:T(8,128)(2,1)S(1)} custom-call(s32[2]{0:T(128)S(1)} %pad_add_fusion.3.scalar_ref, s32[12,32]{1,0:T(8,128)S(1)} %copy.5.rows_ref, s32[32,12]{1,0:T(8,128)S(1)} %bitcast.26, bf16[64,8,128]{2,1,0:T(8,128)(2,1)S(1)} %all-to-all-done.3.lists_ref), custom_call_target="tpu_custom_call" | custom-call | tf_op jit(solution)/shard_map/expand/pallas_call | solution.py:111
  31.1 7.1 %all-to-all-start.4 = ((bf16[8,4,768]{2,1,0:T(4,128)(2,1)}), bf16[8,4,768]{2,1,0:T(4,128)(2,1)S(1)}, u32[]{:S(2)}, u32[]{:S(2)}) async-start(bf16[8,4,768]{2,1,0:T(4,128)(2,1)} %reshape.35), calls=%async_computation.4 | async-start | bytes 98304 | tf_op jit(solution)/shard_map/all_to_all | solution.py:299
  38.2 3.1 %collective-permute-start.2 = (bf16[768,512]{1,0:T(8,128)(2,1)}, bf16[768,512]{1,0:T(8,128)(2,1)S(1)}, u32[]{:S(2)}, u32[]{:S(2)}) collective-permute-start(bf16[768,512]{1,0:T(8,128)(2,1)} %bitcast.22), channel_id=1, source_target_pairs={{0,2},{2,4},{4,6},{6,8},{8,10},{10,12},{12,14},{14,0},{1,3},{3,5},... | collective-permute-start | bytes 2359304 | tf_op jit(solution)/shard_map/ppermute | solution.py:269
  41.3 4.0 %collective-permute-start.3 = (bf16[768,512]{1,0:T(8,128)(2,1)}, bf16[768,512]{1,0:T(8,128)(2,1)S(1)}, u32[]{:S(2)}, u32[]{:S(2)}) collective-permute-start(bf16[768,512]{1,0:T(8,128)(2,1)} %bitcast.23), channel_id=1, source_target_pairs={{0,14},{2,0},{4,2},{6,4},{8,6},{10,8},{12,10},{14,12},{1,15},{3,1}... | collective-permute-start | bytes 2359304 | tf_op jit(solution)/shard_map/ppermute | solution.py:269
  45.2 1.1 all-to-all-done.4
  46.4 0.9 broadcast_in_dim.7
  47.3 10.1 %all-to-all-start.5 = ((bf16[64,4,768]{2,1,0:T(4,128)(2,1)}), bf16[64,4,768]{2,1,0:T(4,128)(2,1)S(1)}, u32[]{:S(2)}, u32[]{:S(2)}) async-start(bf16[64,4,768]{2,1,0:T(4,128)(2,1)} %broadcast_in_dim.7), calls=%async_computation.5 | async-start | bytes 786432 | tf_op jit(solution)/shard_map/all_to_all | solution.py:304
  57.5 7.2 %collective-permute-done.1.rest_4_ = bf16[768,512]{1,0:T(8,128)(2,1)S(1)} collective-permute-done((bf16[768,512]{1,0:T(8,128)(2,1)}, bf16[768,512]{1,0:T(8,128)(2,1)S(1)}, u32[]{:S(2)}, u32[]{:S(2)}) %collective-permute-start.1) | collective-permute-done | bytes 786464 | tf_op jit(solution)/shard_map/ppermute | solution.py:269
  64.6 3.8 %longest.1 = s32[1,1]{1,0:T(1,128)} custom-call(s32[12,2048]{1,0:T(8,128)} %sensors_ref.1), custom_call_target="tpu_custom_call" | custom-call | flops 1258291200 | bytes 98304 | tf_op jit(solution)/shard_map/longest/pallas_call | solution.py:141
  69.0 1.9 %collective-permute-start.5 = (bf16[768,512]{1,0:T(8,128)(2,1)S(1)}, bf16[768,512]{1,0:T(8,128)(2,1)}, u32[]{:S(2)}, u32[]{:S(2)}) collective-permute-start(bf16[768,512]{1,0:T(8,128)(2,1)S(1)} %collective-permute-done.rest_3_), channel_id=1, source_target_pairs={{0,2},{2,4},{4,6},{6,8},{8,10},{10,12},{12,14},{14,0},{1,3},{3,5},... | collective-permute-start | bytes 2359304 | tf_op jit(solution)/shard_map/ppermute | solution.py:269
  71.0 5.1 %collective-permute-start.6 = (bf16[768,512]{1,0:T(8,128)(2,1)S(1)}, bf16[768,512]{1,0:T(8,128)(2,1)}, u32[]{:S(2)}, u32[]{:S(2)}) collective-permute-start(bf16[768,512]{1,0:T(8,128)(2,1)S(1)} %collective-permute-done.1.rest_4_), channel_id=1, source_target_pairs={{0,14},{2,0},{4,2},{6,4},{8,6},{10,8},{12,10},{14,12},{1,15},{3,1}... | collective-permute-start | bytes 2359304 | tf_op jit(solution)/shard_map/ppermute | solution.py:269
  76.1 0.8 reshape.36
  77.7 3.7 %collective-permute-done.3.rest_2_ = bf16[768,512]{1,0:T(8,128)(2,1)S(1)} collective-permute-done((bf16[768,512]{1,0:T(8,128)(2,1)}, bf16[768,512]{1,0:T(8,128)(2,1)S(1)}, u32[]{:S(2)}, u32[]{:S(2)}) %collective-permute-start.3) | collective-permute-done | bytes 786464 | tf_op jit(solution)/shard_map/ppermute | solution.py:269
  81.4 2.0 %send.3 = bf16[5,128,512]{2,1,0:T(8,128)(2,1)S(1)} custom-call(s32[2]{0:T(128)S(1)} %pad_add_fusion.4.scalar_ref, bf16[256,768]{1,0:T(8,128)(2,1)} %get-tuple-element.117.readings_ref, bf16[768,512]{1,0:T(8,128)(2,1)} %bitcast.24, bf16[768,512]{1,0:T(8,128)(2,1)S(1)} %collective-permute-done.2.rest_1_, bf16[768,512]{1,0:T(8,128)(2,1)S(1)} %collective-permute-done.3.rest_2_, ...), custom_call_target="tpu_custom_call" | custom-call | flops 503316480 | bytes 3932160 | tf_op jit(solution)/shard_map/send/pallas_call | solution.py:225
  83.4 2.8 %collective-permute-start.4 = (bf16[5,128,512]{2,1,0:T(8,128)(2,1)S(1)}, bf16[5,128,512]{2,1,0:T(8,128)(2,1)S(1)}, u32[]{:S(2)}, u32[]{:S(2)}) collective-permute-start(bf16[5,128,512]{2,1,0:T(8,128)(2,1)S(1)} %send.3), channel_id=1, source_target_pairs={{0,1},{1,0},{2,3},{3,2},{4,5},{5,4},{6,7},{7,6},{8,9},{9,8},{10,11... | collective-permute-start | bytes 1966088 | tf_op jit(solution)/shard_map/ppermute | solution.py:328
  86.3 3.5 %collective-permute-start.8 = (bf16[384,512]{1,0:T(8,128)(2,1)S(1)}, bf16[384,512]{1,0:T(8,128)(2,1)S(1)}, u32[]{:S(2)}, u32[]{:S(2)}) collective-permute-start(bf16[384,512]{1,0:T(8,128)(2,1)S(1)} %slice.6), channel_id=1, source_target_pairs={{0,4},{2,6},{4,8},{6,10},{8,12},{10,14},{12,0},{14,2},{1,5},{3,7},... | collective-permute-start | bytes 1179656 | tf_op jit(solution)/shard_map/ppermute | solution.py:269
  89.8 4.6 %collective-permute-start.9 = (bf16[384,512]{1,0:T(8,128)(2,1)S(1)}, bf16[384,512]{1,0:T(8,128)(2,1)S(1)}, u32[]{:S(2)}, u32[]{:S(2)}) collective-permute-start(bf16[384,512]{1,0:T(8,128)(2,1)S(1)} %slice.7), channel_id=1, source_target_pairs={{0,12},{2,14},{4,0},{6,2},{8,4},{10,6},{12,8},{14,10},{1,13},{3,15... | collective-permute-start | bytes 1179656 | tf_op jit(solution)/shard_map/ppermute | solution.py:269
  95.1 3.2 %collective-permute-done.6.rest_1_.rest_6_ = bf16[768,512]{1,0:T(8,128)(2,1)} collective-permute-done((bf16[768,512]{1,0:T(8,128)(2,1)S(1)}, bf16[768,512]{1,0:T(8,128)(2,1)}, u32[]{:S(2)}, u32[]{:S(2)}) %collective-permute-start.6) | collective-permute-done | bytes 786464 | tf_op jit(solution)/shard_map/ppermute | solution.py:269
  98.4 1.8 %send.4 = bf16[2,128,512]{2,1,0:T(8,128)(2,1)S(1)} custom-call(s32[2]{0:T(128)S(1)} %pad_add_fusion.4.scalar_ref, bf16[256,768]{1,0:T(8,128)(2,1)S(1)} %copy-done.1, bf16[768,512]{1,0:T(8,128)(2,1)} %collective-permute-done.5.rest_0_.rest_5_, bf16[768,512]{1,0:T(8,128)(2,1)} %collective-permute-done.6.rest_1_.rest_6_), custom_call_target="tpu_custom_call" | custom-call | flops 201326592 | bytes 1572864 | tf_op jit(solution)/shard_map/send/pallas_call | solution.py:225
  100.1 2.8 %collective-permute-start.7 = (bf16[2,128,512]{2,1,0:T(8,128)(2,1)S(1)}, bf16[2,128,512]{2,1,0:T(8,128)(2,1)S(1)}, u32[]{:S(2)}, u32[]{:S(2)}) collective-permute-start(bf16[2,128,512]{2,1,0:T(8,128)(2,1)S(1)} %send.4), channel_id=1, source_target_pairs={{0,1},{1,0},{2,3},{3,2},{4,5},{5,4},{6,7},{7,6},{8,9},{9,8},{10,11... | collective-permute-start | bytes 786440 | tf_op jit(solution)/shard_map/ppermute | solution.py:328
  102.9 3.3 %collective-permute-done.8.rest_0_.rest_7_ = bf16[384,512]{1,0:T(8,128)(2,1)S(1)} collective-permute-done((bf16[384,512]{1,0:T(8,128)(2,1)S(1)}, bf16[384,512]{1,0:T(8,128)(2,1)S(1)}, u32[]{:S(2)}, u32[]{:S(2)}) %collective-permute-start.8) | collective-permute-done | bytes 393248 | tf_op jit(solution)/shard_map/ppermute | solution.py:269
  106.2 8.8 %collective-permute-done.9.rest_1_.rest_8_ = bf16[384,512]{1,0:T(8,128)(2,1)S(1)} collective-permute-done((bf16[384,512]{1,0:T(8,128)(2,1)S(1)}, bf16[384,512]{1,0:T(8,128)(2,1)S(1)}, u32[]{:S(2)}, u32[]{:S(2)}) %collective-permute-start.9) | collective-permute-done | bytes 393248 | tf_op jit(solution)/shard_map/ppermute | solution.py:269
  115.1 0.8 send.5
  115.9 2.7 %collective-permute-start.10 = (bf16[1,128,512]{2,1,0:T(8,128)(2,1)S(1)}, bf16[1,128,512]{2,1,0:T(8,128)(2,1)S(1)}, u32[]{:S(2)}, u32[]{:S(2)}) collective-permute-start(bf16[1,128,512]{2,1,0:T(8,128)(2,1)S(1)} %send.5), channel_id=1, source_target_pairs={{0,1},{1,0},{2,3},{3,2},{4,5},{5,4},{6,7},{7,6},{8,9},{9,8},{10,11... | collective-permute-start | bytes 393224 | tf_op jit(solution)/shard_map/ppermute | solution.py:328
  118.7 3.1 %keep.1.rest_3_ = bf16[128,8192]{1,0:T(8,128)(2,1)} custom-call(s32[2]{0:T(128)S(1)} %pad_add_fusion.4.scalar_ref, bf16[256,768]{1,0:T(8,128)(2,1)S(1)} %copy-done.1, bf16[768,512]{1,0:T(8,128)(2,1)S(1)} %bitcast.25, bf16[768,512]{1,0:T(8,128)(2,1)S(1)} %collective-permute-done.2.rest_1_, bf16[768,512]{1,0:T(8,128)(2,1)S(1)} %collective-permute-done.3.rest_2_, ...), custom_call_target="tpu_custom_call" | custom-call | flops 805306368 | bytes 6291456 | tf_op jit(solution)/shard_map/keep/pallas_call | solution.py:240
  121.8 1.4 %collective-permute-done.10.rest_2_ = bf16[1,128,512]{2,1,0:T(8,128)(2,1)S(1)} collective-permute-done((bf16[1,128,512]{2,1,0:T(8,128)(2,1)S(1)}, bf16[1,128,512]{2,1,0:T(8,128)(2,1)S(1)}, u32[]{:S(2)}, u32[]{:S(2)}) %collective-permute-start.10) | collective-permute-done | bytes 131104 | tf_op jit(solution)/shard_map/ppermute | solution.py:328
  123.2 1.6 %place.1 = bf16[128,8192]{1,0:T(8,128)(2,1)} custom-call(s32[2]{0:T(128)S(1)} %pad_add_fusion.4.scalar_ref, bf16[5,128,512]{2,1,0:T(8,128)(2,1)S(1)} %collective-permute-done.4.rest_0_, bf16[2,128,512]{2,1,0:T(8,128)(2,1)S(1)} %collective-permute-done.7.rest_1_, ...), custom_call_target="tpu_custom_call", output_to_operand_aliasing={{}: (4, {})} | custom-call | tf_op jit(solution)/shard_map/place/pallas_call | solution.py:255
  (23 shorter events, 3.5 us)
Async XLA Ops:
  0.9 30.2 %copy-start.2 = (s32[12,32]{0,1:T(8,128)}, s32[12,32]{0,1:T(8,128)S(1)}, u32[]{:S(2)}) copy-start(s32[12,32]{0,1:T(8,128)S(1)} %copy.7) | copy-start | bytes 4612
  6.0 23.0 %all-to-all-start.3 = ((bf16[64,8,128]{2,1,0:T(8,128)(2,1)}), bf16[64,8,128]{2,1,0:T(8,128)(2,1)S(1)}, u32[]{:S(2)}, u32[]{:S(2)}) async-start(bf16[64,8,128]{2,1,0:T(8,128)(2,1)} %bitcast.9), calls=%async_computation.3 | async-start | bytes 262144 | tf_op jit(solution)/shard_map/all_to_all | solution.py:293
  19.8 37.7 %collective-permute-start = (bf16[768,512]{1,0:T(8,128)(2,1)}, bf16[768,512]{1,0:T(8,128)(2,1)S(1)}, u32[]{:S(2)}, u32[]{:S(2)}) collective-permute-start(bf16[768,512]{1,0:T(8,128)(2,1)} %bitcast.20), channel_id=1, source_target_pairs={{0,4},{2,6},{4,8},{6,10},{8,12},{10,14},{12,0},{14,2},{1,5},{3,7},... | collective-permute-start | bytes 2359304 | tf_op jit(solution)/shard_map/ppermute | solution.py:269
  24.1 40.5 %collective-permute-start.1 = (bf16[768,512]{1,0:T(8,128)(2,1)}, bf16[768,512]{1,0:T(8,128)(2,1)S(1)}, u32[]{:S(2)}, u32[]{:S(2)}) collective-permute-start(bf16[768,512]{1,0:T(8,128)(2,1)} %bitcast.21), channel_id=1, source_target_pairs={{0,12},{2,14},{4,0},{6,2},{8,4},{10,6},{12,8},{14,10},{1,13},{3,15... | collective-permute-start | bytes 2359304 | tf_op jit(solution)/shard_map/ppermute | solution.py:269
  31.1 15.3 %all-to-all-start.4 = ((bf16[8,4,768]{2,1,0:T(4,128)(2,1)}), bf16[8,4,768]{2,1,0:T(4,128)(2,1)S(1)}, u32[]{:S(2)}, u32[]{:S(2)}) async-start(bf16[8,4,768]{2,1,0:T(4,128)(2,1)} %reshape.35), calls=%async_computation.4 | async-start | bytes 98304 | tf_op jit(solution)/shard_map/all_to_all | solution.py:299
  38.2 39.6 %collective-permute-start.2 = (bf16[768,512]{1,0:T(8,128)(2,1)}, bf16[768,512]{1,0:T(8,128)(2,1)S(1)}, u32[]{:S(2)}, u32[]{:S(2)}) collective-permute-start(bf16[768,512]{1,0:T(8,128)(2,1)} %bitcast.22), channel_id=1, source_target_pairs={{0,2},{2,4},{4,6},{6,8},{8,10},{10,12},{12,14},{14,0},{1,3},{3,5},... | collective-permute-start | bytes 2359304 | tf_op jit(solution)/shard_map/ppermute | solution.py:269
  41.3 40.1 %collective-permute-start.3 = (bf16[768,512]{1,0:T(8,128)(2,1)}, bf16[768,512]{1,0:T(8,128)(2,1)S(1)}, u32[]{:S(2)}, u32[]{:S(2)}) collective-permute-start(bf16[768,512]{1,0:T(8,128)(2,1)} %bitcast.23), channel_id=1, source_target_pairs={{0,14},{2,0},{4,2},{6,4},{8,6},{10,8},{12,10},{14,12},{1,15},{3,1}... | collective-permute-start | bytes 2359304 | tf_op jit(solution)/shard_map/ppermute | solution.py:269
  47.3 28.9 %all-to-all-start.5 = ((bf16[64,4,768]{2,1,0:T(4,128)(2,1)}), bf16[64,4,768]{2,1,0:T(4,128)(2,1)S(1)}, u32[]{:S(2)}, u32[]{:S(2)}) async-start(bf16[64,4,768]{2,1,0:T(4,128)(2,1)} %broadcast_in_dim.7), calls=%async_computation.5 | async-start | bytes 786432 | tf_op jit(solution)/shard_map/all_to_all | solution.py:304
  69.0 26.1 %collective-permute-start.5 = (bf16[768,512]{1,0:T(8,128)(2,1)S(1)}, bf16[768,512]{1,0:T(8,128)(2,1)}, u32[]{:S(2)}, u32[]{:S(2)}) collective-permute-start(bf16[768,512]{1,0:T(8,128)(2,1)S(1)} %collective-permute-done.rest_3_), channel_id=1, source_target_pairs={{0,2},{2,4},{4,6},{6,8},{8,10},{10,12},{12,14},{14,0},{1,3},{3,5},... | collective-permute-start | bytes 2359304 | tf_op jit(solution)/shard_map/ppermute | solution.py:269
  71.0 27.4 %collective-permute-start.6 = (bf16[768,512]{1,0:T(8,128)(2,1)S(1)}, bf16[768,512]{1,0:T(8,128)(2,1)}, u32[]{:S(2)}, u32[]{:S(2)}) collective-permute-start(bf16[768,512]{1,0:T(8,128)(2,1)S(1)} %collective-permute-done.1.rest_4_), channel_id=1, source_target_pairs={{0,14},{2,0},{4,2},{6,4},{8,6},{10,8},{12,10},{14,12},{1,15},{3,1}... | collective-permute-start | bytes 2359304 | tf_op jit(solution)/shard_map/ppermute | solution.py:269
  81.4 17.0 %copy-start.1 = (bf16[256,768]{1,0:T(8,128)(2,1)S(1)}, bf16[256,768]{1,0:T(8,128)(2,1)}, u32[]{:S(2)}) copy-start(bf16[256,768]{1,0:T(8,128)(2,1)} %get-tuple-element.117.readings_ref) | copy-start | bytes 1179652
  83.4 39.8 %collective-permute-start.4 = (bf16[5,128,512]{2,1,0:T(8,128)(2,1)S(1)}, bf16[5,128,512]{2,1,0:T(8,128)(2,1)S(1)}, u32[]{:S(2)}, u32[]{:S(2)}) collective-permute-start(bf16[5,128,512]{2,1,0:T(8,128)(2,1)S(1)} %send.3), channel_id=1, source_target_pairs={{0,1},{1,0},{2,3},{3,2},{4,5},{5,4},{6,7},{7,6},{8,9},{9,8},{10,11... | collective-permute-start | bytes 1966088 | tf_op jit(solution)/shard_map/ppermute | solution.py:328
  86.2 32.4 %copy-start = (bf16[12,64,512]{2,1,0:T(8,128)(2,1)S(1)}, bf16[12,64,512]{2,1,0:T(8,128)(2,1)}, u32[]{:S(2)}) copy-start(bf16[12,64,512]{2,1,0:T(8,128)(2,1)} %get-tuple-element.253) | copy-start | bytes 2359300
  86.3 19.9 %collective-permute-start.8 = (bf16[384,512]{1,0:T(8,128)(2,1)S(1)}, bf16[384,512]{1,0:T(8,128)(2,1)S(1)}, u32[]{:S(2)}, u32[]{:S(2)}) collective-permute-start(bf16[384,512]{1,0:T(8,128)(2,1)S(1)} %slice.6), channel_id=1, source_target_pairs={{0,4},{2,6},{4,8},{6,10},{8,12},{10,14},{12,0},{14,2},{1,5},{3,7},... | collective-permute-start | bytes 1179656 | tf_op jit(solution)/shard_map/ppermute | solution.py:269
  89.8 25.3 %collective-permute-start.9 = (bf16[384,512]{1,0:T(8,128)(2,1)S(1)}, bf16[384,512]{1,0:T(8,128)(2,1)S(1)}, u32[]{:S(2)}, u32[]{:S(2)}) collective-permute-start(bf16[384,512]{1,0:T(8,128)(2,1)S(1)} %slice.7), channel_id=1, source_target_pairs={{0,12},{2,14},{4,0},{6,2},{8,4},{10,6},{12,8},{14,10},{1,13},{3,15... | collective-permute-start | bytes 1179656 | tf_op jit(solution)/shard_map/ppermute | solution.py:269
  100.1 23.0 %collective-permute-start.7 = (bf16[2,128,512]{2,1,0:T(8,128)(2,1)S(1)}, bf16[2,128,512]{2,1,0:T(8,128)(2,1)S(1)}, u32[]{:S(2)}, u32[]{:S(2)}) collective-permute-start(bf16[2,128,512]{2,1,0:T(8,128)(2,1)S(1)} %send.4), channel_id=1, source_target_pairs={{0,1},{1,0},{2,3},{3,2},{4,5},{5,4},{6,7},{7,6},{8,9},{9,8},{10,11... | collective-permute-start | bytes 786440 | tf_op jit(solution)/shard_map/ppermute | solution.py:328
  115.9 7.3 %collective-permute-start.10 = (bf16[1,128,512]{2,1,0:T(8,128)(2,1)S(1)}, bf16[1,128,512]{2,1,0:T(8,128)(2,1)S(1)}, u32[]{:S(2)}, u32[]{:S(2)}) collective-permute-start(bf16[1,128,512]{2,1,0:T(8,128)(2,1)S(1)} %send.5), channel_id=1, source_target_pairs={{0,1},{1,0},{2,3},{3,2},{4,5},{5,4},{6,7},{7,6},{8,9},{9,8},{10,11... | collective-permute-start | bytes 393224 | tf_op jit(solution)/shard_map/ppermute | solution.py:328

commit v8 on v6

--- a/solution.py
+++ b/solution.py
@@ -144,7 +144,7 @@
         out_specs=SMEM,
         out_shape=jax.ShapeDtypeStruct((1, 1), jnp.int32),
         cost_estimate=pl.CostEstimate(
-            flops=2 * sensors.size * devices, bytes_accessed=4 * sensors.size, transcendentals=0
+            flops=100 * sensors.size * devices, bytes_accessed=4 * sensors.size, transcendentals=0
         ),
         compiler_params=PARAMS,
         name="longest",
@@ -295,31 +295,22 @@
     def part_of(number, lists):
         return expand(jnp.stack([lax.axis_index("y"), number * SLOTS]), chosen, lists, width)
 
-    def summed_of(part):
-        part = lax.all_to_all(part.reshape(n_y, group // n_y, depth), "y", 0, 0, tiled=True)
-        part = part.astype(F32).sum(axis=0).astype(BF16)
-        return jnp.broadcast_to(part[None], (n_plane, *part.shape))
-
-    def handed_out(part):
-        return lax.all_to_all(part, PLANE, 0, 0, tiled=True).reshape(-1, depth)
-
-    def one_round(number):
-        return handed_out(summed_of(part_of(number, exchanged(listed(number)))))
-
-    part = part_of(jnp.int32(0), exchanged(listed(jnp.int32(0))))
+    lists = listed(jnp.int32(0))
+    seen, _ = lax.optimization_barrier((sensors, lists))
+    rounds = pl.cdiv(longest(seen, group, devices, width), SLOTS)
+    _, part = lax.while_loop(
+        lambda state: state[0] < rounds,
+        lambda state: (state[0] + 1, state[1] + part_of(state[0], exchanged(listed(state[0])))),
+        (jnp.int32(1), part_of(jnp.int32(0), exchanged(lists))),
+    )
     go_on(up, 1, part)
     go_on(down, -1, part)
-    part = summed_of(part)
-    seen, _ = lax.optimization_barrier((sensors, part))
-    rounds = pl.cdiv(longest(seen, group, devices, width), SLOTS)
+    part = lax.all_to_all(part.reshape(n_y, group // n_y, depth), "y", 0, 0, tiled=True)
+    part = part.astype(F32).sum(axis=0).astype(BF16)
     go_on(up, 1, part)
     go_on(down, -1, part)
-    readings = handed_out(part)
-    _, readings = lax.while_loop(
-        lambda state: state[0] < rounds,
-        lambda state: (state[0] + 1, state[1] + one_round(state[0])),
-        (jnp.int32(1), readings),
-    )
+    copies = jnp.broadcast_to(part[None], (n_plane, *part.shape))
+    readings = lax.all_to_all(copies, PLANE, 0, 0, tiled=True).reshape(-1, depth)
 
     here = jnp.stack([z, xl])
 

time: 128 us -> 117 us (0.914); the launches traced: 126 us -> 116 us
  blocking collectives: 0 us -> 15.1 us
  waiting for transfers between devices: 31.1 us -> 19.3 us
  starting transfers between devices: 69.7 us -> 59.1 us
  local copies, waits for them, and re-layouts: 3.86 us -> 2.2 us
    all_to_all x0 -> x1, blocking collectives: none -> 15.1 us  [body(): lax.all_to_all(part.reshape(n_y, group // n_y, depth), 'y', 0, 0, tiled=T...]
    all_to_all x2 -> x1, starting transfers between devices: 17.2 us -> 7.67 us  [body(): lax.all_to_all(copies, PLANE, 0, 0, tiled=True).reshape(-1, depth)]
    ppermute x8, waiting for transfers between devices: 12.2 us -> 7.11 us  [ring(): lax.ppermute(value, 'z', [(i, (i + shift) % size) for i in range(size)])]
    all_to_all x2 -> x1, waiting for transfers between devices: 10.7 us -> 6.83 us  [body(): lax.all_to_all(copies, PLANE, 0, 0, tiled=True).reshape(-1, depth)]
    all_to_all x1, waiting for transfers between devices: 7.6 us -> 4.31 us  [exchanged(): return lax.all_to_all(lists, LISTS, 0, 0, tiled=True)]
  transfers between devices with their start and end apart: 14 -> 13, of which waited for: 8 -> 7; matrix products, arithmetic and copies ran while one was open for 3% -> 2% of each run, Pallas kernels for 11% -> 12%
where the time goes in v8:
time: 117 us; the launch traced here: 116 us
  starting transfers between devices  59.1 us (51%)
  waiting for transfers between devices  19.3 us (16%)
  Pallas kernels  19.1 us (16%)
  blocking collectives  15.1 us (13%)
  local copies, waits for them, and re-layouts  2.2 us (2%)
    ppermute x8, starting transfers between devices, ring(): lax.ppermute(value, 'z', [(i, (i + shift) % size) for i in range(size)])  34.5 us
    all_to_all x1, blocking collectives, body(): lax.all_to_all(part.reshape(n_y, group // n_y, depth), 'y', 0, 0, tiled=T...  15.1 us
    ppermute x3, starting transfers between devices, swapped(): return lax.ppermute(sent, 'xl', [(0, 1), (1, 0)])  9 us
    all_to_all x1, starting transfers between devices, exchanged(): return lax.all_to_all(lists, LISTS, 0, 0, tiled=True)  7.96 us
    all_to_all x1, starting transfers between devices, body(): lax.all_to_all(copies, PLANE, 0, 0, tiled=True).reshape(-1, depth)  7.67 us
    ppermute x8, waiting for transfers between devices, ring(): lax.ppermute(value, 'z', [(i, (i + shift) % size) for i in range(size)])  7.11 us
    all_to_all x1, waiting for transfers between devices, body(): lax.all_to_all(copies, PLANE, 0, 0, tiled=True).reshape(-1, depth)  6.83 us
    pallas_call x1, Pallas kernels, compact(): pl.pallas_call(compact_kernel, in_specs=[SMEM, VMEM, VMEM], out_specs=VME...  5.04 us
  transfers between devices with their start and end apart: 13, of which 7 were waited for; matrix products, arithmetic and copies ran while one was open for 2% of the time, Pallas kernels for 12%

profile of v8, /device:TPU:6, one launch (start us, length us, event | category | flops | bytes accessed | tf_op | source)
XLA Modules:
  0.0 116.3 jit_solution(17008994410236968194)
XLA Ops:
  0.0 4.3 %collective-permute-start = (bf16[768,512]{1,0:T(8,128)(2,1)}, bf16[768,512]{1,0:T(8,128)(2,1)S(1)}, u32[]{:S(2)}, u32[]{:S(2)}) collective-permute-start(bf16[768,512]{1,0:T(8,128)(2,1)} %bitcast.23), channel_id=1, source_target_pairs={{0,2},{2,4},{4,6},{6,8},{8,10},{10,12},{12,14},{14,0},{1,3},{3,5},... | collective-permute-start | bytes 2359304 | tf_op jit(solution)/shard_map/ppermute | solution.py:269
  4.3 8.6 %collective-permute-start.1 = (bf16[768,512]{1,0:T(8,128)(2,1)}, bf16[768,512]{1,0:T(8,128)(2,1)S(1)}, u32[]{:S(2)}, u32[]{:S(2)}) collective-permute-start(bf16[768,512]{1,0:T(8,128)(2,1)} %bitcast.24), channel_id=1, source_target_pairs={{0,14},{2,0},{4,2},{6,4},{8,6},{10,8},{12,10},{14,12},{1,15},{3,1}... | collective-permute-start | bytes 2359304 | tf_op jit(solution)/shard_map/ppermute | solution.py:269
  13.0 5.0 %compact.2 = bf16[512,128]{1,0:T(8,128)(2,1)} custom-call(s32[2]{0:T(128)S(1)} %pad_add_fusion.2.scalar_ref, s32[12,2048]{1,0:T(8,128)} %sensors_ref.2, bf16[12,64,512]{2,1,0:T(8,128)(2,1)} %temps_ref.1), custom_call_target="tpu_custom_call" | custom-call | tf_op jit(solution)/shard_map/compact/pallas_call | solution.py:74
  18.0 8.0 %all-to-all-start.1 = ((bf16[64,8,128]{2,1,0:T(8,128)(2,1)}), bf16[64,8,128]{2,1,0:T(8,128)(2,1)S(1)}, u32[]{:S(2)}, u32[]{:S(2)}) async-start(bf16[64,8,128]{2,1,0:T(8,128)(2,1)} %bitcast.10), calls=%async_computation.1 | async-start | bytes 262144 | tf_op jit(solution)/shard_map/all_to_all | solution.py:291
  26.0 3.8 %longest.1 = s32[1,1]{1,0:T(1,128)} custom-call(s32[12,2048]{1,0:T(8,128)} %sensors_ref.2), custom_call_target="tpu_custom_call" | custom-call | flops 1258291200 | bytes 98304 | tf_op jit(solution)/shard_map/longest/pallas_call | solution.py:141
  30.7 0.1 copy.7
  30.8 4.3 %all-to-all-done.1.lists_ref = bf16[64,8,128]{2,1,0:T(8,128)(2,1)S(1)} async-done(((bf16[64,8,128]{2,1,0:T(8,128)(2,1)}), bf16[64,8,128]{2,1,0:T(8,128)(2,1)S(1)}, u32[]{:S(2)}, u32[]{:S(2)}) %all-to-all-start.1) | async-done | bytes 131104 | tf_op jit(solution)/shard_map/all_to_all | solution.py:291
  35.1 1.5 %expand.2 = bf16[32,768]{1,0:T(8,128)(2,1)S(1)} custom-call(s32[2]{0:T(128)S(1)} %pad_add_fusion.3.scalar_ref, s32[12,32]{1,0:T(8,128)S(1)} %constant_dynamic-slice_fusion.rows_ref, s32[32,12]{1,0:T(8,128)S(1)} %bitcast.27, bf16[64,8,128]{2,1,0:T(8,128)(2,1)S(1)} %all-to-all-done.1.lists_ref), custom_call_target="tpu_custom_call" | custom-call | tf_op jit(solution)/shard_map/expand/pallas_call | solution.py:111
  36.6 4.0 %collective-permute-start.2 = (bf16[768,512]{1,0:T(8,128)(2,1)S(1)}, bf16[768,512]{1,0:T(8,128)(2,1)}, u32[]{:S(2)}, u32[]{:S(2)}) collective-permute-start(bf16[768,512]{1,0:T(8,128)(2,1)S(1)} %collective-permute-done.rest_1_), channel_id=1, source_target_pairs={{0,2},{2,4},{4,6},{6,8},{8,10},{10,12},{12,14},{14,0},{1,3},{3,5},... | collective-permute-start | bytes 2359304 | tf_op jit(solution)/shard_map/ppermute | solution.py:269
  40.7 3.0 %collective-permute-start.3 = (bf16[768,512]{1,0:T(8,128)(2,1)S(1)}, bf16[768,512]{1,0:T(8,128)(2,1)}, u32[]{:S(2)}, u32[]{:S(2)}) collective-permute-start(bf16[768,512]{1,0:T(8,128)(2,1)S(1)} %collective-permute-done.1.rest_2_), channel_id=1, source_target_pairs={{0,14},{2,0},{4,2},{6,4},{8,6},{10,8},{12,10},{14,12},{1,15},{3,1}... | collective-permute-start | bytes 2359304 | tf_op jit(solution)/shard_map/ppermute | solution.py:269
  43.7 15.1 %all_to_all.21 = bf16[8,4,768]{2,1,0:T(4,128)(2,1)S(1)} all-to-all(bf16[8,4,768]{2,1,0:T(4,128)(2,1)S(1)} %reshape.19), channel_id=1, replica_groups=mesh['y'=8,'xh'=2,'core'=2,'z'=8,'xl'=2] {'y'}, dimensions={0} | all-to-all | bytes 98304 | tf_op jit(solution)/shard_map/all_to_all | solution.py:308
  58.9 0.9 broadcast_in_dim.2
  59.7 7.7 %all-to-all-start.3 = ((bf16[64,4,768]{2,1,0:T(4,128)(2,1)}), bf16[64,4,768]{2,1,0:T(4,128)(2,1)}, u32[]{:S(2)}, u32[]{:S(2)}) async-start(bf16[64,4,768]{2,1,0:T(4,128)(2,1)} %broadcast_in_dim.2), calls=%async_computation.3 | async-start | bytes 786432 | tf_op jit(solution)/shard_map/all_to_all | solution.py:313
  67.4 2.0 %collective-permute-start.5 = (bf16[768,512]{1,0:T(8,128)(2,1)}, bf16[768,512]{1,0:T(8,128)(2,1)S(1)}, u32[]{:S(2)}, u32[]{:S(2)}) collective-permute-start(bf16[768,512]{1,0:T(8,128)(2,1)} %collective-permute-done.2.rest_3_), channel_id=1, source_target_pairs={{0,2},{2,4},{4,6},{6,8},{8,10},{10,12},{12,14},{14,0},{1,3},{3,5},... | collective-permute-start | bytes 2359304 | tf_op jit(solution)/shard_map/ppermute | solution.py:269
  69.4 5.0 %collective-permute-start.6 = (bf16[768,512]{1,0:T(8,128)(2,1)}, bf16[768,512]{1,0:T(8,128)(2,1)S(1)}, u32[]{:S(2)}, u32[]{:S(2)}) collective-permute-start(bf16[768,512]{1,0:T(8,128)(2,1)} %collective-permute-done.3.rest_4_), channel_id=1, source_target_pairs={{0,14},{2,0},{4,2},{6,4},{8,6},{10,8},{12,10},{14,12},{1,15},{3,1}... | collective-permute-start | bytes 2359304 | tf_op jit(solution)/shard_map/ppermute | solution.py:269
  74.6 6.8 %all-to-all-done.3 = bf16[64,4,768]{2,1,0:T(4,128)(2,1)} async-done(((bf16[64,4,768]{2,1,0:T(4,128)(2,1)}), bf16[64,4,768]{2,1,0:T(4,128)(2,1)}, u32[]{:S(2)}, u32[]{:S(2)}) %all-to-all-start.3) | async-done | bytes 393248 | tf_op jit(solution)/shard_map/all_to_all | solution.py:313
  81.4 1.1 reshape.20.readings_ref
  82.5 2.3 %send.3 = bf16[5,128,512]{2,1,0:T(8,128)(2,1)S(1)} custom-call(s32[2]{0:T(128)S(1)} %pad_add_fusion.4.scalar_ref, bf16[256,768]{1,0:T(8,128)(2,1)S(1)} %reshape.20.readings_ref, bf16[768,512]{1,0:T(8,128)(2,1)} %bitcast.25, bf16[768,512]{1,0:T(8,128)(2,1)S(1)} %collective-permute-done.rest_1_, bf16[768,512]{1,0:T(8,128)(2,1)S(1)} %collective-permute-done.1.rest_2_, ...), custom_call_target="tpu_custom_call" | custom-call | flops 503316480 | bytes 3932160 | tf_op jit(solution)/shard_map/send/pallas_call | solution.py:225
  84.8 3.7 %collective-permute-start.4 = (bf16[5,128,512]{2,1,0:T(8,128)(2,1)S(1)}, bf16[5,128,512]{2,1,0:T(8,128)(2,1)S(1)}, u32[]{:S(2)}, u32[]{:S(2)}) collective-permute-start(bf16[5,128,512]{2,1,0:T(8,128)(2,1)S(1)} %send.3), channel_id=1, source_target_pairs={{0,1},{1,0},{2,3},{3,2},{4,5},{5,4},{6,7},{7,6},{8,9},{9,8},{10,11... | collective-permute-start | bytes 1966088 | tf_op jit(solution)/shard_map/ppermute | solution.py:318
  88.5 1.8 %collective-permute-done.5.rest_0_.rest_5_ = bf16[768,512]{1,0:T(8,128)(2,1)S(1)} collective-permute-done((bf16[768,512]{1,0:T(8,128)(2,1)}, bf16[768,512]{1,0:T(8,128)(2,1)S(1)}, u32[]{:S(2)}, u32[]{:S(2)}) %collective-permute-start.5) | collective-permute-done | bytes 786464 | tf_op jit(solution)/shard_map/ppermute | solution.py:269
  90.3 1.3 %collective-permute-done.6.rest_1_.rest_6_ = bf16[768,512]{1,0:T(8,128)(2,1)S(1)} collective-permute-done((bf16[768,512]{1,0:T(8,128)(2,1)}, bf16[768,512]{1,0:T(8,128)(2,1)S(1)}, u32[]{:S(2)}, u32[]{:S(2)}) %collective-permute-start.6) | collective-permute-done | bytes 786464 | tf_op jit(solution)/shard_map/ppermute | solution.py:269
  91.7 2.4 %collective-permute-start.8 = (bf16[384,512]{1,0:T(8,128)(2,1)S(1)}, bf16[384,512]{1,0:T(8,128)(2,1)S(1)}, u32[]{:S(2)}, u32[]{:S(2)}) collective-permute-start(bf16[384,512]{1,0:T(8,128)(2,1)S(1)} %slice.6), channel_id=1, source_target_pairs={{0,2},{2,4},{4,6},{6,8},{8,10},{10,12},{12,14},{14,0},{1,3},{3,5},... | collective-permute-start | bytes 1179656 | tf_op jit(solution)/shard_map/ppermute | solution.py:269
  94.1 5.2 %collective-permute-start.9 = (bf16[384,512]{1,0:T(8,128)(2,1)S(1)}, bf16[384,512]{1,0:T(8,128)(2,1)S(1)}, u32[]{:S(2)}, u32[]{:S(2)}) collective-permute-start(bf16[384,512]{1,0:T(8,128)(2,1)S(1)} %slice.7), channel_id=1, source_target_pairs={{0,14},{2,0},{4,2},{6,4},{8,6},{10,8},{12,10},{14,12},{1,15},{3,1}... | collective-permute-start | bytes 1179656 | tf_op jit(solution)/shard_map/ppermute | solution.py:269
  99.3 0.9 send.4
  100.2 2.7 %collective-permute-start.7 = (bf16[2,128,512]{2,1,0:T(8,128)(2,1)S(1)}, bf16[2,128,512]{2,1,0:T(8,128)(2,1)S(1)}, u32[]{:S(2)}, u32[]{:S(2)}) collective-permute-start(bf16[2,128,512]{2,1,0:T(8,128)(2,1)S(1)} %send.4), channel_id=1, source_target_pairs={{0,1},{1,0},{2,3},{3,2},{4,5},{5,4},{6,7},{7,6},{8,9},{9,8},{10,11... | collective-permute-start | bytes 786440 | tf_op jit(solution)/shard_map/ppermute | solution.py:318
  102.9 2.7 %collective-permute-done.8.rest_0_.rest_7_ = bf16[384,512]{1,0:T(8,128)(2,1)S(1)} collective-permute-done((bf16[384,512]{1,0:T(8,128)(2,1)S(1)}, bf16[384,512]{1,0:T(8,128)(2,1)S(1)}, u32[]{:S(2)}, u32[]{:S(2)}) %collective-permute-start.8) | collective-permute-done | bytes 393248 | tf_op jit(solution)/shard_map/ppermute | solution.py:269
  105.6 1.2 %collective-permute-done.9.rest_1_.rest_8_ = bf16[384,512]{1,0:T(8,128)(2,1)S(1)} collective-permute-done((bf16[384,512]{1,0:T(8,128)(2,1)S(1)}, bf16[384,512]{1,0:T(8,128)(2,1)S(1)}, u32[]{:S(2)}, u32[]{:S(2)}) %collective-permute-start.9) | collective-permute-done | bytes 393248 | tf_op jit(solution)/shard_map/ppermute | solution.py:269
  106.8 0.8 send.5
  107.7 2.7 %collective-permute-start.10 = (bf16[1,128,512]{2,1,0:T(8,128)(2,1)S(1)}, bf16[1,128,512]{2,1,0:T(8,128)(2,1)S(1)}, u32[]{:S(2)}, u32[]{:S(2)}) collective-permute-start(bf16[1,128,512]{2,1,0:T(8,128)(2,1)S(1)} %send.5), channel_id=1, source_target_pairs={{0,1},{1,0},{2,3},{3,2},{4,5},{5,4},{6,7},{7,6},{8,9},{9,8},{10,11... | collective-permute-start | bytes 393224 | tf_op jit(solution)/shard_map/ppermute | solution.py:318
  110.3 3.1 %keep.1.rest_3_ = bf16[128,8192]{1,0:T(8,128)(2,1)} custom-call(s32[2]{0:T(128)S(1)} %pad_add_fusion.4.scalar_ref, bf16[256,768]{1,0:T(8,128)(2,1)S(1)} %reshape.20.readings_ref, bf16[768,512]{1,0:T(8,128)(2,1)S(1)} %bitcast.26, bf16[768,512]{1,0:T(8,128)(2,1)S(1)} %collective-permute-done.rest_1_, bf16[768,512]{1,0:T(8,128)(2,1)S(1)} %collective-permute-done.1.rest_2_, ...), custom_call_target="tpu_custom_call" | custom-call | flops 805306368 | bytes 6291456 | tf_op jit(solution)/shard_map/keep/pallas_call | solution.py:240
  113.5 1.0 collective-permute-done.10.rest_2_
  114.5 1.6 %place.1 = bf16[128,8192]{1,0:T(8,128)(2,1)} custom-call(s32[2]{0:T(128)S(1)} %pad_add_fusion.4.scalar_ref, bf16[5,128,512]{2,1,0:T(8,128)(2,1)S(1)} %collective-permute-done.4.rest_0_, bf16[2,128,512]{2,1,0:T(8,128)(2,1)S(1)} %collective-permute-done.7.rest_1_, ...), custom_call_target="tpu_custom_call", output_to_operand_aliasing={{}: (4, {})} | custom-call | tf_op jit(solution)/shard_map/place/pallas_call | solution.py:255
  (21 shorter events, 0.4 us)
Async XLA Ops:
  0.0 36.6 %collective-permute-start = (bf16[768,512]{1,0:T(8,128)(2,1)}, bf16[768,512]{1,0:T(8,128)(2,1)S(1)}, u32[]{:S(2)}, u32[]{:S(2)}) collective-permute-start(bf16[768,512]{1,0:T(8,128)(2,1)} %bitcast.23), channel_id=1, source_target_pairs={{0,2},{2,4},{4,6},{6,8},{8,10},{10,12},{12,14},{14,0},{1,3},{3,5},... | collective-permute-start | bytes 2359304 | tf_op jit(solution)/shard_map/ppermute | solution.py:269
  4.3 36.4 %collective-permute-start.1 = (bf16[768,512]{1,0:T(8,128)(2,1)}, bf16[768,512]{1,0:T(8,128)(2,1)S(1)}, u32[]{:S(2)}, u32[]{:S(2)}) collective-permute-start(bf16[768,512]{1,0:T(8,128)(2,1)} %bitcast.24), channel_id=1, source_target_pairs={{0,14},{2,0},{4,2},{6,4},{8,6},{10,8},{12,10},{14,12},{1,15},{3,1}... | collective-permute-start | bytes 2359304 | tf_op jit(solution)/shard_map/ppermute | solution.py:269
  18.0 17.1 %all-to-all-start.1 = ((bf16[64,8,128]{2,1,0:T(8,128)(2,1)}), bf16[64,8,128]{2,1,0:T(8,128)(2,1)S(1)}, u32[]{:S(2)}, u32[]{:S(2)}) async-start(bf16[64,8,128]{2,1,0:T(8,128)(2,1)} %bitcast.10), calls=%async_computation.1 | async-start | bytes 262144 | tf_op jit(solution)/shard_map/all_to_all | solution.py:291
  26.0 4.6 %copy-start.2 = (s32[12,2048]{1,0:T(8,128)S(1)}, s32[12,2048]{1,0:T(8,128)}, u32[]{:S(2)}) copy-start(s32[12,2048]{1,0:T(8,128)} %sensors_ref.2) | copy-start | bytes 294916
  26.0 10.6 %copy-start = (bf16[12,64,512]{2,1,0:T(8,128)(2,1)S(1)}, bf16[12,64,512]{2,1,0:T(8,128)(2,1)}, u32[]{:S(2)}) copy-start(bf16[12,64,512]{2,1,0:T(8,128)(2,1)} %temps_ref.1) | copy-start | bytes 2359300
  36.6 30.8 %collective-permute-start.2 = (bf16[768,512]{1,0:T(8,128)(2,1)S(1)}, bf16[768,512]{1,0:T(8,128)(2,1)}, u32[]{:S(2)}, u32[]{:S(2)}) collective-permute-start(bf16[768,512]{1,0:T(8,128)(2,1)S(1)} %collective-permute-done.rest_1_), channel_id=1, source_target_pairs={{0,2},{2,4},{4,6},{6,8},{8,10},{10,12},{12,14},{14,0},{1,3},{3,5},... | collective-permute-start | bytes 2359304 | tf_op jit(solution)/shard_map/ppermute | solution.py:269
  40.7 28.8 %collective-permute-start.3 = (bf16[768,512]{1,0:T(8,128)(2,1)S(1)}, bf16[768,512]{1,0:T(8,128)(2,1)}, u32[]{:S(2)}, u32[]{:S(2)}) collective-permute-start(bf16[768,512]{1,0:T(8,128)(2,1)S(1)} %collective-permute-done.1.rest_2_), channel_id=1, source_target_pairs={{0,14},{2,0},{4,2},{6,4},{8,6},{10,8},{12,10},{14,12},{1,15},{3,1}... | collective-permute-start | bytes 2359304 | tf_op jit(solution)/shard_map/ppermute | solution.py:269
  59.7 21.7 %all-to-all-start.3 = ((bf16[64,4,768]{2,1,0:T(4,128)(2,1)}), bf16[64,4,768]{2,1,0:T(4,128)(2,1)}, u32[]{:S(2)}, u32[]{:S(2)}) async-start(bf16[64,4,768]{2,1,0:T(4,128)(2,1)} %broadcast_in_dim.2), calls=%async_computation.3 | async-start | bytes 786432 | tf_op jit(solution)/shard_map/all_to_all | solution.py:313
  67.4 22.9 %collective-permute-start.5 = (bf16[768,512]{1,0:T(8,128)(2,1)}, bf16[768,512]{1,0:T(8,128)(2,1)S(1)}, u32[]{:S(2)}, u32[]{:S(2)}) collective-permute-start(bf16[768,512]{1,0:T(8,128)(2,1)} %collective-permute-done.2.rest_3_), channel_id=1, source_target_pairs={{0,2},{2,4},{4,6},{6,8},{8,10},{10,12},{12,14},{14,0},{1,3},{3,5},... | collective-permute-start | bytes 2359304 | tf_op jit(solution)/shard_map/ppermute | solution.py:269
  69.4 22.2 %collective-permute-start.6 = (bf16[768,512]{1,0:T(8,128)(2,1)}, bf16[768,512]{1,0:T(8,128)(2,1)S(1)}, u32[]{:S(2)}, u32[]{:S(2)}) collective-permute-start(bf16[768,512]{1,0:T(8,128)(2,1)} %collective-permute-done.3.rest_4_), channel_id=1, source_target_pairs={{0,14},{2,0},{4,2},{6,4},{8,6},{10,8},{12,10},{14,12},{1,15},{3,1}... | collective-permute-start | bytes 2359304 | tf_op jit(solution)/shard_map/ppermute | solution.py:269
  84.8 28.7 %collective-permute-start.4 = (bf16[5,128,512]{2,1,0:T(8,128)(2,1)S(1)}, bf16[5,128,512]{2,1,0:T(8,128)(2,1)S(1)}, u32[]{:S(2)}, u32[]{:S(2)}) collective-permute-start(bf16[5,128,512]{2,1,0:T(8,128)(2,1)S(1)} %send.3), channel_id=1, source_target_pairs={{0,1},{1,0},{2,3},{3,2},{4,5},{5,4},{6,7},{7,6},{8,9},{9,8},{10,11... | collective-permute-start | bytes 1966088 | tf_op jit(solution)/shard_map/ppermute | solution.py:318
  91.7 18.7 %copy-start.1 = (bf16[12,64,512]{2,1,0:T(8,128)(2,1)S(1)}, bf16[12,64,512]{2,1,0:T(8,128)(2,1)}, u32[]{:S(2)}) copy-start(bf16[12,64,512]{2,1,0:T(8,128)(2,1)} %temps_ref.1) | copy-start | bytes 2359300
  91.7 13.9 %collective-permute-start.8 = (bf16[384,512]{1,0:T(8,128)(2,1)S(1)}, bf16[384,512]{1,0:T(8,128)(2,1)S(1)}, u32[]{:S(2)}, u32[]{:S(2)}) collective-permute-start(bf16[384,512]{1,0:T(8,128)(2,1)S(1)} %slice.6), channel_id=1, source_target_pairs={{0,2},{2,4},{4,6},{6,8},{8,10},{10,12},{12,14},{14,0},{1,3},{3,5},... | collective-permute-start | bytes 1179656 | tf_op jit(solution)/shard_map/ppermute | solution.py:269
  94.1 12.7 %collective-permute-start.9 = (bf16[384,512]{1,0:T(8,128)(2,1)S(1)}, bf16[384,512]{1,0:T(8,128)(2,1)S(1)}, u32[]{:S(2)}, u32[]{:S(2)}) collective-permute-start(bf16[384,512]{1,0:T(8,128)(2,1)S(1)} %slice.7), channel_id=1, source_target_pairs={{0,14},{2,0},{4,2},{6,4},{8,6},{10,8},{12,10},{14,12},{1,15},{3,1}... | collective-permute-start | bytes 1179656 | tf_op jit(solution)/shard_map/ppermute | solution.py:269
  100.2 13.3 %collective-permute-start.7 = (bf16[2,128,512]{2,1,0:T(8,128)(2,1)S(1)}, bf16[2,128,512]{2,1,0:T(8,128)(2,1)S(1)}, u32[]{:S(2)}, u32[]{:S(2)}) collective-permute-start(bf16[2,128,512]{2,1,0:T(8,128)(2,1)S(1)} %send.4), channel_id=1, source_target_pairs={{0,1},{1,0},{2,3},{3,2},{4,5},{5,4},{6,7},{7,6},{8,9},{9,8},{10,11... | collective-permute-start | bytes 786440 | tf_op jit(solution)/shard_map/ppermute | solution.py:318
  107.7 6.9 %collective-permute-start.10 = (bf16[1,128,512]{2,1,0:T(8,128)(2,1)S(1)}, bf16[1,128,512]{2,1,0:T(8,128)(2,1)S(1)}, u32[]{:S(2)}, u32[]{:S(2)}) collective-permute-start(bf16[1,128,512]{2,1,0:T(8,128)(2,1)S(1)} %send.5), channel_id=1, source_target_pairs={{0,1},{1,0},{2,3},{3,2},{4,5},{5,4},{6,7},{7,6},{8,9},{9,8},{10,11... | collective-permute-start | bytes 393224 | tf_op jit(solution)/shard_map/ppermute | solution.py:318

commit v9 on v8

--- a/solution.py
+++ b/solution.py
@@ -10,8 +10,9 @@
 from jax.sharding import PartitionSpec as P
 
 AXES = ("y", "xh", "core", "z", "xl")
-LISTS = ("z", "xh", "xl", "core")
-PLANE = ("xh", "xl", "core", "y")
+LISTS = ("z", "y")
+SIDE = ("xh", "xl", "core")
+PLANE = ("y", "xh", "xl", "core")
 SLOTS = 8
 F32, BF16 = jnp.float32, jnp.bfloat16
 PARAMS = pltpu.CompilerParams(vmem_limit_bytes=16 * 2**20)
@@ -84,7 +85,7 @@
 def expand_kernel(shift, scalar_ref, rows_ref, columns_ref, lists_ref, out_ref):
     tiers, group = rows_ref.shape
     n_lists, slots, wide = lists_ref.shape
-    y, start = scalar_ref[0], scalar_ref[1]
+    side, start = scalar_ref[0], scalar_ref[1]
     rows, owners = rows_ref[...] >> shift, columns_ref[...] >> shift
     later = lax.broadcasted_iota(jnp.int32, (group, group), 0) > lax.broadcasted_iota(
         jnp.int32, (group, group), 1
@@ -97,8 +98,8 @@
         same = [(owner == rows[t : t + 1]).astype(F32) for t in range(tier + 1)]
         same[-1] = jnp.where(later, same[-1], 0.0)
         slot = sum(same[1:], same[0]).sum(axis=1, keepdims=True).astype(jnp.int32) - start
-        sender = (owner >> 1 & 7) * 8 + (owner >> 5 & 1) * 4 + (owner & 1) * 2 + (owner >> 4 & 1)
-        there = (owner >> 6 == y) & (slot >= 0) & (slot < slots)
+        sender = (owner >> 1 & 7) * 8 + (owner >> 6)
+        there = (owner & 49 == side) & (slot >= 0) & (slot < slots)
         spot = jnp.where(there, sender * slots + slot, -1)
         found.append(matmul(ones(spot == lanes), lists)[:, : wide // 2])
     for tier in range(0, tiers, 2):
@@ -272,7 +273,7 @@
 def body(temps, sensors):
     tiers, snaps, width = temps.shape
     depth = tiers * snaps
-    n_z, n_y, n_lists, n_plane, devices = (lax.axis_size(a) for a in ("z", "y", LISTS, PLANE, AXES))
+    n_side, n_lists, n_plane, devices = (lax.axis_size(a) for a in (SIDE, LISTS, PLANE, AXES))
     group = sensors.shape[1] // n_lists
     z, xl = lax.axis_index("z"), lax.axis_index("xl")
 
@@ -284,6 +285,7 @@
         blocks.append(ring(block, shift))
 
     first = lax.axis_index(AXES) * width
+    side = lax.axis_index("xh") * 32 + lax.axis_index("core") * 16 + xl
     def listed(number):
         return compact(jnp.stack([first, number * SLOTS]), sensors, temps, n_lists)
 
@@ -293,7 +295,7 @@
     chosen = lax.dynamic_slice_in_dim(sensors, lax.axis_index(LISTS) * group, group, axis=1)
 
     def part_of(number, lists):
-        return expand(jnp.stack([lax.axis_index("y"), number * SLOTS]), chosen, lists, width)
+        return expand(jnp.stack([side, number * SLOTS]), chosen, lists, width)
 
     lists = listed(jnp.int32(0))
     seen, _ = lax.optimization_barrier((sensors, lists))
@@ -305,7 +307,7 @@
     )
     go_on(up, 1, part)
     go_on(down, -1, part)
-    part = lax.all_to_all(part.reshape(n_y, group // n_y, depth), "y", 0, 0, tiled=True)
+    part = lax.all_to_all(part.reshape(n_side, group // n_side, depth), SIDE, 0, 0, tiled=True)
     part = part.astype(F32).sum(axis=0).astype(BF16)
     go_on(up, 1, part)
     go_on(down, -1, part)

time: 117 us -> 116 us (level)
  blocking collectives: 15.1 us -> 8.05 us
  waiting for transfers between devices: 19.3 us -> 23.6 us
  starting transfers between devices: 59.1 us -> 60.6 us
    all_to_all x1, blocking collectives: 15.1 us -> 8.05 us  [body(): lax.all_to_all(part.reshape(n_side, group // n_side, depth), SIDE, 0, 0,...]
    all_to_all x1, waiting for transfers between devices: 4.31 us -> 7.92 us  [exchanged(): return lax.all_to_all(lists, LISTS, 0, 0, tiled=True)]
    all_to_all x1, starting transfers between devices: 7.96 us -> 10.7 us  [exchanged(): return lax.all_to_all(lists, LISTS, 0, 0, tiled=True)]
where the time goes in v9:
time: 116 us; the launch traced here: 115 us
  starting transfers between devices  60.6 us (52%)
  waiting for transfers between devices  23.6 us (20%)
  Pallas kernels  19.1 us (16%)
  blocking collectives  8.05 us (7%)
  local copies, waits for them, and re-layouts  2.2 us (2%)
    ppermute x8, starting transfers between devices, ring(): lax.ppermute(value, 'z', [(i, (i + shift) % size) for i in range(size)])  34.5 us
    all_to_all x1, starting transfers between devices, exchanged(): return lax.all_to_all(lists, LISTS, 0, 0, tiled=True)  10.7 us
    ppermute x3, starting transfers between devices, swapped(): return lax.ppermute(sent, 'xl', [(0, 1), (1, 0)])  8.24 us
    all_to_all x1, blocking collectives, body(): lax.all_to_all(part.reshape(n_side, group // n_side, depth), SIDE, 0, 0,...  8.05 us
    all_to_all x1, waiting for transfers between devices, exchanged(): return lax.all_to_all(lists, LISTS, 0, 0, tiled=True)  7.92 us
    all_to_all x1, waiting for transfers between devices, body(): lax.all_to_all(copies, PLANE, 0, 0, tiled=True).reshape(-1, depth)  7.62 us
    ppermute x8, waiting for transfers between devices, ring(): lax.ppermute(value, 'z', [(i, (i + shift) % size) for i in range(size)])  7.13 us
    all_to_all x1, starting transfers between devices, body(): lax.all_to_all(copies, PLANE, 0, 0, tiled=True).reshape(-1, depth)  7.1 us
  transfers between devices with their start and end apart: 13, of which 7 were waited for; matrix products, arithmetic and copies ran while one was open for 2% of the time, Pallas kernels for 12%

profile of v9, /device:TPU:6, one launch (start us, length us, event | category | flops | bytes accessed | tf_op | source)
XLA Modules:
  0.0 115.0 jit_solution(14399491090994168250)
XLA Ops:
  0.0 4.3 %collective-permute-start = (bf16[768,512]{1,0:T(8,128)(2,1)}, bf16[768,512]{1,0:T(8,128)(2,1)S(1)}, u32[]{:S(2)}, u32[]{:S(2)}) collective-permute-start(bf16[768,512]{1,0:T(8,128)(2,1)} %bitcast.23), channel_id=1, source_target_pairs={{0,2},{2,4},{4,6},{6,8},{8,10},{10,12},{12,14},{14,0},{1,3},{3,5},... | collective-permute-start | bytes 2359304 | tf_op jit(solution)/shard_map/ppermute | solution.py:270
  4.3 8.6 %collective-permute-start.1 = (bf16[768,512]{1,0:T(8,128)(2,1)}, bf16[768,512]{1,0:T(8,128)(2,1)S(1)}, u32[]{:S(2)}, u32[]{:S(2)}) collective-permute-start(bf16[768,512]{1,0:T(8,128)(2,1)} %bitcast.24), channel_id=1, source_target_pairs={{0,14},{2,0},{4,2},{6,4},{8,6},{10,8},{12,10},{14,12},{1,15},{3,1}... | collective-permute-start | bytes 2359304 | tf_op jit(solution)/shard_map/ppermute | solution.py:270
  13.0 5.0 %compact.2 = bf16[512,128]{1,0:T(8,128)(2,1)} custom-call(s32[2]{0:T(128)S(1)} %pad_add_fusion.2.scalar_ref, s32[12,2048]{1,0:T(8,128)} %sensors_ref.2, bf16[12,64,512]{2,1,0:T(8,128)(2,1)} %temps_ref.1), custom_call_target="tpu_custom_call" | custom-call | tf_op jit(solution)/shard_map/compact/pallas_call | solution.py:75
  18.0 10.7 %all-to-all-start.1 = ((bf16[64,8,128]{2,1,0:T(8,128)(2,1)}), bf16[64,8,128]{2,1,0:T(8,128)(2,1)S(1)}, u32[]{:S(2)}, u32[]{:S(2)}) async-start(bf16[64,8,128]{2,1,0:T(8,128)(2,1)} %bitcast.10), calls=%async_computation.1 | async-start | bytes 262144 | tf_op jit(solution)/shard_map/all_to_all | solution.py:293
  28.8 3.8 %longest.1 = s32[1,1]{1,0:T(1,128)} custom-call(s32[12,2048]{1,0:T(8,128)} %sensors_ref.2), custom_call_target="tpu_custom_call" | custom-call | flops 1258291200 | bytes 98304 | tf_op jit(solution)/shard_map/longest/pallas_call | solution.py:142
  33.4 0.1 copy.7
  33.6 7.9 %all-to-all-done.1.lists_ref = bf16[64,8,128]{2,1,0:T(8,128)(2,1)S(1)} async-done(((bf16[64,8,128]{2,1,0:T(8,128)(2,1)}), bf16[64,8,128]{2,1,0:T(8,128)(2,1)S(1)}, u32[]{:S(2)}, u32[]{:S(2)}) %all-to-all-start.1) | async-done | bytes 131104 | tf_op jit(solution)/shard_map/all_to_all | solution.py:293
  41.5 1.5 %expand.2 = bf16[32,768]{1,0:T(8,128)(2,1)S(1)} custom-call(s32[2]{0:T(128)S(1)} %pad_add_fusion.3.scalar_ref, s32[12,32]{1,0:T(8,128)S(1)} %constant_dynamic-slice_fusion.rows_ref, s32[32,12]{1,0:T(8,128)S(1)} %bitcast.27, bf16[64,8,128]{2,1,0:T(8,128)(2,1)S(1)} %all-to-all-done.1.lists_ref), custom_call_target="tpu_custom_call" | custom-call | tf_op jit(solution)/shard_map/expand/pallas_call | solution.py:112
  43.0 2.5 %collective-permute-start.2 = (bf16[768,512]{1,0:T(8,128)(2,1)S(1)}, bf16[768,512]{1,0:T(8,128)(2,1)}, u32[]{:S(2)}, u32[]{:S(2)}) collective-permute-start(bf16[768,512]{1,0:T(8,128)(2,1)S(1)} %collective-permute-done.rest_1_), channel_id=1, source_target_pairs={{0,2},{2,4},{4,6},{6,8},{8,10},{10,12},{12,14},{14,0},{1,3},{3,5},... | collective-permute-start | bytes 2359304 | tf_op jit(solution)/shard_map/ppermute | solution.py:270
  45.5 4.5 %collective-permute-start.3 = (bf16[768,512]{1,0:T(8,128)(2,1)S(1)}, bf16[768,512]{1,0:T(8,128)(2,1)}, u32[]{:S(2)}, u32[]{:S(2)}) collective-permute-start(bf16[768,512]{1,0:T(8,128)(2,1)S(1)} %collective-permute-done.1.rest_2_), channel_id=1, source_target_pairs={{0,14},{2,0},{4,2},{6,4},{8,6},{10,8},{12,10},{14,12},{1,15},{3,1}... | collective-permute-start | bytes 2359304 | tf_op jit(solution)/shard_map/ppermute | solution.py:270
  50.1 8.0 %all_to_all.21 = bf16[8,4,768]{2,1,0:T(4,128)(2,1)S(1)} all-to-all(bf16[8,4,768]{2,1,0:T(4,128)(2,1)S(1)} %reshape.19), channel_id=1, replica_groups=mesh['y'=8,'xh'=2,'core'=2,'z'=8,'xl'=2] {'xh','xl','core'}, dimensions={0} | all-to-all | bytes 98304 | tf_op jit(solution)/shard_map/all_to_all | solution.py:310
  58.2 0.9 broadcast_in_dim.2
  59.0 7.1 %all-to-all-start.3 = ((bf16[64,4,768]{2,1,0:T(4,128)(2,1)}), bf16[64,4,768]{2,1,0:T(4,128)(2,1)}, u32[]{:S(2)}, u32[]{:S(2)}) async-start(bf16[64,4,768]{2,1,0:T(4,128)(2,1)} %broadcast_in_dim.2), calls=%async_computation.3 | async-start | bytes 786432 | tf_op jit(solution)/shard_map/all_to_all | solution.py:315
  66.1 1.9 %collective-permute-start.5 = (bf16[768,512]{1,0:T(8,128)(2,1)}, bf16[768,512]{1,0:T(8,128)(2,1)S(1)}, u32[]{:S(2)}, u32[]{:S(2)}) collective-permute-start(bf16[768,512]{1,0:T(8,128)(2,1)} %collective-permute-done.2.rest_3_), channel_id=1, source_target_pairs={{0,2},{2,4},{4,6},{6,8},{8,10},{10,12},{12,14},{14,0},{1,3},{3,5},... | collective-permute-start | bytes 2359304 | tf_op jit(solution)/shard_map/ppermute | solution.py:270
  68.1 5.1 %collective-permute-start.6 = (bf16[768,512]{1,0:T(8,128)(2,1)}, bf16[768,512]{1,0:T(8,128)(2,1)S(1)}, u32[]{:S(2)}, u32[]{:S(2)}) collective-permute-start(bf16[768,512]{1,0:T(8,128)(2,1)} %collective-permute-done.3.rest_4_), channel_id=1, source_target_pairs={{0,14},{2,0},{4,2},{6,4},{8,6},{10,8},{12,10},{14,12},{1,15},{3,1}... | collective-permute-start | bytes 2359304 | tf_op jit(solution)/shard_map/ppermute | solution.py:270
  73.3 7.6 %all-to-all-done.3 = bf16[64,4,768]{2,1,0:T(4,128)(2,1)} async-done(((bf16[64,4,768]{2,1,0:T(4,128)(2,1)}), bf16[64,4,768]{2,1,0:T(4,128)(2,1)}, u32[]{:S(2)}, u32[]{:S(2)}) %all-to-all-start.3) | async-done | bytes 393248 | tf_op jit(solution)/shard_map/all_to_all | solution.py:315
  80.9 1.1 reshape.20.readings_ref
  82.0 2.3 %send.3 = bf16[5,128,512]{2,1,0:T(8,128)(2,1)S(1)} custom-call(s32[2]{0:T(128)S(1)} %pad_add_fusion.4.scalar_ref, bf16[256,768]{1,0:T(8,128)(2,1)S(1)} %reshape.20.readings_ref, bf16[768,512]{1,0:T(8,128)(2,1)} %bitcast.25, bf16[768,512]{1,0:T(8,128)(2,1)S(1)} %collective-permute-done.rest_1_, bf16[768,512]{1,0:T(8,128)(2,1)S(1)} %collective-permute-done.1.rest_2_, ...), custom_call_target="tpu_custom_call" | custom-call | flops 503316480 | bytes 3932160 | tf_op jit(solution)/shard_map/send/pallas_call | solution.py:226
  84.3 2.7 %collective-permute-start.4 = (bf16[5,128,512]{2,1,0:T(8,128)(2,1)S(1)}, bf16[5,128,512]{2,1,0:T(8,128)(2,1)S(1)}, u32[]{:S(2)}, u32[]{:S(2)}) collective-permute-start(bf16[5,128,512]{2,1,0:T(8,128)(2,1)S(1)} %send.3), channel_id=1, source_target_pairs={{0,1},{1,0},{2,3},{3,2},{4,5},{5,4},{6,7},{7,6},{8,9},{9,8},{10,11... | collective-permute-start | bytes 1966088 | tf_op jit(solution)/shard_map/ppermute | solution.py:320
  87.1 2.0 %collective-permute-done.5.rest_0_.rest_5_ = bf16[768,512]{1,0:T(8,128)(2,1)S(1)} collective-permute-done((bf16[768,512]{1,0:T(8,128)(2,1)}, bf16[768,512]{1,0:T(8,128)(2,1)S(1)}, u32[]{:S(2)}, u32[]{:S(2)}) %collective-permute-start.5) | collective-permute-done | bytes 786464 | tf_op jit(solution)/shard_map/ppermute | solution.py:270
  89.1 1.3 %collective-permute-done.6.rest_1_.rest_6_ = bf16[768,512]{1,0:T(8,128)(2,1)S(1)} collective-permute-done((bf16[768,512]{1,0:T(8,128)(2,1)}, bf16[768,512]{1,0:T(8,128)(2,1)S(1)}, u32[]{:S(2)}, u32[]{:S(2)}) %collective-permute-start.6) | collective-permute-done | bytes 786464 | tf_op jit(solution)/shard_map/ppermute | solution.py:270
  90.4 2.1 %collective-permute-start.8 = (bf16[384,512]{1,0:T(8,128)(2,1)S(1)}, bf16[384,512]{1,0:T(8,128)(2,1)S(1)}, u32[]{:S(2)}, u32[]{:S(2)}) collective-permute-start(bf16[384,512]{1,0:T(8,128)(2,1)S(1)} %slice.6), channel_id=1, source_target_pairs={{0,2},{2,4},{4,6},{6,8},{8,10},{10,12},{12,14},{14,0},{1,3},{3,5},... | collective-permute-start | bytes 1179656 | tf_op jit(solution)/shard_map/ppermute | solution.py:270
  92.5 5.5 %collective-permute-start.9 = (bf16[384,512]{1,0:T(8,128)(2,1)S(1)}, bf16[384,512]{1,0:T(8,128)(2,1)S(1)}, u32[]{:S(2)}, u32[]{:S(2)}) collective-permute-start(bf16[384,512]{1,0:T(8,128)(2,1)S(1)} %slice.7), channel_id=1, source_target_pairs={{0,14},{2,0},{4,2},{6,4},{8,6},{10,8},{12,10},{14,12},{1,15},{3,1}... | collective-permute-start | bytes 1179656 | tf_op jit(solution)/shard_map/ppermute | solution.py:270
  98.0 0.9 send.4
  98.9 2.8 %collective-permute-start.7 = (bf16[2,128,512]{2,1,0:T(8,128)(2,1)S(1)}, bf16[2,128,512]{2,1,0:T(8,128)(2,1)S(1)}, u32[]{:S(2)}, u32[]{:S(2)}) collective-permute-start(bf16[2,128,512]{2,1,0:T(8,128)(2,1)S(1)} %send.4), channel_id=1, source_target_pairs={{0,1},{1,0},{2,3},{3,2},{4,5},{5,4},{6,7},{7,6},{8,9},{9,8},{10,11... | collective-permute-start | bytes 786440 | tf_op jit(solution)/shard_map/ppermute | solution.py:320
  101.7 2.6 %collective-permute-done.8.rest_0_.rest_7_ = bf16[384,512]{1,0:T(8,128)(2,1)S(1)} collective-permute-done((bf16[384,512]{1,0:T(8,128)(2,1)S(1)}, bf16[384,512]{1,0:T(8,128)(2,1)S(1)}, u32[]{:S(2)}, u32[]{:S(2)}) %collective-permute-start.8) | collective-permute-done | bytes 393248 | tf_op jit(solution)/shard_map/ppermute | solution.py:270
  104.3 1.2 %collective-permute-done.9.rest_1_.rest_8_ = bf16[384,512]{1,0:T(8,128)(2,1)S(1)} collective-permute-done((bf16[384,512]{1,0:T(8,128)(2,1)S(1)}, bf16[384,512]{1,0:T(8,128)(2,1)S(1)}, u32[]{:S(2)}, u32[]{:S(2)}) %collective-permute-start.9) | collective-permute-done | bytes 393248 | tf_op jit(solution)/shard_map/ppermute | solution.py:270
  105.5 0.8 send.5
  106.4 2.7 %collective-permute-start.10 = (bf16[1,128,512]{2,1,0:T(8,128)(2,1)S(1)}, bf16[1,128,512]{2,1,0:T(8,128)(2,1)S(1)}, u32[]{:S(2)}, u32[]{:S(2)}) collective-permute-start(bf16[1,128,512]{2,1,0:T(8,128)(2,1)S(1)} %send.5), channel_id=1, source_target_pairs={{0,1},{1,0},{2,3},{3,2},{4,5},{5,4},{6,7},{7,6},{8,9},{9,8},{10,11... | collective-permute-start | bytes 393224 | tf_op jit(solution)/shard_map/ppermute | solution.py:320
  109.1 3.1 %keep.1.rest_3_ = bf16[128,8192]{1,0:T(8,128)(2,1)} custom-call(s32[2]{0:T(128)S(1)} %pad_add_fusion.4.scalar_ref, bf16[256,768]{1,0:T(8,128)(2,1)S(1)} %reshape.20.readings_ref, bf16[768,512]{1,0:T(8,128)(2,1)S(1)} %bitcast.26, bf16[768,512]{1,0:T(8,128)(2,1)S(1)} %collective-permute-done.rest_1_, bf16[768,512]{1,0:T(8,128)(2,1)S(1)} %collective-permute-done.1.rest_2_, ...), custom_call_target="tpu_custom_call" | custom-call | flops 805306368 | bytes 6291456 | tf_op jit(solution)/shard_map/keep/pallas_call | solution.py:241
  112.3 0.9 collective-permute-done.10.rest_2_
  113.2 1.6 %place.1 = bf16[128,8192]{1,0:T(8,128)(2,1)} custom-call(s32[2]{0:T(128)S(1)} %pad_add_fusion.4.scalar_ref, bf16[5,128,512]{2,1,0:T(8,128)(2,1)S(1)} %collective-permute-done.4.rest_0_, bf16[2,128,512]{2,1,0:T(8,128)(2,1)S(1)} %collective-permute-done.7.rest_1_, ...), custom_call_target="tpu_custom_call", output_to_operand_aliasing={{}: (4, {})} | custom-call | tf_op jit(solution)/shard_map/place/pallas_call | solution.py:256
  (21 shorter events, 0.4 us)
Async XLA Ops:
  0.0 43.0 %collective-permute-start = (bf16[768,512]{1,0:T(8,128)(2,1)}, bf16[768,512]{1,0:T(8,128)(2,1)S(1)}, u32[]{:S(2)}, u32[]{:S(2)}) collective-permute-start(bf16[768,512]{1,0:T(8,128)(2,1)} %bitcast.23), channel_id=1, source_target_pairs={{0,2},{2,4},{4,6},{6,8},{8,10},{10,12},{12,14},{14,0},{1,3},{3,5},... | collective-permute-start | bytes 2359304 | tf_op jit(solution)/shard_map/ppermute | solution.py:270
  4.3 41.3 %collective-permute-start.1 = (bf16[768,512]{1,0:T(8,128)(2,1)}, bf16[768,512]{1,0:T(8,128)(2,1)S(1)}, u32[]{:S(2)}, u32[]{:S(2)}) collective-permute-start(bf16[768,512]{1,0:T(8,128)(2,1)} %bitcast.24), channel_id=1, source_target_pairs={{0,14},{2,0},{4,2},{6,4},{8,6},{10,8},{12,10},{14,12},{1,15},{3,1}... | collective-permute-start | bytes 2359304 | tf_op jit(solution)/shard_map/ppermute | solution.py:270
  18.0 23.5 %all-to-all-start.1 = ((bf16[64,8,128]{2,1,0:T(8,128)(2,1)}), bf16[64,8,128]{2,1,0:T(8,128)(2,1)S(1)}, u32[]{:S(2)}, u32[]{:S(2)}) async-start(bf16[64,8,128]{2,1,0:T(8,128)(2,1)} %bitcast.10), calls=%async_computation.1 | async-start | bytes 262144 | tf_op jit(solution)/shard_map/all_to_all | solution.py:293
  28.8 4.6 %copy-start.2 = (s32[12,2048]{1,0:T(8,128)S(1)}, s32[12,2048]{1,0:T(8,128)}, u32[]{:S(2)}) copy-start(s32[12,2048]{1,0:T(8,128)} %sensors_ref.2) | copy-start | bytes 294916
  28.8 14.2 %copy-start = (bf16[12,64,512]{2,1,0:T(8,128)(2,1)S(1)}, bf16[12,64,512]{2,1,0:T(8,128)(2,1)}, u32[]{:S(2)}) copy-start(bf16[12,64,512]{2,1,0:T(8,128)(2,1)} %temps_ref.1) | copy-start | bytes 2359300
  43.0 23.1 %collective-permute-start.2 = (bf16[768,512]{1,0:T(8,128)(2,1)S(1)}, bf16[768,512]{1,0:T(8,128)(2,1)}, u32[]{:S(2)}, u32[]{:S(2)}) collective-permute-start(bf16[768,512]{1,0:T(8,128)(2,1)S(1)} %collective-permute-done.rest_1_), channel_id=1, source_target_pairs={{0,2},{2,4},{4,6},{6,8},{8,10},{10,12},{12,14},{14,0},{1,3},{3,5},... | collective-permute-start | bytes 2359304 | tf_op jit(solution)/shard_map/ppermute | solution.py:270
  45.5 22.5 %collective-permute-start.3 = (bf16[768,512]{1,0:T(8,128)(2,1)S(1)}, bf16[768,512]{1,0:T(8,128)(2,1)}, u32[]{:S(2)}, u32[]{:S(2)}) collective-permute-start(bf16[768,512]{1,0:T(8,128)(2,1)S(1)} %collective-permute-done.1.rest_2_), channel_id=1, source_target_pairs={{0,14},{2,0},{4,2},{6,4},{8,6},{10,8},{12,10},{14,12},{1,15},{3,1}... | collective-permute-start | bytes 2359304 | tf_op jit(solution)/shard_map/ppermute | solution.py:270
  59.0 21.9 %all-to-all-start.3 = ((bf16[64,4,768]{2,1,0:T(4,128)(2,1)}), bf16[64,4,768]{2,1,0:T(4,128)(2,1)}, u32[]{:S(2)}, u32[]{:S(2)}) async-start(bf16[64,4,768]{2,1,0:T(4,128)(2,1)} %broadcast_in_dim.2), calls=%async_computation.3 | async-start | bytes 786432 | tf_op jit(solution)/shard_map/all_to_all | solution.py:315
  66.1 22.9 %collective-permute-start.5 = (bf16[768,512]{1,0:T(8,128)(2,1)}, bf16[768,512]{1,0:T(8,128)(2,1)S(1)}, u32[]{:S(2)}, u32[]{:S(2)}) collective-permute-start(bf16[768,512]{1,0:T(8,128)(2,1)} %collective-permute-done.2.rest_3_), channel_id=1, source_target_pairs={{0,2},{2,4},{4,6},{6,8},{8,10},{10,12},{12,14},{14,0},{1,3},{3,5},... | collective-permute-start | bytes 2359304 | tf_op jit(solution)/shard_map/ppermute | solution.py:270
  68.1 22.3 %collective-permute-start.6 = (bf16[768,512]{1,0:T(8,128)(2,1)}, bf16[768,512]{1,0:T(8,128)(2,1)S(1)}, u32[]{:S(2)}, u32[]{:S(2)}) collective-permute-start(bf16[768,512]{1,0:T(8,128)(2,1)} %collective-permute-done.3.rest_4_), channel_id=1, source_target_pairs={{0,14},{2,0},{4,2},{6,4},{8,6},{10,8},{12,10},{14,12},{1,15},{3,1}... | collective-permute-start | bytes 2359304 | tf_op jit(solution)/shard_map/ppermute | solution.py:270
  84.3 27.9 %collective-permute-start.4 = (bf16[5,128,512]{2,1,0:T(8,128)(2,1)S(1)}, bf16[5,128,512]{2,1,0:T(8,128)(2,1)S(1)}, u32[]{:S(2)}, u32[]{:S(2)}) collective-permute-start(bf16[5,128,512]{2,1,0:T(8,128)(2,1)S(1)} %send.3), channel_id=1, source_target_pairs={{0,1},{1,0},{2,3},{3,2},{4,5},{5,4},{6,7},{7,6},{8,9},{9,8},{10,11... | collective-permute-start | bytes 1966088 | tf_op jit(solution)/shard_map/ppermute | solution.py:320
  90.4 18.7 %copy-start.1 = (bf16[12,64,512]{2,1,0:T(8,128)(2,1)S(1)}, bf16[12,64,512]{2,1,0:T(8,128)(2,1)}, u32[]{:S(2)}) copy-start(bf16[12,64,512]{2,1,0:T(8,128)(2,1)} %temps_ref.1) | copy-start | bytes 2359300
  90.4 13.9 %collective-permute-start.8 = (bf16[384,512]{1,0:T(8,128)(2,1)S(1)}, bf16[384,512]{1,0:T(8,128)(2,1)S(1)}, u32[]{:S(2)}, u32[]{:S(2)}) collective-permute-start(bf16[384,512]{1,0:T(8,128)(2,1)S(1)} %slice.6), channel_id=1, source_target_pairs={{0,2},{2,4},{4,6},{6,8},{8,10},{10,12},{12,14},{14,0},{1,3},{3,5},... | collective-permute-start | bytes 1179656 | tf_op jit(solution)/shard_map/ppermute | solution.py:270
  92.5 13.0 %collective-permute-start.9 = (bf16[384,512]{1,0:T(8,128)(2,1)S(1)}, bf16[384,512]{1,0:T(8,128)(2,1)S(1)}, u32[]{:S(2)}, u32[]{:S(2)}) collective-permute-start(bf16[384,512]{1,0:T(8,128)(2,1)S(1)} %slice.7), channel_id=1, source_target_pairs={{0,14},{2,0},{4,2},{6,4},{8,6},{10,8},{12,10},{14,12},{1,15},{3,1}... | collective-permute-start | bytes 1179656 | tf_op jit(solution)/shard_map/ppermute | solution.py:270
  98.9 13.4 %collective-permute-start.7 = (bf16[2,128,512]{2,1,0:T(8,128)(2,1)S(1)}, bf16[2,128,512]{2,1,0:T(8,128)(2,1)S(1)}, u32[]{:S(2)}, u32[]{:S(2)}) collective-permute-start(bf16[2,128,512]{2,1,0:T(8,128)(2,1)S(1)} %send.4), channel_id=1, source_target_pairs={{0,1},{1,0},{2,3},{3,2},{4,5},{5,4},{6,7},{7,6},{8,9},{9,8},{10,11... | collective-permute-start | bytes 786440 | tf_op jit(solution)/shard_map/ppermute | solution.py:320
  106.4 6.9 %collective-permute-start.10 = (bf16[1,128,512]{2,1,0:T(8,128)(2,1)S(1)}, bf16[1,128,512]{2,1,0:T(8,128)(2,1)S(1)}, u32[]{:S(2)}, u32[]{:S(2)}) collective-permute-start(bf16[1,128,512]{2,1,0:T(8,128)(2,1)S(1)} %send.5), channel_id=1, source_target_pairs={{0,1},{1,0},{2,3},{3,2},{4,5},{5,4},{6,7},{7,6},{8,9},{9,8},{10,11... | collective-permute-start | bytes 393224 | tf_op jit(solution)/shard_map/ppermute | solution.py:320

commit v10 on v9

--- a/solution.py
+++ b/solution.py
@@ -278,7 +278,7 @@
     z, xl = lax.axis_index("z"), lax.axis_index("xl")
 
     pixels = temps.reshape(depth, width)
-    up, down = [pixels, ring(pixels, 1)], [pixels, ring(pixels, -1)]
+    up, down = [pixels, ring(pixels, 1)], [pixels]
 
     def go_on(blocks, shift, ready):
         block, _ = lax.optimization_barrier((blocks[-1], ready))
@@ -298,6 +298,7 @@
         return expand(jnp.stack([side, number * SLOTS]), chosen, lists, width)
 
     lists = listed(jnp.int32(0))
+    go_on(down, -1, lists)
     seen, _ = lax.optimization_barrier((sensors, lists))
     rounds = pl.cdiv(longest(seen, group, devices, width), SLOTS)
     _, part = lax.while_loop(

time: 116 us -> 119 us (1.026)
  waiting for transfers between devices: 23.6 us -> 26.9 us
    ppermute x8, waiting for transfers between devices: 7.13 us -> 10.3 us  [ring(): lax.ppermute(value, 'z', [(i, (i + shift) % size) for i in range(size)])]
    ppermute x8, starting transfers between devices: 34.5 us -> 32.8 us  [ring(): lax.ppermute(value, 'z', [(i, (i + shift) % size) for i in range(size)])]
    all_to_all x1, starting transfers between devices: 7.1 us -> 8.61 us  [body(): lax.all_to_all(copies, PLANE, 0, 0, tiled=True).reshape(-1, depth)]
  transfers between devices with their start and end apart: 13 -> 13, of which waited for: 7 -> 7; matrix products, arithmetic and copies ran while one was open for 2% -> 2% of each run, Pallas kernels for 12% -> 11%
where the time goes in v10:
time: 119 us; the launch traced here: 118 us
  starting transfers between devices  60.4 us (51%)
  waiting for transfers between devices  26.9 us (23%)
  Pallas kernels  19.1 us (16%)
  blocking collectives  8.04 us (7%)
  local copies, waits for them, and re-layouts  2.2 us (2%)
    ppermute x8, starting transfers between devices, ring(): lax.ppermute(value, 'z', [(i, (i + shift) % size) for i in range(size)])  32.8 us
    all_to_all x1, starting transfers between devices, exchanged(): return lax.all_to_all(lists, LISTS, 0, 0, tiled=True)  10.7 us
    ppermute x8, waiting for transfers between devices, ring(): lax.ppermute(value, 'z', [(i, (i + shift) % size) for i in range(size)])  10.3 us
    all_to_all x1, starting transfers between devices, body(): lax.all_to_all(copies, PLANE, 0, 0, tiled=True).reshape(-1, depth)  8.61 us
    ppermute x3, starting transfers between devices, swapped(): return lax.ppermute(sent, 'xl', [(0, 1), (1, 0)])  8.29 us
    all_to_all x1, blocking collectives, body(): lax.all_to_all(part.reshape(n_side, group // n_side, depth), SIDE, 0, 0,...  8.04 us
    all_to_all x1, waiting for transfers between devices, exchanged(): return lax.all_to_all(lists, LISTS, 0, 0, tiled=True)  7.92 us
    all_to_all x1, waiting for transfers between devices, body(): lax.all_to_all(copies, PLANE, 0, 0, tiled=True).reshape(-1, depth)  7.68 us
  transfers between devices with their start and end apart: 13, of which 7 were waited for; matrix products, arithmetic and copies ran while one was open for 2% of the time, Pallas kernels for 11%

profile of v10, /device:TPU:6, one launch (start us, length us, event | category | flops | bytes accessed | tf_op | source)
XLA Modules:
  0.0 118.0 jit_solution(5258408604849207623)
XLA Ops:
  0.0 4.3 %collective-permute-start = (bf16[768,512]{1,0:T(8,128)(2,1)}, bf16[768,512]{1,0:T(8,128)(2,1)S(1)}, u32[]{:S(2)}, u32[]{:S(2)}) collective-permute-start(bf16[768,512]{1,0:T(8,128)(2,1)} %bitcast.23), channel_id=1, source_target_pairs={{0,2},{2,4},{4,6},{6,8},{8,10},{10,12},{12,14},{14,0},{1,3},{3,5},... | collective-permute-start | bytes 2359304 | tf_op jit(solution)/shard_map/ppermute | solution.py:270
  4.4 5.0 %compact.2 = bf16[512,128]{1,0:T(8,128)(2,1)} custom-call(s32[2]{0:T(128)S(1)} %pad_add_fusion.2.scalar_ref, s32[12,2048]{1,0:T(8,128)} %sensors_ref.2, bf16[12,64,512]{2,1,0:T(8,128)(2,1)} %temps_ref.1), custom_call_target="tpu_custom_call" | custom-call | tf_op jit(solution)/shard_map/compact/pallas_call | solution.py:75
  9.4 8.6 %collective-permute-start.1 = (bf16[768,512]{1,0:T(8,128)(2,1)}, bf16[768,512]{1,0:T(8,128)(2,1)S(1)}, u32[]{:S(2)}, u32[]{:S(2)}) collective-permute-start(bf16[768,512]{1,0:T(8,128)(2,1)} %bitcast.24), channel_id=1, source_target_pairs={{0,14},{2,0},{4,2},{6,4},{8,6},{10,8},{12,10},{14,12},{1,15},{3,1}... | collective-permute-start | bytes 2359304 | tf_op jit(solution)/shard_map/ppermute | solution.py:270
  18.0 10.7 %all-to-all-start.1 = ((bf16[64,8,128]{2,1,0:T(8,128)(2,1)}), bf16[64,8,128]{2,1,0:T(8,128)(2,1)S(1)}, u32[]{:S(2)}, u32[]{:S(2)}) async-start(bf16[64,8,128]{2,1,0:T(8,128)(2,1)} %bitcast.10), calls=%async_computation.1 | async-start | bytes 262144 | tf_op jit(solution)/shard_map/all_to_all | solution.py:293
  28.8 3.8 %longest.1 = s32[1,1]{1,0:T(1,128)} custom-call(s32[12,2048]{1,0:T(8,128)} %sensors_ref.2), custom_call_target="tpu_custom_call" | custom-call | flops 1258291200 | bytes 98304 | tf_op jit(solution)/shard_map/longest/pallas_call | solution.py:142
  33.4 0.1 copy.7
  33.6 7.9 %all-to-all-done.1.lists_ref = bf16[64,8,128]{2,1,0:T(8,128)(2,1)S(1)} async-done(((bf16[64,8,128]{2,1,0:T(8,128)(2,1)}), bf16[64,8,128]{2,1,0:T(8,128)(2,1)S(1)}, u32[]{:S(2)}, u32[]{:S(2)}) %all-to-all-start.1) | async-done | bytes 131104 | tf_op jit(solution)/shard_map/all_to_all | solution.py:293
  41.5 1.5 %expand.2 = bf16[32,768]{1,0:T(8,128)(2,1)S(1)} custom-call(s32[2]{0:T(128)S(1)} %pad_add_fusion.3.scalar_ref, s32[12,32]{1,0:T(8,128)S(1)} %constant_dynamic-slice_fusion.rows_ref, s32[32,12]{1,0:T(8,128)S(1)} %bitcast.27, bf16[64,8,128]{2,1,0:T(8,128)(2,1)S(1)} %all-to-all-done.1.lists_ref), custom_call_target="tpu_custom_call" | custom-call | tf_op jit(solution)/shard_map/expand/pallas_call | solution.py:112
  43.0 2.4 %collective-permute-start.3 = (bf16[768,512]{1,0:T(8,128)(2,1)S(1)}, bf16[768,512]{1,0:T(8,128)(2,1)}, u32[]{:S(2)}, u32[]{:S(2)}) collective-permute-start(bf16[768,512]{1,0:T(8,128)(2,1)S(1)} %collective-permute-done.1.rest_2_), channel_id=1, source_target_pairs={{0,14},{2,0},{4,2},{6,4},{8,6},{10,8},{12,10},{14,12},{1,15},{3,1}... | collective-permute-start | bytes 2359304 | tf_op jit(solution)/shard_map/ppermute | solution.py:270
  45.4 3.4 %collective-permute-start.2 = (bf16[768,512]{1,0:T(8,128)(2,1)S(1)}, bf16[768,512]{1,0:T(8,128)(2,1)}, u32[]{:S(2)}, u32[]{:S(2)}) collective-permute-start(bf16[768,512]{1,0:T(8,128)(2,1)S(1)} %collective-permute-done.rest_1_), channel_id=1, source_target_pairs={{0,2},{2,4},{4,6},{6,8},{8,10},{10,12},{12,14},{14,0},{1,3},{3,5},... | collective-permute-start | bytes 2359304 | tf_op jit(solution)/shard_map/ppermute | solution.py:270
  48.9 8.0 %all_to_all.21 = bf16[8,4,768]{2,1,0:T(4,128)(2,1)S(1)} all-to-all(bf16[8,4,768]{2,1,0:T(4,128)(2,1)S(1)} %reshape.19), channel_id=1, replica_groups=mesh['y'=8,'xh'=2,'core'=2,'z'=8,'xl'=2] {'xh','xl','core'}, dimensions={0} | all-to-all | bytes 98304 | tf_op jit(solution)/shard_map/all_to_all | solution.py:311
  57.0 0.9 broadcast_in_dim.2
  57.8 8.6 %all-to-all-start.3 = ((bf16[64,4,768]{2,1,0:T(4,128)(2,1)}), bf16[64,4,768]{2,1,0:T(4,128)(2,1)}, u32[]{:S(2)}, u32[]{:S(2)}) async-start(bf16[64,4,768]{2,1,0:T(4,128)(2,1)} %broadcast_in_dim.2), calls=%async_computation.3 | async-start | bytes 786432 | tf_op jit(solution)/shard_map/all_to_all | solution.py:316
  66.4 5.0 %collective-permute-start.6 = (bf16[768,512]{1,0:T(8,128)(2,1)}, bf16[768,512]{1,0:T(8,128)(2,1)S(1)}, u32[]{:S(2)}, u32[]{:S(2)}) collective-permute-start(bf16[768,512]{1,0:T(8,128)(2,1)} %collective-permute-done.3.rest_4_), channel_id=1, source_target_pairs={{0,14},{2,0},{4,2},{6,4},{8,6},{10,8},{12,10},{14,12},{1,15},{3,1}... | collective-permute-start | bytes 2359304 | tf_op jit(solution)/shard_map/ppermute | solution.py:270
  71.4 1.9 %collective-permute-start.5 = (bf16[768,512]{1,0:T(8,128)(2,1)}, bf16[768,512]{1,0:T(8,128)(2,1)S(1)}, u32[]{:S(2)}, u32[]{:S(2)}) collective-permute-start(bf16[768,512]{1,0:T(8,128)(2,1)} %collective-permute-done.2.rest_3_), channel_id=1, source_target_pairs={{0,2},{2,4},{4,6},{6,8},{8,10},{10,12},{12,14},{14,0},{1,3},{3,5},... | collective-permute-start | bytes 2359304 | tf_op jit(solution)/shard_map/ppermute | solution.py:270
  73.5 7.7 %all-to-all-done.3 = bf16[64,4,768]{2,1,0:T(4,128)(2,1)} async-done(((bf16[64,4,768]{2,1,0:T(4,128)(2,1)}), bf16[64,4,768]{2,1,0:T(4,128)(2,1)}, u32[]{:S(2)}, u32[]{:S(2)}) %all-to-all-start.3) | async-done | bytes 393248 | tf_op jit(solution)/shard_map/all_to_all | solution.py:316
  81.1 1.1 reshape.20.readings_ref
  82.2 2.3 %send.3 = bf16[5,128,512]{2,1,0:T(8,128)(2,1)S(1)} custom-call(s32[2]{0:T(128)S(1)} %pad_add_fusion.4.scalar_ref, bf16[256,768]{1,0:T(8,128)(2,1)S(1)} %reshape.20.readings_ref, bf16[768,512]{1,0:T(8,128)(2,1)} %bitcast.25, bf16[768,512]{1,0:T(8,128)(2,1)S(1)} %collective-permute-done.rest_1_, bf16[768,512]{1,0:T(8,128)(2,1)S(1)} %collective-permute-done.1.rest_2_, ...), custom_call_target="tpu_custom_call" | custom-call | flops 503316480 | bytes 3932160 | tf_op jit(solution)/shard_map/send/pallas_call | solution.py:226
  84.5 2.8 %collective-permute-start.4 = (bf16[5,128,512]{2,1,0:T(8,128)(2,1)S(1)}, bf16[5,128,512]{2,1,0:T(8,128)(2,1)S(1)}, u32[]{:S(2)}, u32[]{:S(2)}) collective-permute-start(bf16[5,128,512]{2,1,0:T(8,128)(2,1)S(1)} %send.3), channel_id=1, source_target_pairs={{0,1},{1,0},{2,3},{3,2},{4,5},{5,4},{6,7},{7,6},{8,9},{9,8},{10,11... | collective-permute-start | bytes 1966088 | tf_op jit(solution)/shard_map/ppermute | solution.py:321
  87.3 1.5 %collective-permute-done.6.rest_1_.rest_6_ = bf16[768,512]{1,0:T(8,128)(2,1)S(1)} collective-permute-done((bf16[768,512]{1,0:T(8,128)(2,1)}, bf16[768,512]{1,0:T(8,128)(2,1)S(1)}, u32[]{:S(2)}, u32[]{:S(2)}) %collective-permute-start.6) | collective-permute-done | bytes 786464 | tf_op jit(solution)/shard_map/ppermute | solution.py:270
  88.8 5.2 %collective-permute-done.5.rest_0_.rest_5_ = bf16[768,512]{1,0:T(8,128)(2,1)S(1)} collective-permute-done((bf16[768,512]{1,0:T(8,128)(2,1)}, bf16[768,512]{1,0:T(8,128)(2,1)S(1)}, u32[]{:S(2)}, u32[]{:S(2)}) %collective-permute-start.5) | collective-permute-done | bytes 786464 | tf_op jit(solution)/shard_map/ppermute | solution.py:270
  94.1 2.1 %collective-permute-start.8 = (bf16[384,512]{1,0:T(8,128)(2,1)S(1)}, bf16[384,512]{1,0:T(8,128)(2,1)S(1)}, u32[]{:S(2)}, u32[]{:S(2)}) collective-permute-start(bf16[384,512]{1,0:T(8,128)(2,1)S(1)} %slice.6), channel_id=1, source_target_pairs={{0,2},{2,4},{4,6},{6,8},{8,10},{10,12},{12,14},{14,0},{1,3},{3,5},... | collective-permute-start | bytes 1179656 | tf_op jit(solution)/shard_map/ppermute | solution.py:270
  96.2 5.1 %collective-permute-start.9 = (bf16[384,512]{1,0:T(8,128)(2,1)S(1)}, bf16[384,512]{1,0:T(8,128)(2,1)S(1)}, u32[]{:S(2)}, u32[]{:S(2)}) collective-permute-start(bf16[384,512]{1,0:T(8,128)(2,1)S(1)} %slice.7), channel_id=1, source_target_pairs={{0,14},{2,0},{4,2},{6,4},{8,6},{10,8},{12,10},{14,12},{1,15},{3,1}... | collective-permute-start | bytes 1179656 | tf_op jit(solution)/shard_map/ppermute | solution.py:270
  101.4 0.9 send.4
  102.3 2.8 %collective-permute-start.7 = (bf16[2,128,512]{2,1,0:T(8,128)(2,1)S(1)}, bf16[2,128,512]{2,1,0:T(8,128)(2,1)S(1)}, u32[]{:S(2)}, u32[]{:S(2)}) collective-permute-start(bf16[2,128,512]{2,1,0:T(8,128)(2,1)S(1)} %send.4), channel_id=1, source_target_pairs={{0,1},{1,0},{2,3},{3,2},{4,5},{5,4},{6,7},{7,6},{8,9},{9,8},{10,11... | collective-permute-start | bytes 786440 | tf_op jit(solution)/shard_map/ppermute | solution.py:321
  105.0 2.3 %collective-permute-done.8.rest_0_.rest_7_ = bf16[384,512]{1,0:T(8,128)(2,1)S(1)} collective-permute-done((bf16[384,512]{1,0:T(8,128)(2,1)S(1)}, bf16[384,512]{1,0:T(8,128)(2,1)S(1)}, u32[]{:S(2)}, u32[]{:S(2)}) %collective-permute-start.8) | collective-permute-done | bytes 393248 | tf_op jit(solution)/shard_map/ppermute | solution.py:270
  107.4 1.2 %collective-permute-done.9.rest_1_.rest_8_ = bf16[384,512]{1,0:T(8,128)(2,1)S(1)} collective-permute-done((bf16[384,512]{1,0:T(8,128)(2,1)S(1)}, bf16[384,512]{1,0:T(8,128)(2,1)S(1)}, u32[]{:S(2)}, u32[]{:S(2)}) %collective-permute-start.9) | collective-permute-done | bytes 393248 | tf_op jit(solution)/shard_map/ppermute | solution.py:270
  108.6 0.8 send.5
  109.4 2.8 %collective-permute-start.10 = (bf16[1,128,512]{2,1,0:T(8,128)(2,1)S(1)}, bf16[1,128,512]{2,1,0:T(8,128)(2,1)S(1)}, u32[]{:S(2)}, u32[]{:S(2)}) collective-permute-start(bf16[1,128,512]{2,1,0:T(8,128)(2,1)S(1)} %send.5), channel_id=1, source_target_pairs={{0,1},{1,0},{2,3},{3,2},{4,5},{5,4},{6,7},{7,6},{8,9},{9,8},{10,11... | collective-permute-start | bytes 393224 | tf_op jit(solution)/shard_map/ppermute | solution.py:321
  112.2 3.1 %keep.1.rest_3_ = bf16[128,8192]{1,0:T(8,128)(2,1)} custom-call(s32[2]{0:T(128)S(1)} %pad_add_fusion.4.scalar_ref, bf16[256,768]{1,0:T(8,128)(2,1)S(1)} %reshape.20.readings_ref, bf16[768,512]{1,0:T(8,128)(2,1)S(1)} %bitcast.26, bf16[768,512]{1,0:T(8,128)(2,1)S(1)} %collective-permute-done.rest_1_, bf16[768,512]{1,0:T(8,128)(2,1)S(1)} %collective-permute-done.1.rest_2_, ...), custom_call_target="tpu_custom_call" | custom-call | flops 805306368 | bytes 6291456 | tf_op jit(solution)/shard_map/keep/pallas_call | solution.py:241
  115.4 0.9 collective-permute-done.10.rest_2_
  116.3 1.6 %place.1 = bf16[128,8192]{1,0:T(8,128)(2,1)} custom-call(s32[2]{0:T(128)S(1)} %pad_add_fusion.4.scalar_ref, bf16[5,128,512]{2,1,0:T(8,128)(2,1)S(1)} %collective-permute-done.4.rest_0_, bf16[2,128,512]{2,1,0:T(8,128)(2,1)S(1)} %collective-permute-done.7.rest_1_, ...), custom_call_target="tpu_custom_call", output_to_operand_aliasing={{}: (4, {})} | custom-call | tf_op jit(solution)/shard_map/place/pallas_call | solution.py:256
  (21 shorter events, 0.4 us)
Async XLA Ops:
  0.0 45.4 %collective-permute-start = (bf16[768,512]{1,0:T(8,128)(2,1)}, bf16[768,512]{1,0:T(8,128)(2,1)S(1)}, u32[]{:S(2)}, u32[]{:S(2)}) collective-permute-start(bf16[768,512]{1,0:T(8,128)(2,1)} %bitcast.23), channel_id=1, source_target_pairs={{0,2},{2,4},{4,6},{6,8},{8,10},{10,12},{12,14},{14,0},{1,3},{3,5},... | collective-permute-start | bytes 2359304 | tf_op jit(solution)/shard_map/ppermute | solution.py:270
  9.4 33.6 %collective-permute-start.1 = (bf16[768,512]{1,0:T(8,128)(2,1)}, bf16[768,512]{1,0:T(8,128)(2,1)S(1)}, u32[]{:S(2)}, u32[]{:S(2)}) collective-permute-start(bf16[768,512]{1,0:T(8,128)(2,1)} %bitcast.24), channel_id=1, source_target_pairs={{0,14},{2,0},{4,2},{6,4},{8,6},{10,8},{12,10},{14,12},{1,15},{3,1}... | collective-permute-start | bytes 2359304 | tf_op jit(solution)/shard_map/ppermute | solution.py:270
  18.0 23.5 %all-to-all-start.1 = ((bf16[64,8,128]{2,1,0:T(8,128)(2,1)}), bf16[64,8,128]{2,1,0:T(8,128)(2,1)S(1)}, u32[]{:S(2)}, u32[]{:S(2)}) async-start(bf16[64,8,128]{2,1,0:T(8,128)(2,1)} %bitcast.10), calls=%async_computation.1 | async-start | bytes 262144 | tf_op jit(solution)/shard_map/all_to_all | solution.py:293
  28.8 4.6 %copy-start.2 = (s32[12,2048]{1,0:T(8,128)S(1)}, s32[12,2048]{1,0:T(8,128)}, u32[]{:S(2)}) copy-start(s32[12,2048]{1,0:T(8,128)} %sensors_ref.2) | copy-start | bytes 294916
  28.8 14.2 %copy-start = (bf16[12,64,512]{2,1,0:T(8,128)(2,1)S(1)}, bf16[12,64,512]{2,1,0:T(8,128)(2,1)}, u32[]{:S(2)}) copy-start(bf16[12,64,512]{2,1,0:T(8,128)(2,1)} %temps_ref.1) | copy-start | bytes 2359300
  43.0 23.4 %collective-permute-start.3 = (bf16[768,512]{1,0:T(8,128)(2,1)S(1)}, bf16[768,512]{1,0:T(8,128)(2,1)}, u32[]{:S(2)}, u32[]{:S(2)}) collective-permute-start(bf16[768,512]{1,0:T(8,128)(2,1)S(1)} %collective-permute-done.1.rest_2_), channel_id=1, source_target_pairs={{0,14},{2,0},{4,2},{6,4},{8,6},{10,8},{12,10},{14,12},{1,15},{3,1}... | collective-permute-start | bytes 2359304 | tf_op jit(solution)/shard_map/ppermute | solution.py:270
  45.4 26.0 %collective-permute-start.2 = (bf16[768,512]{1,0:T(8,128)(2,1)S(1)}, bf16[768,512]{1,0:T(8,128)(2,1)}, u32[]{:S(2)}, u32[]{:S(2)}) collective-permute-start(bf16[768,512]{1,0:T(8,128)(2,1)S(1)} %collective-permute-done.rest_1_), channel_id=1, source_target_pairs={{0,2},{2,4},{4,6},{6,8},{8,10},{10,12},{12,14},{14,0},{1,3},{3,5},... | collective-permute-start | bytes 2359304 | tf_op jit(solution)/shard_map/ppermute | solution.py:270
  57.8 23.3 %all-to-all-start.3 = ((bf16[64,4,768]{2,1,0:T(4,128)(2,1)}), bf16[64,4,768]{2,1,0:T(4,128)(2,1)}, u32[]{:S(2)}, u32[]{:S(2)}) async-start(bf16[64,4,768]{2,1,0:T(4,128)(2,1)} %broadcast_in_dim.2), calls=%async_computation.3 | async-start | bytes 786432 | tf_op jit(solution)/shard_map/all_to_all | solution.py:316
  66.4 22.4 %collective-permute-start.6 = (bf16[768,512]{1,0:T(8,128)(2,1)}, bf16[768,512]{1,0:T(8,128)(2,1)S(1)}, u32[]{:S(2)}, u32[]{:S(2)}) collective-permute-start(bf16[768,512]{1,0:T(8,128)(2,1)} %collective-permute-done.3.rest_4_), channel_id=1, source_target_pairs={{0,14},{2,0},{4,2},{6,4},{8,6},{10,8},{12,10},{14,12},{1,15},{3,1}... | collective-permute-start | bytes 2359304 | tf_op jit(solution)/shard_map/ppermute | solution.py:270
  71.4 22.6 %collective-permute-start.5 = (bf16[768,512]{1,0:T(8,128)(2,1)}, bf16[768,512]{1,0:T(8,128)(2,1)S(1)}, u32[]{:S(2)}, u32[]{:S(2)}) collective-permute-start(bf16[768,512]{1,0:T(8,128)(2,1)} %collective-permute-done.2.rest_3_), channel_id=1, source_target_pairs={{0,2},{2,4},{4,6},{6,8},{8,10},{10,12},{12,14},{14,0},{1,3},{3,5},... | collective-permute-start | bytes 2359304 | tf_op jit(solution)/shard_map/ppermute | solution.py:270
  84.5 30.8 %collective-permute-start.4 = (bf16[5,128,512]{2,1,0:T(8,128)(2,1)S(1)}, bf16[5,128,512]{2,1,0:T(8,128)(2,1)S(1)}, u32[]{:S(2)}, u32[]{:S(2)}) collective-permute-start(bf16[5,128,512]{2,1,0:T(8,128)(2,1)S(1)} %send.3), channel_id=1, source_target_pairs={{0,1},{1,0},{2,3},{3,2},{4,5},{5,4},{6,7},{7,6},{8,9},{9,8},{10,11... | collective-permute-start | bytes 1966088 | tf_op jit(solution)/shard_map/ppermute | solution.py:321
  94.1 18.1 %copy-start.1 = (bf16[12,64,512]{2,1,0:T(8,128)(2,1)S(1)}, bf16[12,64,512]{2,1,0:T(8,128)(2,1)}, u32[]{:S(2)}) copy-start(bf16[12,64,512]{2,1,0:T(8,128)(2,1)} %temps_ref.1) | copy-start | bytes 2359300
  94.1 13.3 %collective-permute-start.8 = (bf16[384,512]{1,0:T(8,128)(2,1)S(1)}, bf16[384,512]{1,0:T(8,128)(2,1)S(1)}, u32[]{:S(2)}, u32[]{:S(2)}) collective-permute-start(bf16[384,512]{1,0:T(8,128)(2,1)S(1)} %slice.6), channel_id=1, source_target_pairs={{0,2},{2,4},{4,6},{6,8},{8,10},{10,12},{12,14},{14,0},{1,3},{3,5},... | collective-permute-start | bytes 1179656 | tf_op jit(solution)/shard_map/ppermute | solution.py:270
  96.2 12.4 %collective-permute-start.9 = (bf16[384,512]{1,0:T(8,128)(2,1)S(1)}, bf16[384,512]{1,0:T(8,128)(2,1)S(1)}, u32[]{:S(2)}, u32[]{:S(2)}) collective-permute-start(bf16[384,512]{1,0:T(8,128)(2,1)S(1)} %slice.7), channel_id=1, source_target_pairs={{0,14},{2,0},{4,2},{6,4},{8,6},{10,8},{12,10},{14,12},{1,15},{3,1}... | collective-permute-start | bytes 1179656 | tf_op jit(solution)/shard_map/ppermute | solution.py:270
  102.3 13.1 %collective-permute-start.7 = (bf16[2,128,512]{2,1,0:T(8,128)(2,1)S(1)}, bf16[2,128,512]{2,1,0:T(8,128)(2,1)S(1)}, u32[]{:S(2)}, u32[]{:S(2)}) collective-permute-start(bf16[2,128,512]{2,1,0:T(8,128)(2,1)S(1)} %send.4), channel_id=1, source_target_pairs={{0,1},{1,0},{2,3},{3,2},{4,5},{5,4},{6,7},{7,6},{8,9},{9,8},{10,11... | collective-permute-start | bytes 786440 | tf_op jit(solution)/shard_map/ppermute | solution.py:321
  109.4 6.9 %collective-permute-start.10 = (bf16[1,128,512]{2,1,0:T(8,128)(2,1)S(1)}, bf16[1,128,512]{2,1,0:T(8,128)(2,1)S(1)}, u32[]{:S(2)}, u32[]{:S(2)}) collective-permute-start(bf16[1,128,512]{2,1,0:T(8,128)(2,1)S(1)} %send.5), channel_id=1, source_target_pairs={{0,1},{1,0},{2,3},{3,2},{4,5},{5,4},{6,7},{7,6},{8,9},{9,8},{10,11... | collective-permute-start | bytes 393224 | tf_op jit(solution)/shard_map/ppermute | solution.py:321

commit v11 on v9

--- a/solution.py
+++ b/solution.py
@@ -254,7 +254,9 @@
 
 def place(here, pieces, shifts, whole):
     return pl.pallas_call(
-        functools.partial(place_kernel, len(shifts), shifts),
+        functools.partial(
+            place_kernel, whole.shape[1] // (2 * pieces[0].shape[2]), shifts
+        ),
         in_specs=[SMEM] + [HBM] * (len(pieces) + 1),
         out_specs=HBM,
         out_shape=jax.ShapeDtypeStruct(whole.shape, BF16),
@@ -327,7 +329,8 @@
     shifts = [0, -1, 1, -2, 2, -3, 3, 4]
     pieces = [swapped(sent)]
     pieces += [swapped(send(here, readings, blocks[low:high])) for low, high in ((5, 7), (7, 8))]
-    return place(here, pieces, shifts, keep(here, readings, blocks, shifts))
+    whole = place(here, pieces[:2], shifts[:7], keep(here, readings, blocks, shifts))
+    return place(here, pieces[2:], shifts[7:], whole)
 
 
 def solution(mesh):

time: 116 us -> 117 us (level)
  Pallas kernels: 19.1 us -> 20.3 us
    pallas_call x1 -> x2, Pallas kernels: 1.57 us -> 2.74 us  [place(): pl.pallas_call(functools.partial(place_kernel, whole.shape[1] // (2 * pie...]
  transfers between devices with their start and end apart: 13 -> 13, of which waited for: 7 -> 6; matrix products, arithmetic and copies ran while one was open for 2% -> 2% of each run, Pallas kernels for 12% -> 13%
where the time goes in v11:
time: 117 us; the launch traced here: 115 us
  starting transfers between devices  60.6 us (52%)
  waiting for transfers between devices  22.7 us (19%)
  Pallas kernels  20.3 us (17%)
  blocking collectives  8.05 us (7%)
  local copies, waits for them, and re-layouts  2.2 us (2%)
    ppermute x8, starting transfers between devices, ring(): lax.ppermute(value, 'z', [(i, (i + shift) % size) for i in range(size)])  34.5 us
    all_to_all x1, starting transfers between devices, exchanged(): return lax.all_to_all(lists, LISTS, 0, 0, tiled=True)  10.7 us
    ppermute x3, starting transfers between devices, swapped(): return lax.ppermute(sent, 'xl', [(0, 1), (1, 0)])  8.24 us
    all_to_all x1, blocking collectives, body(): lax.all_to_all(part.reshape(n_side, group // n_side, depth), SIDE, 0, 0,...  8.05 us
    all_to_all x1, waiting for transfers between devices, exchanged(): return lax.all_to_all(lists, LISTS, 0, 0, tiled=True)  7.92 us
    all_to_all x1, waiting for transfers between devices, body(): lax.all_to_all(copies, PLANE, 0, 0, tiled=True).reshape(-1, depth)  7.62 us
    ppermute x8, waiting for transfers between devices, ring(): lax.ppermute(value, 'z', [(i, (i + shift) % size) for i in range(size)])  7.13 us
    all_to_all x1, starting transfers between devices, body(): lax.all_to_all(copies, PLANE, 0, 0, tiled=True).reshape(-1, depth)  7.1 us
  transfers between devices with their start and end apart: 13, of which 6 were waited for; matrix products, arithmetic and copies ran while one was open for 2% of the time, Pallas kernels for 13%

profile of v11, /device:TPU:6, one launch (start us, length us, event | category | flops | bytes accessed | tf_op | source)
XLA Modules:
  0.0 115.2 jit_solution(16779154773122896343)
XLA Ops:
  0.0 4.3 %collective-permute-start = (bf16[768,512]{1,0:T(8,128)(2,1)}, bf16[768,512]{1,0:T(8,128)(2,1)S(1)}, u32[]{:S(2)}, u32[]{:S(2)}) collective-permute-start(bf16[768,512]{1,0:T(8,128)(2,1)} %bitcast.23), channel_id=1, source_target_pairs={{0,2},{2,4},{4,6},{6,8},{8,10},{10,12},{12,14},{14,0},{1,3},{3,5},... | collective-permute-start | bytes 2359304 | tf_op jit(solution)/shard_map/ppermute | solution.py:272
  4.3 8.6 %collective-permute-start.3 = (bf16[768,512]{1,0:T(8,128)(2,1)}, bf16[768,512]{1,0:T(8,128)(2,1)S(1)}, u32[]{:S(2)}, u32[]{:S(2)}) collective-permute-start(bf16[768,512]{1,0:T(8,128)(2,1)} %bitcast.24), channel_id=1, source_target_pairs={{0,14},{2,0},{4,2},{6,4},{8,6},{10,8},{12,10},{14,12},{1,15},{3,1}... | collective-permute-start | bytes 2359304 | tf_op jit(solution)/shard_map/ppermute | solution.py:272
  13.0 5.0 %compact.2 = bf16[512,128]{1,0:T(8,128)(2,1)} custom-call(s32[2]{0:T(128)S(1)} %pad_add_fusion.2.scalar_ref, s32[12,2048]{1,0:T(8,128)} %sensors_ref.2, bf16[12,64,512]{2,1,0:T(8,128)(2,1)} %temps_ref.1), custom_call_target="tpu_custom_call" | custom-call | tf_op jit(solution)/shard_map/compact/pallas_call | solution.py:75
  18.0 10.7 %all-to-all-start.1 = ((bf16[64,8,128]{2,1,0:T(8,128)(2,1)}), bf16[64,8,128]{2,1,0:T(8,128)(2,1)S(1)}, u32[]{:S(2)}, u32[]{:S(2)}) async-start(bf16[64,8,128]{2,1,0:T(8,128)(2,1)} %bitcast.10), calls=%async_computation.1 | async-start | bytes 262144 | tf_op jit(solution)/shard_map/all_to_all | solution.py:295
  28.8 3.8 %longest.1 = s32[1,1]{1,0:T(1,128)} custom-call(s32[12,2048]{1,0:T(8,128)} %sensors_ref.2), custom_call_target="tpu_custom_call" | custom-call | flops 1258291200 | bytes 98304 | tf_op jit(solution)/shard_map/longest/pallas_call | solution.py:142
  33.4 0.1 copy.8
  33.6 7.9 %all-to-all-done.1.lists_ref = bf16[64,8,128]{2,1,0:T(8,128)(2,1)S(1)} async-done(((bf16[64,8,128]{2,1,0:T(8,128)(2,1)}), bf16[64,8,128]{2,1,0:T(8,128)(2,1)S(1)}, u32[]{:S(2)}, u32[]{:S(2)}) %all-to-all-start.1) | async-done | bytes 131104 | tf_op jit(solution)/shard_map/all_to_all | solution.py:295
  41.5 1.5 %expand.2 = bf16[32,768]{1,0:T(8,128)(2,1)S(1)} custom-call(s32[2]{0:T(128)S(1)} %pad_add_fusion.3.scalar_ref, s32[12,32]{1,0:T(8,128)S(1)} %constant_dynamic-slice_fusion.rows_ref, s32[32,12]{1,0:T(8,128)S(1)} %bitcast.27, bf16[64,8,128]{2,1,0:T(8,128)(2,1)S(1)} %all-to-all-done.1.lists_ref), custom_call_target="tpu_custom_call" | custom-call | tf_op jit(solution)/shard_map/expand/pallas_call | solution.py:112
  43.0 2.5 %collective-permute-start.1 = (bf16[768,512]{1,0:T(8,128)(2,1)S(1)}, bf16[768,512]{1,0:T(8,128)(2,1)}, u32[]{:S(2)}, u32[]{:S(2)}) collective-permute-start(bf16[768,512]{1,0:T(8,128)(2,1)S(1)} %collective-permute-done.rest_1_), channel_id=1, source_target_pairs={{0,2},{2,4},{4,6},{6,8},{8,10},{10,12},{12,14},{14,0},{1,3},{3,5},... | collective-permute-start | bytes 2359304 | tf_op jit(solution)/shard_map/ppermute | solution.py:272
  45.5 4.5 %collective-permute-start.4 = (bf16[768,512]{1,0:T(8,128)(2,1)S(1)}, bf16[768,512]{1,0:T(8,128)(2,1)}, u32[]{:S(2)}, u32[]{:S(2)}) collective-permute-start(bf16[768,512]{1,0:T(8,128)(2,1)S(1)} %collective-permute-done.3.rest_2_), channel_id=1, source_target_pairs={{0,14},{2,0},{4,2},{6,4},{8,6},{10,8},{12,10},{14,12},{1,15},{3,1}... | collective-permute-start | bytes 2359304 | tf_op jit(solution)/shard_map/ppermute | solution.py:272
  50.1 8.0 %all_to_all.21 = bf16[8,4,768]{2,1,0:T(4,128)(2,1)S(1)} all-to-all(bf16[8,4,768]{2,1,0:T(4,128)(2,1)S(1)} %reshape.19), channel_id=1, replica_groups=mesh['y'=8,'xh'=2,'core'=2,'z'=8,'xl'=2] {'xh','xl','core'}, dimensions={0} | all-to-all | bytes 98304 | tf_op jit(solution)/shard_map/all_to_all | solution.py:312
  58.2 0.9 broadcast_in_dim.2
  59.0 7.1 %all-to-all-start.3 = ((bf16[64,4,768]{2,1,0:T(4,128)(2,1)}), bf16[64,4,768]{2,1,0:T(4,128)(2,1)}, u32[]{:S(2)}, u32[]{:S(2)}) async-start(bf16[64,4,768]{2,1,0:T(4,128)(2,1)} %broadcast_in_dim.2), calls=%async_computation.3 | async-start | bytes 786432 | tf_op jit(solution)/shard_map/all_to_all | solution.py:317
  66.1 1.9 %collective-permute-start.2 = (bf16[768,512]{1,0:T(8,128)(2,1)}, bf16[768,512]{1,0:T(8,128)(2,1)S(1)}, u32[]{:S(2)}, u32[]{:S(2)}) collective-permute-start(bf16[768,512]{1,0:T(8,128)(2,1)} %collective-permute-done.1.rest_3_), channel_id=1, source_target_pairs={{0,2},{2,4},{4,6},{6,8},{8,10},{10,12},{12,14},{14,0},{1,3},{3,5},... | collective-permute-start | bytes 2359304 | tf_op jit(solution)/shard_map/ppermute | solution.py:272
  68.1 5.1 %collective-permute-start.5 = (bf16[768,512]{1,0:T(8,128)(2,1)}, bf16[768,512]{1,0:T(8,128)(2,1)S(1)}, u32[]{:S(2)}, u32[]{:S(2)}) collective-permute-start(bf16[768,512]{1,0:T(8,128)(2,1)} %collective-permute-done.4.rest_4_), channel_id=1, source_target_pairs={{0,14},{2,0},{4,2},{6,4},{8,6},{10,8},{12,10},{14,12},{1,15},{3,1}... | collective-permute-start | bytes 2359304 | tf_op jit(solution)/shard_map/ppermute | solution.py:272
  73.3 7.6 %all-to-all-done.3 = bf16[64,4,768]{2,1,0:T(4,128)(2,1)} async-done(((bf16[64,4,768]{2,1,0:T(4,128)(2,1)}), bf16[64,4,768]{2,1,0:T(4,128)(2,1)}, u32[]{:S(2)}, u32[]{:S(2)}) %all-to-all-start.3) | async-done | bytes 393248 | tf_op jit(solution)/shard_map/all_to_all | solution.py:317
  80.9 1.1 reshape.20.readings_ref
  82.0 2.3 %send.3 = bf16[5,128,512]{2,1,0:T(8,128)(2,1)S(1)} custom-call(s32[2]{0:T(128)S(1)} %pad_add_fusion.4.scalar_ref, bf16[256,768]{1,0:T(8,128)(2,1)S(1)} %reshape.20.readings_ref, bf16[768,512]{1,0:T(8,128)(2,1)} %bitcast.25, bf16[768,512]{1,0:T(8,128)(2,1)S(1)} %collective-permute-done.rest_1_, bf16[768,512]{1,0:T(8,128)(2,1)S(1)} %collective-permute-done.3.rest_2_, ...), custom_call_target="tpu_custom_call" | custom-call | flops 503316480 | bytes 3932160 | tf_op jit(solution)/shard_map/send/pallas_call | solution.py:226
  84.3 2.7 %collective-permute-start.9 = (bf16[5,128,512]{2,1,0:T(8,128)(2,1)S(1)}, bf16[5,128,512]{2,1,0:T(8,128)(2,1)S(1)}, u32[]{:S(2)}, u32[]{:S(2)}) collective-permute-start(bf16[5,128,512]{2,1,0:T(8,128)(2,1)S(1)} %send.3), channel_id=1, source_target_pairs={{0,1},{1,0},{2,3},{3,2},{4,5},{5,4},{6,7},{7,6},{8,9},{9,8},{10,11... | collective-permute-start | bytes 1966088 | tf_op jit(solution)/shard_map/ppermute | solution.py:322
  87.1 2.0 %collective-permute-done.2.rest_0_.rest_5_ = bf16[768,512]{1,0:T(8,128)(2,1)S(1)} collective-permute-done((bf16[768,512]{1,0:T(8,128)(2,1)}, bf16[768,512]{1,0:T(8,128)(2,1)S(1)}, u32[]{:S(2)}, u32[]{:S(2)}) %collective-permute-start.2) | collective-permute-done | bytes 786464 | tf_op jit(solution)/shard_map/ppermute | solution.py:272
  89.1 1.3 %collective-permute-done.5.rest_1_.rest_6_ = bf16[768,512]{1,0:T(8,128)(2,1)S(1)} collective-permute-done((bf16[768,512]{1,0:T(8,128)(2,1)}, bf16[768,512]{1,0:T(8,128)(2,1)S(1)}, u32[]{:S(2)}, u32[]{:S(2)}) %collective-permute-start.5) | collective-permute-done | bytes 786464 | tf_op jit(solution)/shard_map/ppermute | solution.py:272
  90.4 2.1 %collective-permute-start.6 = (bf16[384,512]{1,0:T(8,128)(2,1)S(1)}, bf16[384,512]{1,0:T(8,128)(2,1)S(1)}, u32[]{:S(2)}, u32[]{:S(2)}) collective-permute-start(bf16[384,512]{1,0:T(8,128)(2,1)S(1)} %slice.6), channel_id=1, source_target_pairs={{0,2},{2,4},{4,6},{6,8},{8,10},{10,12},{12,14},{14,0},{1,3},{3,5},... | collective-permute-start | bytes 1179656 | tf_op jit(solution)/shard_map/ppermute | solution.py:272
  92.5 5.5 %collective-permute-start.7 = (bf16[384,512]{1,0:T(8,128)(2,1)S(1)}, bf16[384,512]{1,0:T(8,128)(2,1)S(1)}, u32[]{:S(2)}, u32[]{:S(2)}) collective-permute-start(bf16[384,512]{1,0:T(8,128)(2,1)S(1)} %slice.7), channel_id=1, source_target_pairs={{0,14},{2,0},{4,2},{6,4},{8,6},{10,8},{12,10},{14,12},{1,15},{3,1}... | collective-permute-start | bytes 1179656 | tf_op jit(solution)/shard_map/ppermute | solution.py:272
  98.0 0.9 send.5
  98.9 2.8 %collective-permute-start.10 = (bf16[2,128,512]{2,1,0:T(8,128)(2,1)S(1)}, bf16[2,128,512]{2,1,0:T(8,128)(2,1)S(1)}, u32[]{:S(2)}, u32[]{:S(2)}) collective-permute-start(bf16[2,128,512]{2,1,0:T(8,128)(2,1)S(1)} %send.5), channel_id=1, source_target_pairs={{0,1},{1,0},{2,3},{3,2},{4,5},{5,4},{6,7},{7,6},{8,9},{9,8},{10,11... | collective-permute-start | bytes 786440 | tf_op jit(solution)/shard_map/ppermute | solution.py:322
  101.7 2.6 %collective-permute-done.6.rest_0_.rest_7_ = bf16[384,512]{1,0:T(8,128)(2,1)S(1)} collective-permute-done((bf16[384,512]{1,0:T(8,128)(2,1)S(1)}, bf16[384,512]{1,0:T(8,128)(2,1)S(1)}, u32[]{:S(2)}, u32[]{:S(2)}) %collective-permute-start.6) | collective-permute-done | bytes 393248 | tf_op jit(solution)/shard_map/ppermute | solution.py:272
  104.3 1.2 %collective-permute-done.7.rest_1_.rest_8_ = bf16[384,512]{1,0:T(8,128)(2,1)S(1)} collective-permute-done((bf16[384,512]{1,0:T(8,128)(2,1)S(1)}, bf16[384,512]{1,0:T(8,128)(2,1)S(1)}, u32[]{:S(2)}, u32[]{:S(2)}) %collective-permute-start.7) | collective-permute-done | bytes 393248 | tf_op jit(solution)/shard_map/ppermute | solution.py:272
  105.5 0.8 send.4
  106.4 2.7 %collective-permute-start.8 = (bf16[1,128,512]{2,1,0:T(8,128)(2,1)S(1)}, bf16[1,128,512]{2,1,0:T(8,128)(2,1)S(1)}, u32[]{:S(2)}, u32[]{:S(2)}) collective-permute-start(bf16[1,128,512]{2,1,0:T(8,128)(2,1)S(1)} %send.4), channel_id=1, source_target_pairs={{0,1},{1,0},{2,3},{3,2},{4,5},{5,4},{6,7},{7,6},{8,9},{9,8},{10,11... | collective-permute-start | bytes 393224 | tf_op jit(solution)/shard_map/ppermute | solution.py:322
  109.1 3.1 %keep.1.rest_2_ = bf16[128,8192]{1,0:T(8,128)(2,1)} custom-call(s32[2]{0:T(128)S(1)} %pad_add_fusion.4.scalar_ref, bf16[256,768]{1,0:T(8,128)(2,1)S(1)} %reshape.20.readings_ref, bf16[768,512]{1,0:T(8,128)(2,1)S(1)} %bitcast.26, bf16[768,512]{1,0:T(8,128)(2,1)S(1)} %collective-permute-done.rest_1_, bf16[768,512]{1,0:T(8,128)(2,1)S(1)} %collective-permute-done.3.rest_2_, ...), custom_call_target="tpu_custom_call" | custom-call | flops 805306368 | bytes 6291456 | tf_op jit(solution)/shard_map/keep/pallas_call | solution.py:241
  112.3 1.5 %place.2.rest_1_ = bf16[128,8192]{1,0:T(8,128)(2,1)} custom-call(s32[2]{0:T(128)S(1)} %pad_add_fusion.4.scalar_ref, bf16[5,128,512]{2,1,0:T(8,128)(2,1)S(1)} %collective-permute-done.9.rest_0_, bf16[2,128,512]{2,1,0:T(8,128)(2,1)S(1)} %collective-permute-done.10.rest_1_, bf16[128,8192]{1,0:T(8,128)(2,1)} %keep.1.rest_2_), custom_call_target="tpu_custom_call", output_to_operand_aliasing={{}: (3, {})} | custom-call | tf_op jit(solution)/shard_map/place/pallas_call | solution.py:256
  113.8 1.2 %place.3 = bf16[128,8192]{1,0:T(8,128)(2,1)} custom-call(s32[2]{0:T(128)S(1)} %pad_add_fusion.4.scalar_ref, bf16[1,128,512]{2,1,0:T(8,128)(2,1)S(1)} %collective-permute-done.8.rest_0_, bf16[128,8192]{1,0:T(8,128)(2,1)} %place.2.rest_1_), custom_call_target="tpu_custom_call", output_to_operand_aliasing={{}: (2, {})} | custom-call | tf_op jit(solution)/shard_map/place/pallas_call | solution.py:256
  (22 shorter events, 0.5 us)
Async XLA Ops:
  0.0 43.0 %collective-permute-start = (bf16[768,512]{1,0:T(8,128)(2,1)}, bf16[768,512]{1,0:T(8,128)(2,1)S(1)}, u32[]{:S(2)}, u32[]{:S(2)}) collective-permute-start(bf16[768,512]{1,0:T(8,128)(2,1)} %bitcast.23), channel_id=1, source_target_pairs={{0,2},{2,4},{4,6},{6,8},{8,10},{10,12},{12,14},{14,0},{1,3},{3,5},... | collective-permute-start | bytes 2359304 | tf_op jit(solution)/shard_map/ppermute | solution.py:272
  4.3 41.3 %collective-permute-start.3 = (bf16[768,512]{1,0:T(8,128)(2,1)}, bf16[768,512]{1,0:T(8,128)(2,1)S(1)}, u32[]{:S(2)}, u32[]{:S(2)}) collective-permute-start(bf16[768,512]{1,0:T(8,128)(2,1)} %bitcast.24), channel_id=1, source_target_pairs={{0,14},{2,0},{4,2},{6,4},{8,6},{10,8},{12,10},{14,12},{1,15},{3,1}... | collective-permute-start | bytes 2359304 | tf_op jit(solution)/shard_map/ppermute | solution.py:272
  18.0 23.5 %all-to-all-start.1 = ((bf16[64,8,128]{2,1,0:T(8,128)(2,1)}), bf16[64,8,128]{2,1,0:T(8,128)(2,1)S(1)}, u32[]{:S(2)}, u32[]{:S(2)}) async-start(bf16[64,8,128]{2,1,0:T(8,128)(2,1)} %bitcast.10), calls=%async_computation.1 | async-start | bytes 262144 | tf_op jit(solution)/shard_map/all_to_all | solution.py:295
  28.8 4.6 %copy-start.2 = (s32[12,2048]{1,0:T(8,128)S(1)}, s32[12,2048]{1,0:T(8,128)}, u32[]{:S(2)}) copy-start(s32[12,2048]{1,0:T(8,128)} %sensors_ref.2) | copy-start | bytes 294916
  28.8 14.2 %copy-start = (bf16[12,64,512]{2,1,0:T(8,128)(2,1)S(1)}, bf16[12,64,512]{2,1,0:T(8,128)(2,1)}, u32[]{:S(2)}) copy-start(bf16[12,64,512]{2,1,0:T(8,128)(2,1)} %temps_ref.1) | copy-start | bytes 2359300
  43.0 23.1 %collective-permute-start.1 = (bf16[768,512]{1,0:T(8,128)(2,1)S(1)}, bf16[768,512]{1,0:T(8,128)(2,1)}, u32[]{:S(2)}, u32[]{:S(2)}) collective-permute-start(bf16[768,512]{1,0:T(8,128)(2,1)S(1)} %collective-permute-done.rest_1_), channel_id=1, source_target_pairs={{0,2},{2,4},{4,6},{6,8},{8,10},{10,12},{12,14},{14,0},{1,3},{3,5},... | collective-permute-start | bytes 2359304 | tf_op jit(solution)/shard_map/ppermute | solution.py:272
  45.5 22.5 %collective-permute-start.4 = (bf16[768,512]{1,0:T(8,128)(2,1)S(1)}, bf16[768,512]{1,0:T(8,128)(2,1)}, u32[]{:S(2)}, u32[]{:S(2)}) collective-permute-start(bf16[768,512]{1,0:T(8,128)(2,1)S(1)} %collective-permute-done.3.rest_2_), channel_id=1, source_target_pairs={{0,14},{2,0},{4,2},{6,4},{8,6},{10,8},{12,10},{14,12},{1,15},{3,1}... | collective-permute-start | bytes 2359304 | tf_op jit(solution)/shard_map/ppermute | solution.py:272
  59.0 21.9 %all-to-all-start.3 = ((bf16[64,4,768]{2,1,0:T(4,128)(2,1)}), bf16[64,4,768]{2,1,0:T(4,128)(2,1)}, u32[]{:S(2)}, u32[]{:S(2)}) async-start(bf16[64,4,768]{2,1,0:T(4,128)(2,1)} %broadcast_in_dim.2), calls=%async_computation.3 | async-start | bytes 786432 | tf_op jit(solution)/shard_map/all_to_all | solution.py:317
  66.1 22.9 %collective-permute-start.2 = (bf16[768,512]{1,0:T(8,128)(2,1)}, bf16[768,512]{1,0:T(8,128)(2,1)S(1)}, u32[]{:S(2)}, u32[]{:S(2)}) collective-permute-start(bf16[768,512]{1,0:T(8,128)(2,1)} %collective-permute-done.1.rest_3_), channel_id=1, source_target_pairs={{0,2},{2,4},{4,6},{6,8},{8,10},{10,12},{12,14},{14,0},{1,3},{3,5},... | collective-permute-start | bytes 2359304 | tf_op jit(solution)/shard_map/ppermute | solution.py:272
  68.1 22.3 %collective-permute-start.5 = (bf16[768,512]{1,0:T(8,128)(2,1)}, bf16[768,512]{1,0:T(8,128)(2,1)S(1)}, u32[]{:S(2)}, u32[]{:S(2)}) collective-permute-start(bf16[768,512]{1,0:T(8,128)(2,1)} %collective-permute-done.4.rest_4_), channel_id=1, source_target_pairs={{0,14},{2,0},{4,2},{6,4},{8,6},{10,8},{12,10},{14,12},{1,15},{3,1}... | collective-permute-start | bytes 2359304 | tf_op jit(solution)/shard_map/ppermute | solution.py:272
  84.3 27.9 %collective-permute-start.9 = (bf16[5,128,512]{2,1,0:T(8,128)(2,1)S(1)}, bf16[5,128,512]{2,1,0:T(8,128)(2,1)S(1)}, u32[]{:S(2)}, u32[]{:S(2)}) collective-permute-start(bf16[5,128,512]{2,1,0:T(8,128)(2,1)S(1)} %send.3), channel_id=1, source_target_pairs={{0,1},{1,0},{2,3},{3,2},{4,5},{5,4},{6,7},{7,6},{8,9},{9,8},{10,11... | collective-permute-start | bytes 1966088 | tf_op jit(solution)/shard_map/ppermute | solution.py:322
  90.4 18.7 %copy-start.1 = (bf16[12,64,512]{2,1,0:T(8,128)(2,1)S(1)}, bf16[12,64,512]{2,1,0:T(8,128)(2,1)}, u32[]{:S(2)}) copy-start(bf16[12,64,512]{2,1,0:T(8,128)(2,1)} %temps_ref.1) | copy-start | bytes 2359300
  90.4 13.9 %collective-permute-start.6 = (bf16[384,512]{1,0:T(8,128)(2,1)S(1)}, bf16[384,512]{1,0:T(8,128)(2,1)S(1)}, u32[]{:S(2)}, u32[]{:S(2)}) collective-permute-start(bf16[384,512]{1,0:T(8,128)(2,1)S(1)} %slice.6), channel_id=1, source_target_pairs={{0,2},{2,4},{4,6},{6,8},{8,10},{10,12},{12,14},{14,0},{1,3},{3,5},... | collective-permute-start | bytes 1179656 | tf_op jit(solution)/shard_map/ppermute | solution.py:272
  92.5 13.0 %collective-permute-start.7 = (bf16[384,512]{1,0:T(8,128)(2,1)S(1)}, bf16[384,512]{1,0:T(8,128)(2,1)S(1)}, u32[]{:S(2)}, u32[]{:S(2)}) collective-permute-start(bf16[384,512]{1,0:T(8,128)(2,1)S(1)} %slice.7), channel_id=1, source_target_pairs={{0,14},{2,0},{4,2},{6,4},{8,6},{10,8},{12,10},{14,12},{1,15},{3,1}... | collective-permute-start | bytes 1179656 | tf_op jit(solution)/shard_map/ppermute | solution.py:272
  98.9 13.4 %collective-permute-start.10 = (bf16[2,128,512]{2,1,0:T(8,128)(2,1)S(1)}, bf16[2,128,512]{2,1,0:T(8,128)(2,1)S(1)}, u32[]{:S(2)}, u32[]{:S(2)}) collective-permute-start(bf16[2,128,512]{2,1,0:T(8,128)(2,1)S(1)} %send.5), channel_id=1, source_target_pairs={{0,1},{1,0},{2,3},{3,2},{4,5},{5,4},{6,7},{7,6},{8,9},{9,8},{10,11... | collective-permute-start | bytes 786440 | tf_op jit(solution)/shard_map/ppermute | solution.py:322
  106.4 7.5 %collective-permute-start.8 = (bf16[1,128,512]{2,1,0:T(8,128)(2,1)S(1)}, bf16[1,128,512]{2,1,0:T(8,128)(2,1)S(1)}, u32[]{:S(2)}, u32[]{:S(2)}) collective-permute-start(bf16[1,128,512]{2,1,0:T(8,128)(2,1)S(1)} %send.4), channel_id=1, source_target_pairs={{0,1},{1,0},{2,3},{3,2},{4,5},{5,4},{6,7},{7,6},{8,9},{9,8},{10,11... | collective-permute-start | bytes 393224 | tf_op jit(solution)/shard_map/ppermute | solution.py:322
